TPU v7x, 32 devices: a whole 2x2x4 slice. The times are simulated.
32 devices in a mesh: dp: 4 (over y, x), expert: 8 (over z, core).
Axes of the slice: x: 2, y: 2, z: 4, core: 2. Of those that a mesh axis runs over, the one named last changes fastest.
Arguments:
- tokens: bfloat16 [32, 256, 1280], P(('dp', 'expert')), may hold values from -6 to 6
- lengths: int32 [32], P(('dp', 'expert')), may hold values from 64 to 256, as said below
- routes: int32 [32, 256, 7], P(('dp', 'expert')), may hold values from 0 to 14, all different within a row; in each aligned block of 256 rows (0 to 255, 256 to 511, ..., all dimensions but the last counted through in order) at most 168 rows name the same one
- attn_gain: bfloat16 [1280], P('expert'), may hold values from 0.099609375 to 1.8984375
- query_weight: bfloat16 [1280, 1280], P('expert'), may hold values from -0.15625 to 0.15625
- key_weight: bfloat16 [1280, 1280], P('expert'), may hold values from -0.15625 to 0.15625
- value_weight: bfloat16 [1280, 1280], P('expert'), may hold values from -0.15625 to 0.15625
- out_weight: bfloat16 [1280, 1280], P('expert'), may hold values from -1.25 to 1.25
- ffn_gain: bfloat16 [1280], P('expert'), may hold values from 0.099609375 to 1.8984375
- shared_gate: bfloat16 [1280, 896], P('expert'), may hold values from -0.15625 to 0.15625
- shared_up: bfloat16 [1280, 896], P('expert'), may hold values from -0.15625 to 0.15625
- shared_down: bfloat16 [896, 1280], P('expert'), may hold values from -0.1875 to 0.1875
- router_weight: bfloat16 [1280, 15], P('expert'), may hold values from -0.15625 to 0.15625
- expert_gate: bfloat16 [16, 1280, 896], P('expert'), may hold values from -0.15625 to 0.15625
- expert_up: bfloat16 [16, 1280, 896], P('expert'), may hold values from -0.15625 to 0.15625
- expert_down: bfloat16 [16, 896, 1280], P('expert'), may hold values from -3.5 to 3.5
- cotangent: bfloat16 [32, 256, 1280], P(('dp', 'expert')), may hold values from -6 to 6
Outputs:
- output: bfloat16 [32, 256, 1280], P(('dp', 'expert'))
- grad_tokens: float32 [32, 256, 1280], P(('dp', 'expert'))
- grad_attn_gain: float32 [1280], P('expert')
- grad_query: float32 [1280, 1280], P('expert')
- grad_key: float32 [1280, 1280], P('expert')
- grad_value: float32 [1280, 1280], P('expert')
- grad_out: float32 [1280, 1280], P('expert')
- grad_ffn_gain: float32 [1280], P('expert')
- grad_shared_gate: float32 [1280, 896], P('expert')
- grad_shared_up: float32 [1280, 896], P('expert')
- grad_shared_down: float32 [896, 1280], P('expert')
- grad_router: float32 [1280, 15], P('expert')
- grad_expert_gate: float32 [16, 1280, 896], P('expert', 'dp')
- grad_expert_up: float32 [16, 1280, 896], P('expert', 'dp')
- grad_expert_down: float32 [16, 896, 1280], P('expert', 'dp')
Inputs may be any that keep to these rules, and one draw needn't show every extreme that they name: `routes`: in each sequence, no expert is chosen by more than 168 of its token choices, and in some sequence one expert is chosen by exactly 168; every routed expert is chosen somewhere. `lengths`: some sequence has length exactly 256.
All inputs are finite; a program needn't handle non-finite values.
Results may differ from a plain program's by a relative error of at most 0.025.
Values may be sent and summed in bfloat16 or wider, within the bound.
No kernel may reach another device: no remote copies, remote signals or barrier semaphores. Data moves between devices by JAX's collectives and lax.ppermute only.
A program may use at most 320 MiB of HBM per device.

v0:
```python
from functools import partial
import math

import jax
import jax.numpy as jnp
from jax import lax
from jax.sharding import PartitionSpec as P

D = 1280
HEADS = 10
HEAD_DIM = 128
TOP = 7
SEQ = 256


epsilon = 1e-06


def rms_norm(values, gain_vector):
    return (
        values
        * lax.rsqrt(jnp.mean(values * values, axis=-1, keepdims=True) + epsilon)
        * gain_vector
    )


def rotary_tables(length):
    halfway = HEAD_DIM // 2
    inverse = 10000.0 ** (-2.0 * jnp.arange(halfway, dtype=jnp.float32) / HEAD_DIM)
    angles = jnp.arange(length, dtype=jnp.float32)[:, None] * inverse[None, :]
    return (jnp.cos(angles)[:, None, :], jnp.sin(angles)[:, None, :])


def rotate(values, cosine_table, sine_table):
    halfway = values.shape[-1] // 2
    first_half = values[..., :halfway]
    second_half = values[..., halfway:]
    return jnp.concatenate(
        [
            first_half * cosine_table - second_half * sine_table,
            second_half * cosine_table + first_half * sine_table,
        ],
        axis=-1,
    )


def gating(gate_part, up_part):
    return jax.nn.silu(gate_part) * up_part


def slot_table(choices, slot_count, capacity):
    flat_ids = choices.reshape(-1)
    onehot = (flat_ids[:, None] == jnp.arange(slot_count, dtype=jnp.int32)[None, :]).astype(
        jnp.int32
    )
    earlier = jnp.cumsum(onehot, axis=0) - onehot
    places = jnp.sum(earlier * onehot, axis=1)
    targets = flat_ids * capacity + places
    sources = jnp.full((slot_count * capacity,), flat_ids.shape[0], jnp.int32)
    sources = sources.at[targets].set(jnp.arange(flat_ids.shape[0], dtype=jnp.int32))
    return (targets, sources)


def matmul(left_side, right_side):
    return jnp.dot(left_side, right_side, preferred_element_type=jnp.float32)


def contract_rows(left_side, right_side):
    return lax.dot_general(
        left_side, right_side, (((0,), (0,)), ((), ())), preferred_element_type=jnp.float32
    )


def times_transposed(left_side, right_side):
    return lax.dot_general(
        left_side, right_side, (((1,), (1,)), ((), ())), preferred_element_type=jnp.float32
    )


def per_device(
    tokens,
    lengths,
    routes,
    attn_gain,
    query_weight,
    key_weight,
    value_weight,
    out_weight,
    ffn_gain,
    shared_gate,
    shared_up,
    shared_down,
    router_weight,
    expert_gate,
    expert_up,
    expert_down,
    cotangent,
):
    expert_count = lax.axis_size("expert")
    slot_dev = expert_gate.shape[0]
    slot_count = slot_dev * expert_count
    capacity = max(2, 3 * SEQ * TOP // (2 * slot_count))
    routed_count = router_weight.shape[1]
    dense_local = (
        attn_gain,
        query_weight,
        key_weight,
        value_weight,
        out_weight,
        ffn_gain,
        shared_gate,
        shared_up,
        shared_down,
        router_weight,
    )
    dense_full = (
        lax.all_gather(dense_local[0], "expert", axis=0, tiled=True),
        lax.all_gather(dense_local[1], "expert", axis=0, tiled=True),
        lax.all_gather(dense_local[2], "expert", axis=0, tiled=True),
        lax.all_gather(dense_local[3], "expert", axis=0, tiled=True),
        lax.all_gather(dense_local[4], "expert", axis=0, tiled=True),
        lax.all_gather(dense_local[5], "expert", axis=0, tiled=True),
        lax.all_gather(dense_local[6], "expert", axis=0, tiled=True),
        lax.all_gather(dense_local[7], "expert", axis=0, tiled=True),
        lax.all_gather(dense_local[8], "expert", axis=0, tiled=True),
        lax.all_gather(dense_local[9], "expert", axis=0, tiled=True),
    )
    (
        full_attn_gain,
        full_query,
        full_key,
        full_value,
        full_out,
        full_ffn_gain,
        full_shared_gate,
        full_shared_up,
        full_shared_down,
        full_router,
    ) = dense_full
    inputs = tokens[0].astype(jnp.float32)
    length_here = lengths[0]
    choices = routes[0]
    cosine_table, sine_table = rotary_tables(SEQ)
    turning = partial(rotate, cosine_table=cosine_table, sine_table=sine_table)
    root_scale = math.sqrt(HEAD_DIM)
    normed_float, norm_pull = jax.vjp(rms_norm, inputs, full_attn_gain.astype(jnp.float32))
    normed = normed_float.astype(jnp.bfloat16)
    query_pre = matmul(normed, full_query).reshape(SEQ, HEADS, HEAD_DIM)
    key_pre = matmul(normed, full_key).reshape(SEQ, HEADS, HEAD_DIM)
    query_turned, query_pull = jax.vjp(turning, query_pre)
    key_turned, key_pull = jax.vjp(turning, key_pre)
    queries = query_turned.astype(jnp.bfloat16)
    keys_all = key_turned.astype(jnp.bfloat16)
    values_all = matmul(normed, full_value).astype(jnp.bfloat16).reshape(SEQ, HEADS, HEAD_DIM)
    positions = jnp.arange(SEQ, dtype=jnp.int32)
    allowed = (positions[None, :] <= positions[:, None]) & (positions[None, :] < length_here)

    def attention_scores():
        raw_scores = (
            jnp.einsum("qhd,khd->hqk", queries, keys_all, preferred_element_type=jnp.float32)
            / root_scale
        )
        return jnp.where(allowed[None], raw_scores, -1e30)

    scores = attention_scores()
    largest = jnp.max(scores, axis=-1, keepdims=True)
    exp_total = jnp.sum(jnp.exp(scores - largest), axis=-1, keepdims=True)
    log_total = largest + jnp.log(exp_total)
    probabilities = jnp.exp(scores - log_total)
    attended = (
        jnp.einsum(
            "hqk,khd->qhd",
            probabilities.astype(jnp.bfloat16),
            values_all,
            preferred_element_type=jnp.float32,
        )
        .astype(jnp.bfloat16)
        .reshape(SEQ, D)
    )
    middle = inputs + matmul(attended, full_out)
    second_float, second_pull = jax.vjp(rms_norm, middle, full_ffn_gain.astype(jnp.float32))
    second = second_float.astype(jnp.bfloat16)
    shared_gate_part = matmul(second, full_shared_gate)
    shared_up_part = matmul(second, full_shared_up)
    shared_hidden = gating(shared_gate_part, shared_up_part).astype(jnp.bfloat16)
    shared_out = matmul(shared_hidden, full_shared_down)
    logits = matmul(second, full_router)
    gate_probs, gate_pull = jax.vjp(partial(jax.nn.softmax, axis=-1), logits)
    chosen = jnp.take_along_axis(gate_probs, choices, axis=1)
    targets, sources = slot_table(choices, slot_count, capacity)
    padded = jnp.concatenate([second, jnp.zeros((1, D), jnp.bfloat16)], axis=0)
    outgoing = padded[sources // TOP].reshape(expert_count, slot_dev, capacity, D)
    arrived = lax.all_to_all(outgoing, "expert", split_axis=0, concat_axis=2, tiled=True)
    expert_rows = arrived.reshape(slot_dev, expert_count * capacity, D)
    gate_part = jnp.einsum(
        "erd,edf->erf", expert_rows, expert_gate, preferred_element_type=jnp.float32
    )
    up_part = jnp.einsum("erd,edf->erf", expert_rows, expert_up, preferred_element_type=jnp.float32)
    expert_hidden = gating(gate_part, up_part).astype(jnp.bfloat16)
    expert_out = jnp.einsum(
        "erf,efd->erd", expert_hidden, expert_down, preferred_element_type=jnp.float32
    ).astype(jnp.bfloat16)
    returned = lax.all_to_all(
        expert_out.reshape(1, slot_dev, expert_count * capacity, D),
        "expert",
        split_axis=2,
        concat_axis=0,
        tiled=True,
    )
    picked = (
        returned.reshape(slot_count * capacity, D)[targets].reshape(SEQ, TOP, D).astype(jnp.float32)
    )
    routed = jnp.sum(picked * chosen[:, :, None], axis=1)
    output = (middle + shared_out + routed).astype(jnp.bfloat16)
    (
        back_attn_gain,
        back_query,
        back_key,
        back_value,
        back_out,
        back_ffn_gain,
        back_shared_gate,
        back_shared_up,
        back_shared_down,
        back_router,
    ) = dense_full
    incoming = cotangent[0]
    upstream = incoming.astype(jnp.float32)
    grad_chosen = jnp.sum(picked * upstream[:, None, :], axis=-1)
    grad_picked = (
        (chosen[:, :, None] * upstream[:, None, :]).astype(jnp.bfloat16).reshape(SEQ * TOP, D)
    )
    padded_grad = jnp.concatenate([grad_picked, jnp.zeros((1, D), jnp.bfloat16)], axis=0)
    grad_slots = padded_grad[sources].reshape(expert_count, slot_dev, capacity, D)
    grad_arrived = lax.all_to_all(
        grad_slots, "expert", split_axis=0, concat_axis=2, tiled=True
    ).reshape(slot_dev, expert_count * capacity, D)
    grad_expert_down = jnp.einsum(
        "erf,erd->efd", expert_hidden, grad_arrived, preferred_element_type=jnp.float32
    )
    grad_hidden = jnp.einsum(
        "erd,efd->erf", grad_arrived, expert_down, preferred_element_type=jnp.float32
    )
    unused_value, expert_gating_pull = jax.vjp(gating, gate_part, up_part)
    grad_gate_part, grad_up_part = expert_gating_pull(grad_hidden)
    grad_gate_low = grad_gate_part.astype(jnp.bfloat16)
    grad_up_low = grad_up_part.astype(jnp.bfloat16)
    grad_expert_gate = jnp.einsum(
        "erd,erf->edf", expert_rows, grad_gate_low, preferred_element_type=jnp.float32
    )
    grad_expert_up = jnp.einsum(
        "erd,erf->edf", expert_rows, grad_up_low, preferred_element_type=jnp.float32
    )
    grad_rows = jnp.einsum(
        "erf,edf->erd", grad_gate_low, expert_gate, preferred_element_type=jnp.float32
    )
    grad_rows = (
        grad_rows
        + jnp.einsum("erf,edf->erd", grad_up_low, expert_up, preferred_element_type=jnp.float32)
    ).astype(jnp.bfloat16)
    grad_returned = lax.all_to_all(
        grad_rows.reshape(1, slot_dev, expert_count * capacity, D),
        "expert",
        split_axis=2,
        concat_axis=0,
        tiled=True,
    )
    grad_second = jnp.sum(
        grad_returned.reshape(slot_count * capacity, D)[targets]
        .reshape(SEQ, TOP, D)
        .astype(jnp.float32),
        axis=1,
    )
    expert_summed = (
        lax.psum_scatter(
            grad_expert_gate.astype(jnp.bfloat16), "dp", scatter_dimension=1, tiled=True
        ).astype(jnp.float32),
        lax.psum_scatter(
            grad_expert_up.astype(jnp.bfloat16), "dp", scatter_dimension=1, tiled=True
        ).astype(jnp.float32),
        lax.psum_scatter(
            grad_expert_down.astype(jnp.bfloat16), "dp", scatter_dimension=1, tiled=True
        ).astype(jnp.float32),
    )
    route_match = (
        choices[:, :, None] == jnp.arange(routed_count, dtype=jnp.int32)[None, None, :]
    ).astype(jnp.float32)
    grad_gates = jnp.sum(grad_chosen[:, :, None] * route_match, axis=1)
    (grad_logits,) = gate_pull(grad_gates)
    grad_logits_low = grad_logits.astype(jnp.bfloat16)
    grad_router = contract_rows(second, grad_logits_low)
    grad_second = grad_second + times_transposed(grad_logits_low, back_router)
    grad_shared_down = contract_rows(shared_hidden, incoming)
    grad_shared_hidden = times_transposed(incoming, back_shared_down)
    unused_shared, shared_gating_pull = jax.vjp(gating, shared_gate_part, shared_up_part)
    grad_sgate, grad_sup = shared_gating_pull(grad_shared_hidden)
    grad_sgate_low = grad_sgate.astype(jnp.bfloat16)
    grad_sup_low = grad_sup.astype(jnp.bfloat16)
    grad_shared_gate = contract_rows(second, grad_sgate_low)
    grad_shared_up = contract_rows(second, grad_sup_low)
    grad_second = (
        grad_second
        + times_transposed(grad_sgate_low, back_shared_gate)
        + times_transposed(grad_sup_low, back_shared_up)
    )
    grad_middle_norm, grad_ffn_gain = second_pull(grad_second)
    grad_middle = upstream + grad_middle_norm
    grad_middle_low = grad_middle.astype(jnp.bfloat16)
    grad_out = contract_rows(attended, grad_middle_low)
    grad_attended = (
        times_transposed(grad_middle_low, back_out)
        .astype(jnp.bfloat16)
        .reshape(SEQ, HEADS, HEAD_DIM)
    )
    recomputed = jnp.exp(attention_scores() - log_total)
    grad_probs = jnp.einsum(
        "qhd,khd->hqk", grad_attended, values_all, preferred_element_type=jnp.float32
    )
    grad_values = jnp.einsum(
        "hqk,qhd->khd",
        recomputed.astype(jnp.bfloat16),
        grad_attended,
        preferred_element_type=jnp.float32,
    )
    grad_scores = (
        recomputed * (grad_probs - jnp.sum(grad_probs * recomputed, axis=-1, keepdims=True))
    ).astype(jnp.bfloat16)
    grad_queries_turned = (
        jnp.einsum("hqk,khd->qhd", grad_scores, keys_all, preferred_element_type=jnp.float32)
        / root_scale
    )
    grad_keys_turned = (
        jnp.einsum("hqk,qhd->khd", grad_scores, queries, preferred_element_type=jnp.float32)
        / root_scale
    )
    (grad_query_pre,) = query_pull(grad_queries_turned)
    (grad_key_pre,) = key_pull(grad_keys_turned)
    grad_query_low = grad_query_pre.astype(jnp.bfloat16).reshape(SEQ, D)
    grad_key_low = grad_key_pre.astype(jnp.bfloat16).reshape(SEQ, D)
    grad_value_low = grad_values.astype(jnp.bfloat16).reshape(SEQ, D)
    grad_query = contract_rows(normed, grad_query_low)
    grad_key = contract_rows(normed, grad_key_low)
    grad_value = contract_rows(normed, grad_value_low)
    grad_normed = (
        times_transposed(grad_query_low, back_query)
        + times_transposed(grad_key_low, back_key)
        + times_transposed(grad_value_low, back_value)
    )
    grad_inputs_norm, grad_attn_gain = norm_pull(grad_normed)
    grad_inputs = grad_middle + grad_inputs_norm
    dense_terms = (
        grad_attn_gain,
        grad_query,
        grad_key,
        grad_value,
        grad_out,
        grad_ffn_gain,
        grad_shared_gate,
        grad_shared_up,
        grad_shared_down,
        grad_router,
    )
    scattered = (
        lax.psum_scatter(
            dense_terms[0].astype(jnp.bfloat16), "expert", scatter_dimension=0, tiled=True
        ).astype(jnp.float32),
        lax.psum_scatter(
            dense_terms[1].astype(jnp.bfloat16), "expert", scatter_dimension=0, tiled=True
        ).astype(jnp.float32),
        lax.psum_scatter(
            dense_terms[2].astype(jnp.bfloat16), "expert", scatter_dimension=0, tiled=True
        ).astype(jnp.float32),
        lax.psum_scatter(
            dense_terms[3].astype(jnp.bfloat16), "expert", scatter_dimension=0, tiled=True
        ).astype(jnp.float32),
        lax.psum_scatter(
            dense_terms[4].astype(jnp.bfloat16), "expert", scatter_dimension=0, tiled=True
        ).astype(jnp.float32),
        lax.psum_scatter(
            dense_terms[5].astype(jnp.bfloat16), "expert", scatter_dimension=0, tiled=True
        ).astype(jnp.float32),
        lax.psum_scatter(
            dense_terms[6].astype(jnp.bfloat16), "expert", scatter_dimension=0, tiled=True
        ).astype(jnp.float32),
        lax.psum_scatter(
            dense_terms[7].astype(jnp.bfloat16), "expert", scatter_dimension=0, tiled=True
        ).astype(jnp.float32),
        lax.psum_scatter(
            dense_terms[8].astype(jnp.bfloat16), "expert", scatter_dimension=0, tiled=True
        ).astype(jnp.float32),
        lax.psum_scatter(
            dense_terms[9].astype(jnp.bfloat16), "expert", scatter_dimension=0, tiled=True
        ).astype(jnp.float32),
    )
    summed = (
        lax.psum(scattered[0].astype(jnp.bfloat16), "dp").astype(jnp.float32),
        lax.psum(scattered[1].astype(jnp.bfloat16), "dp").astype(jnp.float32),
        lax.psum(scattered[2].astype(jnp.bfloat16), "dp").astype(jnp.float32),
        lax.psum(scattered[3].astype(jnp.bfloat16), "dp").astype(jnp.float32),
        lax.psum(scattered[4].astype(jnp.bfloat16), "dp").astype(jnp.float32),
        lax.psum(scattered[5].astype(jnp.bfloat16), "dp").astype(jnp.float32),
        lax.psum(scattered[6].astype(jnp.bfloat16), "dp").astype(jnp.float32),
        lax.psum(scattered[7].astype(jnp.bfloat16), "dp").astype(jnp.float32),
        lax.psum(scattered[8].astype(jnp.bfloat16), "dp").astype(jnp.float32),
        lax.psum(scattered[9].astype(jnp.bfloat16), "dp").astype(jnp.float32),
    )
    return (
        output[None],
        grad_inputs[None],
        summed[0],
        summed[1],
        summed[2],
        summed[3],
        summed[4],
        summed[5],
        summed[6],
        summed[7],
        summed[8],
        summed[9],
        expert_summed[0],
        expert_summed[1],
        expert_summed[2],
    )


def solution(mesh):
    return jax.shard_map(
        per_device,
        mesh=mesh,
        in_specs=(
            P(("dp", "expert"), None, None),
            P(("dp", "expert")),
            P(("dp", "expert"), None, None),
            P("expert"),
            P("expert", None),
            P("expert", None),
            P("expert", None),
            P("expert", None),
            P("expert"),
            P("expert", None),
            P("expert", None),
            P("expert", None),
            P("expert", None),
            P("expert", None, None),
            P("expert", None, None),
            P("expert", None, None),
            P(("dp", "expert"), None, None),
        ),
        out_specs=(
            P(("dp", "expert"), None, None),
            P(("dp", "expert"), None, None),
            P("expert"),
            P("expert", None),
            P("expert", None),
            P("expert", None),
            P("expert", None),
            P("expert"),
            P("expert", None),
            P("expert", None),
            P("expert", None),
            P("expert", None),
            P("expert", "dp", None),
            P("expert", "dp", None),
            P("expert", "dp", None),
        ),
        check_vma=False,
    )
```

profile of v0, /device:TPU:0, one launch (start us, length us, event | category | flops | bytes accessed | tf_op | source)
XLA Modules:
  0.0 1540.8 jit_solution(2502746226716424366)
XLA Ops:
  15.0 19.6 %all-reduce.11 = (bf16[1280]{0:T(1024)(128)(2,1)S(1)}, bf16[1280]{0:T(1024)(128)(2,1)S(1)}) all-reduce(bf16[1280]{0:T(1024)(128)(2,1)S(1)} %dynamic-update-slice, bf16[1280]{0:T(1024)(128)(2,1)S(1)} %dynamic-update-slice.1), channel_id=1, replica_groups=mesh['dp'=4,'expert'=8] {'expert'}, use_global_device_ids=true, to_apply=%add.6 | all-reduce | flops 2560 | bytes 10240
  35.4 14.8 all-gather
  98.2 34.3 %all-gather.9.cloned.1.call-done = bf16[1280,1280]{1,0:T(8,128)(2,1)} async-done(((bf16[160,1280]{1,0:T(8,128)(2,1)}), bf16[1280,1280]{1,0:T(8,128)(2,1)}) %all-gather.9.cloned.1.call-update) | async-done | bytes 3276816 | tf_op jit(solution)/shard_map/all_gather | solution.py:120
  143.7 28.5 %all-gather.15.cloned.1.call-done = bf16[1280,1280]{1,0:T(8,128)(2,1)} async-done(((bf16[160,1280]{1,0:T(8,128)(2,1)}), bf16[1280,1280]{1,0:T(8,128)(2,1)}) %all-gather.15.cloned.1.call-update) | async-done | bytes 3276816 | tf_op jit(solution)/shard_map/all_gather | solution.py:121
  177.0 14.1 gather_fusion.4
  197.8 18.1 %gather_fusion.2 = bf16[2688,1280]{1,0:T(8,128)(2,1)} fusion(bf16[1793,1280]{1,0:T(8,128)(2,1)} %concatenate.17, s32[3072]{0:T(1024)S(1)} %get-tuple-element.69), kind=kCustom, calls=%fused_computation.2 | custom fusion | bytes 13773312 | tf_op jit(solution)/shard_map/gather | solution.py:234
  230.8 141.5 %all-to-all-done.2 = bf16[8,2,168,1280]{3,2,1,0:T(8,128)(2,1)} async-done(((bf16[8,2,168,1280]{3,2,1,0:T(8,128)(2,1)}), bf16[8,2,168,1280]{3,2,1,0:T(8,128)(2,1)}, u32[]{:S(2)}, u32[]{:S(2)}) %all-to-all-start.2) | async-done | bytes 6881312 | tf_op jit(solution)/shard_map/all_to_all | solution.py:235
  383.8 145.3 %all-to-all-done = bf16[8,2,168,1280]{3,2,1,0:T(8,128)(2,1)} async-done(((bf16[8,2,168,1280]{3,2,1,0:T(8,128)(2,1)}), bf16[8,2,168,1280]{3,2,1,0:T(8,128)(2,1)}, u32[]{:S(2)}, u32[]{:S(2)}) %all-to-all-start) | async-done | bytes 6881312 | tf_op jit(solution)/shard_map/all_to_all | solution.py:193
  554.2 19.6 %multiply_convert_fusion = (bf16[2,1344,896]{2,1,0:T(8,128)(2,1)}, bf16[2,1344,896]{2,1,0:T(8,128)(2,1)}, bf16[2,1344,896]{2,1,0:T(8,128)(2,1)}) fusion(f32[2,1344,896]{2,1,0:T(8,128)} %fusion.81, f32[2,1344,896]{2,1,0:T(8,128)} %fusion.82, bf16[2,1344,1280]{2,1,0:T(8,128)(2,1)} %bitcast.205, bf16[2,896,1280]{2,1,0:T(8,128)(2,1)} %param.32), kind=kOutput, calls=%fused_computation.15 | convolution fusion | flops 6204162048 | bytes 45187072 | tf_op jit(solution)/shard_map/erd,efd->erf/dot_general | solution.py:241
  584.3 23.0 %copy.131 = bf16[1,2,1344,1280]{3,1,0,2:T(2,128)(2,1)} copy(bf16[1,2,1344,1280]{3,2,1,0:T(8,128)(2,1)S(1)} %fusion.6) | data formatting | bytes 13762560 | tf_op jit(solution)/shard_map/reshape | solution.py:204
  614.0 50.7 %all-gather.17.cloned.1.call-done = bf16[1280,896]{1,0:T(8,128)(2,1)} async-done(((bf16[160,896]{1,0:T(8,128)(2,1)}), bf16[1280,896]{1,0:T(8,128)(2,1)}) %all-gather.17.cloned.1.call-update) | async-done | bytes 2293776 | tf_op jit(solution)/shard_map/all_gather | solution.py:123
  668.1 57.7 %all-gather.19.cloned.1.call-done = bf16[1280,896]{1,0:T(8,128)(2,1)} async-done(((bf16[160,896]{1,0:T(8,128)(2,1)}), bf16[1280,896]{1,0:T(8,128)(2,1)}) %all-gather.19.cloned.1.call-update) | async-done | bytes 2293776 | tf_op jit(solution)/shard_map/all_gather | solution.py:124
  755.5 23.0 %copy.137 = bf16[1,2,1344,1280]{3,1,0,2:T(2,128)(2,1)} copy(bf16[1,2,1344,1280]{3,2,1,0:T(8,128)(2,1)S(1)} %fusion.5) | data formatting | bytes 13762560 | tf_op jit(solution)/shard_map/reshape | solution.py:262
  778.4 40.5 %all-to-all-done.1 = bf16[1,2,1344,1280]{3,1,0,2:T(2,128)(2,1)} async-done(((bf16[1,2,1344,1280]{3,1,0,2:T(2,128)(2,1)}), bf16[1,2,1344,1280]{3,1,0,2:T(2,128)(2,1)}, u32[]{:S(2)}, u32[]{:S(2)}) %all-to-all-start.1) | async-done | bytes 6881312 | tf_op jit(solution)/shard_map/all_to_all | solution.py:203
  841.7 14.1 gather_fusion.1
  873.0 151.7 %all-to-all-done.3 = bf16[1,2,1344,1280]{3,1,0,2:T(2,128)(2,1)} async-done(((bf16[1,2,1344,1280]{3,1,0,2:T(2,128)(2,1)}), bf16[1,2,1344,1280]{3,1,0,2:T(2,128)(2,1)}, u32[]{:S(2)}, u32[]{:S(2)}) %all-to-all-start.3) | async-done | bytes 6881312 | tf_op jit(solution)/shard_map/all_to_all | solution.py:261
  1031.4 14.2 gather_fusion.3
  1152.4 42.5 %reduce-scatter.16.cloned.1.call-done = bf16[160,1280]{1,0:T(8,128)(2,1)} async-done(((bf16[1280,1280]{1,0:T(8,128)(2,1)}), bf16[160,1280]{1,0:T(8,128)(2,1)}) %reduce-scatter.16.cloned.1.call-update) | async-done | bytes 409616 | tf_op jit(solution)/shard_map/reduce_scatter | solution.py:370
  1195.0 42.4 %reduce-scatter.14.cloned.1.call-done = bf16[160,1280]{1,0:T(8,128)(2,1)} async-done(((bf16[1280,1280]{1,0:T(8,128)(2,1)}), bf16[160,1280]{1,0:T(8,128)(2,1)}) %reduce-scatter.14.cloned.1.call-update) | async-done | bytes 409616 | tf_op jit(solution)/shard_map/reduce_scatter | solution.py:367
  1238.1 57.1 %reduce-scatter.32.cloned.1.call-done = bf16[2,224,1280]{2,1,0:T(8,128)(2,1)} async-done(((bf16[2,896,1280]{2,1,0:T(8,128)(2,1)}), bf16[2,224,1280]{2,1,0:T(8,128)(2,1)}) %reduce-scatter.32.cloned.1.call-update) | async-done | bytes 1146896 | tf_op jit(solution)/shard_map/reduce_scatter | solution.py:281
  1297.9 56.0 %reduce-scatter.28.cloned.1.call-done = bf16[2,320,896]{2,1,0:T(8,128)(2,1)} async-done(((bf16[2,1280,896]{2,1,0:T(8,128)(2,1)}), bf16[2,320,896]{2,1,0:T(8,128)(2,1)}) %reduce-scatter.28.cloned.1.call-update) | async-done | bytes 1146896 | tf_op jit(solution)/shard_map/reduce_scatter | solution.py:275
  1356.8 56.0 %reduce-scatter.30.cloned.1.call-done = bf16[2,320,896]{2,1,0:T(8,128)(2,1)} async-done(((bf16[2,1280,896]{2,1,0:T(8,128)(2,1)}), bf16[2,320,896]{2,1,0:T(8,128)(2,1)}) %reduce-scatter.30.cloned.1.call-update) | async-done | bytes 1146896 | tf_op jit(solution)/shard_map/reduce_scatter | solution.py:278
  1422.2 16.6 %all-reduce.10 = (bf16[1280]{0:T(1024)(128)(2,1)S(1)}, bf16[1280]{0:T(1024)(128)(2,1)S(1)}) all-reduce(bf16[1280]{0:T(1024)(128)(2,1)S(1)} %get-tuple-element.19, bf16[1280]{0:T(1024)(128)(2,1)S(1)} %get-tuple-element.17), channel_id=2, replica_groups=mesh['dp'=4,'expert'=8] {'expert'}, use_global_device_ids=true, to_apply=%region_19.20.clone | all-reduce | flops 2560 | bytes 10240
  1459.4 66.1 %all-reduce.16.cloned.1.call-done = (bf16[160,1280]{1,0:T(8,128)(2,1)}, bf16[160,1280]{1,0:T(8,128)(2,1)}, bf16[160,1280]{1,0:T(8,128)(2,1)}, bf16[160,1280]{1,0...) async-done(((bf16[160,1280]{1,0:T(8,128)(2,1)}, bf16[160,1280]{1,0:T(8,128)(2,1)}, bf16[160,1280]{1,0:T(8,128)(2,1)}, ...) | async-done | bytes 2498576 | tf_op jit(solution)/shard_map/psum | solution.py:397
  (354 shorter events, 375.5 us)
Async XLA Ops:
  7.2 74.5 %all-gather.13.cloned.1.call-start = ((), (), s32[]{:S(2)}) async-start(), calls=%async_computation.17 | async-start | bytes 3686400 | tf_op jit(solution)/shard_map/all_gather | solution.py:119
  7.9 84.7 %all-gather.11.cloned.1.call-start = ((), (), s32[]{:S(2)}) async-start(), calls=%async_computation.16 | async-start | bytes 3686400 | tf_op jit(solution)/shard_map/all_gather | solution.py:118
  8.7 123.8 %all-gather.9.cloned.1.call-start = ((), (), s32[]{:S(2)}) async-start(), calls=%async_computation.15 | async-start | bytes 3686400 | tf_op jit(solution)/shard_map/all_gather | solution.py:120
  9.4 162.8 %all-gather.15.cloned.1.call-start = ((), (), s32[]{:S(2)}) async-start(), calls=%async_computation.18 | async-start | bytes 3686400 | tf_op jit(solution)/shard_map/all_gather | solution.py:121
  216.0 156.4 %all-to-all-start.2 = ((bf16[8,2,168,1280]{3,2,1,0:T(8,128)(2,1)}), bf16[8,2,168,1280]{3,2,1,0:T(8,128)(2,1)}, u32[]{:S(2)}, u32[]{:S(2)}) async-start(bf16[8,2,168,1280]{3,2,1,0:T(8,128)(2,1)} %bitcast.199), calls=%async_computation.2 | async-start | bytes 13762560 | tf_op jit(solution)/shard_map/all_to_all | solution.py:235
  372.3 156.8 %all-to-all-start = ((bf16[8,2,168,1280]{3,2,1,0:T(8,128)(2,1)}), bf16[8,2,168,1280]{3,2,1,0:T(8,128)(2,1)}, u32[]{:S(2)}, u32[]{:S(2)}) async-start(bf16[8,2,168,1280]{3,2,1,0:T(8,128)(2,1)} %bitcast.198), calls=%async_computation | async-start | bytes 13762560 | tf_op jit(solution)/shard_map/all_to_all | solution.py:193
  377.6 155.1 %slice-start = ((s8[4587520]{0:T(1024)(128)(4,1)}), s8[393216]{0:T(1024)(128)(4,1)S(1)}, s32[]{:S(2)}) async-start(s8[4587520]{0:T(1024)(128)(4,1)} %bitcast.226), calls=%async_computation.34 | async-start | bytes 786432
  607.3 211.7 %all-to-all-start.1 = ((bf16[1,2,1344,1280]{3,1,0,2:T(2,128)(2,1)}), bf16[1,2,1344,1280]{3,1,0,2:T(2,128)(2,1)}, u32[]{:S(2)}, u32[]{:S(2)}) async-start(bf16[1,2,1344,1280]{3,1,0,2:T(2,128)(2,1)} %copy.131), calls=%async_computation.1 | async-start | bytes 13762560 | tf_op jit(solution)/shard_map/all_to_all | solution.py:203
  612.1 52.6 %all-gather.17.cloned.1.call-start = ((), (), s32[]{:S(2)}) async-start(), calls=%async_computation.19 | async-start | bytes 2580480 | tf_op jit(solution)/shard_map/all_gather | solution.py:123
  612.7 113.2 %all-gather.19.cloned.1.call-start = ((), (), s32[]{:S(2)}) async-start(), calls=%async_computation.20 | async-start | bytes 2580480 | tf_op jit(solution)/shard_map/all_gather | solution.py:124
  613.2 210.6 %all-gather.21.cloned.1.call-start = ((), (), s32[]{:S(2)}) async-start(), calls=%async_computation.21 | async-start | bytes 2580480 | tf_op jit(solution)/shard_map/all_gather | solution.py:125
  818.9 205.8 %all-to-all-start.3 = ((bf16[1,2,1344,1280]{3,1,0,2:T(2,128)(2,1)}), bf16[1,2,1344,1280]{3,1,0,2:T(2,128)(2,1)}, u32[]{:S(2)}, u32[]{:S(2)}) async-start(bf16[1,2,1344,1280]{3,1,0,2:T(2,128)(2,1)} %copy.137), calls=%async_computation.3 | async-start | bytes 13762560 | tf_op jit(solution)/shard_map/all_to_all | solution.py:261
  823.8 314.8 %reduce-scatter.22.cloned.1.call-start = ((), (), s32[]{:S(2)}) async-start(), calls=%async_computation.26 | async-start | bytes 2580480 | tf_op jit(solution)/shard_map/reduce_scatter | solution.py:382
  829.4 309.2 %reduce-scatter.24.cloned.1.call-start = ((), (), s32[]{:S(2)}) async-start(), calls=%async_computation.27 | async-start | bytes 2580480 | tf_op jit(solution)/shard_map/reduce_scatter | solution.py:385
  831.8 306.9 %reduce-scatter.26.cloned.1.call-start = ((), (), s32[]{:S(2)}) async-start(), calls=%async_computation.28 | async-start | bytes 2580480 | tf_op jit(solution)/shard_map/reduce_scatter | solution.py:388
  834.1 304.6 %reduce-scatter.20.cloned.1.call-start = ((), (), s32[]{:S(2)}) async-start(), calls=%async_computation.25 | async-start | bytes 3686400 | tf_op jit(solution)/shard_map/reduce_scatter | solution.py:376
  1070.5 81.9 %reduce-scatter.18.cloned.1.call-start = ((), (), s32[]{:S(2)}) async-start(), calls=%async_computation.24 | async-start | bytes 3686400 | tf_op jit(solution)/shard_map/reduce_scatter | solution.py:373
  1082.8 112.2 %reduce-scatter.16.cloned.1.call-start = ((), (), s32[]{:S(2)}) async-start(), calls=%async_computation.23 | async-start | bytes 3686400 | tf_op jit(solution)/shard_map/reduce_scatter | solution.py:370
  1092.2 145.2 %reduce-scatter.14.cloned.1.call-start = ((), (), s32[]{:S(2)}) async-start(), calls=%async_computation.22 | async-start | bytes 3686400 | tf_op jit(solution)/shard_map/reduce_scatter | solution.py:367
  1096.3 198.8 %reduce-scatter.32.cloned.1.call-start = ((), (), s32[]{:S(2)}) async-start(), calls=%async_computation.31 | async-start | bytes 5734400 | tf_op jit(solution)/shard_map/reduce_scatter | solution.py:281
  1110.1 243.8 %reduce-scatter.28.cloned.1.call-start = ((), (), s32[]{:S(2)}) async-start(), calls=%async_computation.29 | async-start | bytes 5734400 | tf_op jit(solution)/shard_map/reduce_scatter | solution.py:275
  1123.6 289.2 %reduce-scatter.30.cloned.1.call-start = ((), (), s32[]{:S(2)}) async-start(), calls=%async_computation.30 | async-start | bytes 5734400 | tf_op jit(solution)/shard_map/reduce_scatter | solution.py:278
  1137.1 309.5 %reduce-scatter.34.cloned.1.call-start = ((), (), s32[]{:S(2)}) async-start(), calls=%async_computation.32 | async-start | bytes 368640
  1138.3 387.2 %all-reduce.16.cloned.1.call-start = ((), (), s32[]{:S(2)}) async-start(), calls=%async_computation.33 | async-start | bytes 4997120 | tf_op jit(solution)/shard_map/psum | solution.py:397
  (82 other events, 1150.1 us)
Sparse Core Ops, SparseCore 0:
  9.6 42.9 all-gather.12
  54.3 38.2 all-gather.10
  94.3 38.1 all-gather.8
  134.0 38.1 all-gather.14
  614.2 50.4 all-gather.16
  666.2 59.5 all-gather.18
  727.5 66.0 all-gather.20
  829.5 81.3 reduce-scatter.21
  913.8 81.4 reduce-scatter.23
  998.0 45.9 reduce-scatter.25
  1070.6 39.3 reduce-scatter.19
  1112.2 40.2 reduce-scatter.17
  1154.7 40.1 reduce-scatter.15
  1197.1 40.1 reduce-scatter.13
  1240.3 54.8 reduce-scatter.31
  1298.1 55.8 reduce-scatter.27
  1356.9 55.8 reduce-scatter.29
  1415.5 31.0 reduce-scatter.33
  1450.6 74.8 all-reduce.15
where the time goes:
time: 1550 us; the launch traced here: 1540 us
  waiting for transfers between devices  997 us (64%)
  local copies, waits for them, and re-layouts  213 us (14%)
  matrix products  179 us (12%)
  blocking collectives  61.2 us (4%)
  other arithmetic  51.6 us (3%)
  starting transfers between devices  21.3 us (1%)
  between operations  17.7 us (1%)
    all_to_all x1, waiting for transfers between devices, per_device(): lax.all_to_all(grad_rows.reshape(1, slot_dev, expert_count * capacity, D)...  152 us
    all_to_all x1, waiting for transfers between devices, per_device(): lax.all_to_all(outgoing, 'expert', split_axis=0, concat_axis=2, tiled=True)  145 us
    all_to_all x1, waiting for transfers between devices, per_device(): lax.all_to_all(grad_slots, 'expert', split_axis=0, concat_axis=2, tiled=T...  142 us
    psum x1, waiting for transfers between devices, per_device(): lax.psum(scattered[1].astype(jnp.bfloat16), 'dp').astype(jnp.float32)  66.1 us
    all_gather x1, waiting for transfers between devices, per_device(): lax.all_gather(dense_local[7], 'expert', axis=0, tiled=True)  57.7 us
    reduce_scatter x1, waiting for transfers between devices, per_device(): lax.psum_scatter(grad_expert_down.astype(jnp.bfloat16), 'dp', scatter_dim...  57.1 us
    reduce_scatter x1, waiting for transfers between devices, per_device(): lax.psum_scatter(grad_expert_up.astype(jnp.bfloat16), 'dp', scatter_dimen...  56 us
    reduce_scatter x1, waiting for transfers between devices, per_device(): lax.psum_scatter(grad_expert_gate.astype(jnp.bfloat16), 'dp', scatter_dim...  56 us
  transfers between devices with their start and end apart: 23, of which 17 were waited for; matrix products, arithmetic and copies ran while one was open for 20% of the time, Pallas kernels for 0%

commit v1 on v0

v1 whole, which is shorter than its diff:
```python
import math

import jax
import jax.numpy as jnp
from jax import lax
from jax.sharding import PartitionSpec as P

HEAD_DIM = 128
LANES = 128
EPS = 1e-06
LOW = jnp.bfloat16
WIDE = jnp.float32


def dot(a, b, dims=((1,), (0,))):
    return lax.dot_general(a, b, (dims, ((), ())), preferred_element_type=WIDE)


def dot_t(a, b):
    return dot(a, b, ((1,), (1,)))


def dot_rows(a, b):
    return dot(a, b, ((0,), (0,)))


def inverse_rms(v):
    return lax.rsqrt(jnp.mean(v * v, axis=-1, keepdims=True) + EPS)


def rms_back(grad, v, r, gain):
    scaled = grad * gain
    grad_v = r * (scaled - v * (r * r) * jnp.mean(scaled * v, axis=-1, keepdims=True))
    return grad_v, jnp.sum(grad * v * r, axis=0)


def rotary_tables(length):
    halfway = HEAD_DIM // 2
    inverse = 10000.0 ** (-2.0 * jnp.arange(halfway, dtype=WIDE) / HEAD_DIM)
    angles = jnp.arange(length, dtype=WIDE)[:, None] * inverse[None, :]
    return jnp.cos(angles)[:, None, :], jnp.sin(angles)[:, None, :]


def rotate(v, cosine, sine):
    half = v.shape[-1] // 2
    a, b = v[..., :half], v[..., half:]
    return jnp.concatenate([a * cosine - b * sine, b * cosine + a * sine], axis=-1)


def exchange(x, bit):
    count = lax.axis_size("dp")
    return lax.ppermute(x, "dp", [(i, i ^ bit) for i in range(count)])


def dp_bits():
    bits, b = [], 1
    while b < lax.axis_size("dp"):
        bits.append(b)
        b *= 2
    return bits


def dp_sum(x):
    bits = dp_bits()
    cut = x.shape[1] // 2 // LANES * LANES
    parts = []
    for piece, order in ((x[:, :cut], bits), (x[:, cut:], bits[::-1])):
        for bit in order:
            got = exchange(piece, bit)
            piece = (piece.astype(WIDE) + got.astype(WIDE)).astype(LOW)
        parts.append(piece)
    return jnp.concatenate(parts, axis=1)


def dp_scatter(x, order):
    count = lax.axis_size("dp")
    me = lax.axis_index("dp")
    rows = x.shape[0] // count
    x = x.reshape((2,) * len(dp_bits()) + (rows, x.shape[1]))
    axes = {bit: n for n, bit in enumerate(reversed(dp_bits()))}
    left = list(reversed(dp_bits()))
    for bit in order:
        axis = left.index(bit)
        mine = (me // bit) % 2
        kept = lax.dynamic_index_in_dim(x, mine, axis, keepdims=False)
        sent = lax.dynamic_index_in_dim(x, 1 - mine, axis, keepdims=False)
        got = exchange(sent, bit)
        left.remove(bit)
        total = kept.astype(WIDE) + got.astype(WIDE)
        x = total if not left else total.astype(LOW)
    return x


def per_device(
    tokens,
    lengths,
    routes,
    attn_gain,
    query_weight,
    key_weight,
    value_weight,
    out_weight,
    ffn_gain,
    shared_gate,
    shared_up,
    shared_down,
    router_weight,
    expert_gate,
    expert_up,
    expert_down,
    cotangent,
):
    group = lax.axis_size("expert")
    place_of_me = lax.axis_index("expert")
    slot_dev = expert_gate.shape[0]
    slot_count = slot_dev * group
    seq, width = tokens.shape[1:]
    top = routes.shape[2]
    heads = width // HEAD_DIM
    ff = expert_gate.shape[2]
    ff_part = ff // group
    rows_w = width // group
    capacity = max(2, 3 * seq * top // (2 * slot_count))
    cap = -(-capacity // 8) * 8
    routed_count = router_weight.shape[1]

    qkv_local = jnp.concatenate([query_weight, key_weight, value_weight], axis=1)
    qkv = lax.all_gather(qkv_local, "expert", axis=0, tiled=True)
    w_out = lax.all_gather(out_weight, "expert", axis=0, tiled=True)

    small = jnp.concatenate(
        [attn_gain, ffn_gain, router_weight.reshape(-1), routes[0].reshape(-1).astype(LOW)]
    )
    small_all = lax.all_gather(small, "expert", axis=0, tiled=False)
    at = 0
    pieces = []
    for n in (rows_w, rows_w, rows_w * routed_count, seq * top):
        pieces.append(small_all[:, at : at + n])
        at += n
    gain_a = pieces[0].reshape(1, width).astype(WIDE)
    gain_f = pieces[1].reshape(1, width).astype(WIDE)
    router = pieces[2].reshape(width, routed_count)
    routes_all = pieces[3].reshape(group, seq, top).astype(jnp.int32)

    def to_columns(w):
        return w.reshape(w.shape[0], group, ff_part).transpose(1, 0, 2)

    cols_local = jnp.concatenate([to_columns(shared_gate), to_columns(shared_up)], axis=2)
    cols = lax.all_to_all(cols_local, "expert", split_axis=0, concat_axis=0, tiled=True)
    shared_cols = cols.reshape(width, 2 * ff_part)

    inputs = tokens[0].astype(WIDE)
    length_here = lengths[0]
    cosine, sine = rotary_tables(seq)

    r_a = inverse_rms(inputs)
    normed = (inputs * r_a * gain_a).astype(LOW)
    qkv_pre = dot(normed, qkv)
    q_pre = qkv_pre[:, :width].reshape(seq, heads, HEAD_DIM)
    k_pre = qkv_pre[:, width : 2 * width].reshape(seq, heads, HEAD_DIM)
    queries = rotate(q_pre, cosine, sine).astype(LOW)
    keys = rotate(k_pre, cosine, sine).astype(LOW)
    values = qkv_pre[:, 2 * width :].astype(LOW).reshape(seq, heads, HEAD_DIM)
    positions = jnp.arange(seq, dtype=jnp.int32)
    allowed = (positions[None, :] <= positions[:, None]) & (positions[None, :] < length_here)
    root = math.sqrt(HEAD_DIM)
    scores = jnp.einsum("qhd,khd->hqk", queries, keys, preferred_element_type=WIDE) / root
    scores = jnp.where(allowed[None], scores, -1e30)
    probs = jax.nn.softmax(scores, axis=-1)
    probs_low = probs.astype(LOW)
    attended = (
        jnp.einsum("hqk,khd->qhd", probs_low, values, preferred_element_type=WIDE)
        .astype(LOW)
        .reshape(seq, width)
    )
    middle = inputs + dot(attended, w_out)
    r_f = inverse_rms(middle)
    second = (middle * r_f * gain_f).astype(LOW)

    incoming = cotangent[0]
    second_all = lax.all_gather(second, "expert", axis=0, tiled=True)
    up_all = lax.all_gather(incoming, "expert", axis=0, tiled=True)

    my_slots = place_of_me * slot_dev + jnp.arange(slot_dev, dtype=jnp.int32)
    member = jnp.any(
        routes_all[None] == my_slots[:, None, None, None], axis=-1
    )
    earlier = (positions[:, None] < positions[None, :]).astype(LOW)
    place = jnp.einsum("egb,bt->egt", member.astype(LOW), earlier, preferred_element_type=WIDE)
    place = place.astype(jnp.int32)
    hit = (place[:, :, None, :] == jnp.arange(cap, dtype=jnp.int32)[None, None, :, None]) & (
        member[:, :, None, :]
    )
    pick = hit.astype(LOW)

    logits_all = dot(second_all, router)
    probs_all = jax.nn.softmax(logits_all, axis=-1).reshape(group, seq, routed_count)
    chosen_all = jnp.sum(
        jnp.where(
            jnp.arange(routed_count, dtype=jnp.int32)[None, None, None, :]
            == my_slots[:, None, None, None],
            probs_all[None],
            0.0,
        ),
        axis=-1,
    )
    chosen_rows = jnp.sum(jnp.where(hit, chosen_all[:, :, None, :], 0.0), axis=-1)
    chosen_rows = chosen_rows.reshape(slot_dev, group * cap, 1)

    def to_slots(x):
        x = x.reshape(group, seq, width)
        out = jnp.einsum("egct,gtd->egcd", pick, x, preferred_element_type=WIDE).astype(LOW)
        return out.reshape(slot_dev, group * cap, width)

    def to_tokens(x):
        x = x.reshape(slot_dev, group, cap, width)
        out = jnp.einsum("egct,egcd->gtd", pick, x, preferred_element_type=WIDE)
        return out.reshape(group * seq, width)

    def per_slot(spec, a, b):
        return jnp.einsum(spec, a, b, preferred_element_type=WIDE)

    rows = to_slots(second_all)
    gate = per_slot("erd,edf->erf", rows, expert_gate)
    up = per_slot("erd,edf->erf", rows, expert_up)
    sig = jax.nn.sigmoid(gate)
    silu = gate * sig
    hidden = (silu * up).astype(LOW)
    expert_out = per_slot("erf,efd->erd", hidden, expert_down).astype(LOW)

    sh = dot(second_all, shared_cols)
    s_gate, s_up = sh[:, :ff_part], sh[:, ff_part:]
    s_sig = jax.nn.sigmoid(s_gate)
    s_silu = s_gate * s_sig
    s_hidden = (s_silu * s_up).astype(LOW)

    weighted = (expert_out.astype(WIDE) * chosen_rows).astype(LOW)
    forward_part = (to_tokens(weighted) + dot(s_hidden, shared_down)).astype(LOW)
    forward_sum = lax.psum_scatter(forward_part, "expert", scatter_dimension=0, tiled=True)
    output = (middle + forward_sum.astype(WIDE)).astype(LOW)

    g_rows_up = to_slots(up_all)
    g_choice_rows = jnp.sum(g_rows_up.astype(WIDE) * expert_out.astype(WIDE), axis=-1)
    g_expert_out = (chosen_rows * g_rows_up.astype(WIDE)).astype(LOW)
    g_hidden = per_slot("erd,efd->erf", g_expert_out, expert_down)
    g_gate = (g_hidden * up * (sig * (1.0 + gate * (1.0 - sig)))).astype(LOW)
    g_up = (g_hidden * silu).astype(LOW)
    g_rows = (
        per_slot("erf,edf->erd", g_gate, expert_gate) + per_slot("erf,edf->erd", g_up, expert_up)
    ).astype(LOW)

    g_s_hidden = dot_t(up_all, shared_down)
    g_s_gate = (g_s_hidden * s_up * (s_sig * (1.0 + s_gate * (1.0 - s_sig)))).astype(LOW)
    g_s_up = (g_s_hidden * s_silu).astype(LOW)
    g_s = jnp.concatenate([g_s_gate, g_s_up], axis=1)

    g_choice = jnp.einsum(
        "egct,egc->egt",
        hit.astype(WIDE),
        g_choice_rows.reshape(slot_dev, group, cap),
        precision=lax.Precision.HIGHEST,
    )
    lane = jnp.arange(LANES, dtype=jnp.int32)
    spread = jnp.zeros((group, seq, 2 * slot_count), WIDE)
    columns = jnp.arange(2 * slot_count, dtype=jnp.int32)
    high = g_choice.astype(LOW).astype(WIDE)
    rest = g_choice - high
    for n in range(slot_dev):
        spread = spread + jnp.where(columns == my_slots[n], high[n][..., None], 0.0)
        spread = spread + jnp.where(columns == my_slots[n] + slot_count, rest[n][..., None], 0.0)
    spread = spread.reshape(group * seq, 2 * slot_count).astype(LOW)
    spread = jnp.pad(spread, ((0, 0), (0, -(2 * slot_count) % LANES)))
    back_part = (to_tokens(g_rows) + dot_t(g_s, shared_cols)).astype(LOW)
    back_part = jnp.concatenate([back_part, spread], axis=1)
    back_sum = lax.psum_scatter(back_part, "expert", scatter_dimension=0, tiled=True)

    def scattered(a, b):
        out = []
        for n in range(slot_dev):
            g = dot_rows(a[n], b[n]).astype(LOW)
            bits = dp_bits()
            out.append(dp_scatter(g, bits if n % 2 == 0 else bits[::-1]))
        return jnp.stack(out)

    grad_down = scattered(hidden, g_expert_out)
    grad_gate = scattered(rows, g_gate)
    grad_up = scattered(rows, g_up)

    g_cols = dot_rows(second_all, g_s).astype(LOW)
    grad_sdown = dot_rows(s_hidden, up_all).astype(LOW)
    g_cols = lax.all_to_all(
        g_cols.reshape(group, rows_w, 2 * ff_part), "expert", split_axis=0, concat_axis=0, tiled=True
    )
    g_cols = g_cols.transpose(1, 0, 2)
    grad_sgate = g_cols[:, :, :ff_part].reshape(rows_w, ff)
    grad_sup = g_cols[:, :, ff_part:].reshape(rows_w, ff)
    shared_sum = dp_sum(jnp.concatenate([grad_sgate, grad_sup], axis=1))
    sdown_sum = dp_sum(grad_sdown)

    upstream = incoming.astype(WIDE)
    logits = dot(second, router)
    gate_probs = jax.nn.softmax(logits, axis=-1)
    g_gates = (
        back_sum[:, width : width + routed_count].astype(WIDE)
        + back_sum[:, width + slot_count : width + slot_count + routed_count].astype(WIDE)
    )
    g_logits = gate_probs * (g_gates - jnp.sum(g_gates * gate_probs, axis=-1, keepdims=True))
    g_logits = g_logits.astype(LOW)
    grad_router = dot_rows(second, g_logits)
    g_second = back_sum[:, :width].astype(WIDE) + dot_t(g_logits, router)
    g_norm, grad_ffn_gain = rms_back(g_second, middle, r_f, gain_f)
    g_middle = upstream + g_norm
    g_middle_low = g_middle.astype(LOW)
    grad_out = dot_rows(attended, g_middle_low)
    extra = jnp.concatenate([grad_router, grad_ffn_gain[:, None]], axis=1)
    extra = jnp.pad(extra, ((0, 0), (0, -(routed_count + 1) % LANES)))
    first_sum = dp_sum(
        lax.psum_scatter(
            jnp.concatenate([grad_out.astype(LOW), extra.astype(LOW)], axis=1),
            "expert",
            scatter_dimension=0,
            tiled=True,
        )
    )

    g_attended = dot_t(g_middle_low, w_out).astype(LOW).reshape(seq, heads, HEAD_DIM)
    g_probs = jnp.einsum("qhd,khd->hqk", g_attended, values, preferred_element_type=WIDE)
    g_values = jnp.einsum("hqk,qhd->khd", probs_low, g_attended, preferred_element_type=WIDE)
    g_scores = (probs * (g_probs - jnp.sum(g_probs * probs, axis=-1, keepdims=True))).astype(LOW)
    g_q = jnp.einsum("hqk,khd->qhd", g_scores, keys, preferred_element_type=WIDE) / root
    g_k = jnp.einsum("hqk,qhd->khd", g_scores, queries, preferred_element_type=WIDE) / root
    g_q = rotate(g_q, cosine, -sine).astype(LOW).reshape(seq, width)
    g_k = rotate(g_k, cosine, -sine).astype(LOW).reshape(seq, width)
    g_v = g_values.astype(LOW).reshape(seq, width)
    g_qkv = jnp.concatenate([g_q, g_k, g_v], axis=1)
    grad_qkv = dot_rows(normed, g_qkv)
    g_normed = dot_t(g_qkv, qkv)
    g_inputs, grad_attn_gain = rms_back(g_normed, inputs, r_a, gain_a)
    grad_tokens = g_middle + g_inputs
    extra = jnp.pad(grad_attn_gain[:, None], ((0, 0), (0, LANES - 1)))
    second_sum = dp_sum(
        lax.psum_scatter(
            jnp.concatenate([grad_qkv.astype(LOW), extra.astype(LOW)], axis=1),
            "expert",
            scatter_dimension=0,
            tiled=True,
        )
    )

    def wide(x):
        return x.astype(WIDE)

    return (
        output[None],
        grad_tokens[None],
        wide(second_sum[:, 3 * width]),
        wide(second_sum[:, :width]),
        wide(second_sum[:, width : 2 * width]),
        wide(second_sum[:, 2 * width : 3 * width]),
        wide(first_sum[:, :width]),
        wide(first_sum[:, width + routed_count]),
        wide(shared_sum[:, :ff]),
        wide(shared_sum[:, ff:]),
        wide(sdown_sum),
        wide(first_sum[:, width : width + routed_count]),
        wide(grad_gate),
        wide(grad_up),
        wide(grad_down),
    )


def solution(mesh):
    split = ("dp", "expert")
    e1, e2, e3 = P("expert"), P("expert", None), P("expert", None, None)
    s3 = P(split, None, None)
    scattered = P("expert", "dp", None)
    return jax.shard_map(
        per_device,
        mesh=mesh,
        in_specs=(s3, P(split), s3, e1, e2, e2, e2, e2, e1, e2, e2, e2, e2, e3, e3, e3, s3),
        out_specs=(s3, s3, e1, e2, e2, e2, e2, e1, e2, e2, e2, e2) + (scattered,) * 3,
        check_vma=False,
    )
```

time: 1550 us -> 922 us (0.59)
  waiting for transfers between devices: 997 us -> 453 us
  local copies, waits for them, and re-layouts: 213 us -> 115 us
  blocking collectives: 61.2 us -> 0 us
  matrix products: 179 us -> 216 us
  other arithmetic: 51.6 us -> 72.6 us
    all_to_all x4 -> x2, waiting for transfers between devices: 479 us -> 0.01 us  [the longest x1 0.01 us: per_device(): lax.all_to_all(cols_local, 'expert', split_axis=0, concat_axis=0, tiled=T...]
    reduce_scatter x10 -> x3, waiting for transfers between devices: 268 us -> 89.9 us  [the longest x1 57.2 us: per_device(): lax.psum_scatter(forward_part, 'expert', scatter_dimension=0, tiled=True)]
    ppermute x0 -> x28, waiting for transfers between devices: none -> 128 us  [exchange(): return lax.ppermute(x, 'dp', [(i, i ^ bit) for i in range(count)])]
    gather x8 -> x0, local copies, waits for them, and re-layouts: 71 us -> none  [the longest x1 18.1 us: per_device(): padded_grad[sources].reshape(expert_count, slot_dev, capacity, D)]
    psum x1 -> x0, waiting for transfers between devices: 66.1 us -> none  [per_device(): lax.psum(scattered[1].astype(jnp.bfloat16), 'dp').astype(jnp.float32)]
    unnamed x20 -> x11, waiting for transfers between devices: 7.04 us -> 47.5 us
    unnamed x2 -> x0, blocking collectives: 36.3 us -> none
    dot_general x39, matrix products: 179 us -> 211 us  [the longest x22 88.2 us: dot(): return lax.dot_general(a, b, (dims, ((), ())), preferred_element_type=WIDE)]
  transfers between devices with their start and end apart: 23 -> 39, of which waited for: 17 -> 21; matrix products, arithmetic and copies ran while one was open for 20% -> 39% of each run, Pallas kernels for 0% -> 0%
where the time goes in v1:
time: 922 us; the launch traced here: 911 us
  waiting for transfers between devices  453 us (49%)
  matrix products  216 us (23%)
  local copies, waits for them, and re-layouts  115 us (12%)
  other arithmetic  72.6 us (8%)
  starting transfers between devices  35.4 us (4%)
  between operations  18.2 us (2%)
    ppermute x28, waiting for transfers between devices, exchange(): return lax.ppermute(x, 'dp', [(i, i ^ bit) for i in range(count)])  128 us
    all_gather x1, waiting for transfers between devices, per_device(): qkv = lax.all_gather(qkv_local, 'expert', axis=0, tiled=True)  97.4 us
    dot_general x22, matrix products, dot(): return lax.dot_general(a, b, (dims, ((), ())), preferred_element_type=WIDE)  88.2 us
    dot_general x6, matrix products, per_slot(): return jnp.einsum(spec, a, b, preferred_element_type=WIDE)  84.7 us
    reduce_scatter x1, waiting for transfers between devices, per_device(): lax.psum_scatter(forward_part, 'expert', scatter_dimension=0, tiled=True)  57.2 us
    all_gather x1, waiting for transfers between devices, per_device(): up_all = lax.all_gather(incoming, 'expert', axis=0, tiled=True)  51.9 us
    unnamed x11, waiting for transfers between devices  47.5 us
    all_gather x1, waiting for transfers between devices, per_device(): second_all = lax.all_gather(second, 'expert', axis=0, tiled=True)  36.3 us
  transfers between devices with their start and end apart: 39, of which 21 were waited for; matrix products, arithmetic and copies ran while one was open for 39% of the time, Pallas kernels for 0%

profile of v1, /device:TPU:0, one launch (start us, length us, event | category | flops | bytes accessed | tf_op | source)
XLA Modules:
  0.0 910.8 jit_solution(12772809685281484961)
XLA Ops:
  20.6 46.1 %all-reduce.6.cloned.1.call-done = bf16[36096]{0:T(1024)(128)(2,1)} async-done(((bf16[36096]{0:T(1024)(128)(2,1)}), bf16[36096]{0:T(1024)(128)(2,1)}) %all-reduce.6.cloned.1.call-update) | async-done | bytes 72208
  68.0 97.4 %all-gather.7.cloned.1.call-done = bf16[1280,3840]{1,0:T(8,128)(2,1)} async-done(((bf16[160,3840]{1,0:T(8,128)(2,1)}), bf16[1280,3840]{1,0:T(8,128)(2,1)}) %all-gather.7.cloned.1.call-update) | async-done | bytes 9830416 | tf_op jit(solution)/shard_map/all_gather | solution.py:128
  223.1 51.9 %all-gather.13.cloned.1.call-done = bf16[1,2048,1280]{2,1,0:T(8,128)(2,1)} async-done(((bf16[1,256,1280]{2,1,0:T(8,128)(2,1)}), bf16[1,2048,1280]{2,1,0:T(8,128)(2,1)}) %all-gather.13.cloned.1.call-update) | async-done | bytes 5242896 | tf_op jit(solution)/shard_map/all_gather | solution.py:182
  275.0 9.7 %convert_bitcast_fusion = f32[2,8,168,1280]{3,2,0,1:T(8,128)} fusion(bf16[8,256,1280,1]{2,1,3,0:T(8,128)(2,1)} %bitcast.272, s32[2,8,256]{2,0,1:T(2,128)S(1)} %copy.281, pred[2,8,256]{2,0,1:T(4,128)(4,1)S(1)} %copy.282), kind=kOutput, calls=%fused_computation.9 | convolution fusion | flops 1769865216 | bytes 19025920 | tf_op jit(solution)/shard_map/egct,gtd->egcd/dot_general | solution.py:212
  284.7 11.2 %copy.293 = f32[2,8,168,1280]{3,2,1,0:T(8,128)} copy(f32[2,8,168,1280]{3,2,0,1:T(8,128)} %convert_bitcast_fusion) | data formatting | bytes 27525120 | tf_op jit(solution)/shard_map/convert_element_type | solution.py:244
  295.9 36.3 %all-gather.11.cloned.1.call-done = bf16[2048,1280]{0,1:T(8,128)(2,1)} async-done(((bf16[256,1280]{0,1:T(8,128)(2,1)}), bf16[2048,1280]{0,1:T(8,128)(2,1)}) %all-gather.11.cloned.1.call-update) | async-done | bytes 5242896 | tf_op jit(solution)/shard_map/all_gather | solution.py:181
  353.9 13.1 %fusion.105 = f32[2,1344,896]{2,1,0:T(8,128)} fusion(bf16[2,1344,1280]{2,1,0:T(8,128)(2,1)} %bitcast.278, bf16[2,1280,896]{2,1,0:T(8,128)(2,1)} %param.31), kind=kOutput, calls=%fused_computation.263 | convolution fusion | flops 6165626880 | bytes 21102592 | tf_op jit(solution)/shard_map/erd,edf->erf/dot_general | solution.py:221
  367.0 9.8 %fusion.104 = f32[2,1344,896]{2,1,0:T(8,128)} fusion(bf16[2,1344,1280]{2,1,0:T(8,128)(2,1)S(1)} %bitcast.279, bf16[2,1280,896]{2,1,0:T(8,128)(2,1)S(1)} %bitcast.320), kind=kOutput, calls=%fused_computation.262 | convolution fusion | flops 6165626880 | bytes 21102592 | tf_op jit(solution)/shard_map/erd,edf->erf/dot_general | solution.py:221
  376.8 8.6 multiply_convert_fusion
  385.4 19.6 %multiply_convert_fusion.1 = (bf16[2,1344,896]{2,1,0:T(8,128)(2,1)}, bf16[2,1344,896]{2,1,0:T(8,128)(2,1)}, bf16[2,1344,896]{2,1,0:T(8,128)(2,1)}) fusion(f32[2,1344,896]{2,1,0:T(8,128)} %fusion.104, f32[2,1344,896]{2,1,0:T(8,128)} %fusion.105, bf16[2,1344,1280]{2,1,0:T(8,128)(2,1)} %multiply_convert_fusion, bf16[2,896,1280]{2,1,0:T(8,128)(2,1)} %param.32), kind=kOutput, calls=%fused_computation.18 | convolution fusion | flops 6201753600 | bytes 45187072 | tf_op jit(solution)/shard_map/erd,efd->erf/dot_general | solution.py:221
  405.0 15.8 %fusion.3 = (f32[2,1344]{1,0:T(2,128)S(1)}, bf16[2,1344,1280]{2,1,0:T(8,128)(2,1)}) fusion(f32[2,1344,1280]{2,1,0:T(8,128)} %bitcast.267, f32[2,1344]{1,0:T(2,128)S(1)} %mul.480, bf16[2,1344,896]{2,1,0:T(8,128)(2,1)} %get-tuple-element.126, bf16[2,896,1280]{2,1,0:T(8,128)(2,1)} %param.32), kind=kOutput, calls=%fused_computation.8 | convolution fusion | flops 6186268160 | bytes 30069760 | tf_op jit(solution)/shard_map/erf,efd->erd/dot_general | solution.py:221
  422.0 13.4 %fusion.107 = f32[2,1344,1280]{2,1,0:T(8,128)} fusion(bf16[2,1344,896]{2,1,0:T(8,128)(2,1)} %get-tuple-element.125, bf16[2,1280,896]{2,1,0:T(8,128)(2,1)} %param.30), kind=kOutput, calls=%fused_computation.265 | convolution fusion | flops 6165626880 | bytes 23166976 | tf_op jit(solution)/shard_map/erf,edf->erd/dot_general | solution.py:221
  435.4 13.0 %fusion.5 = bf16[2,1344,1280]{2,1,0:T(8,128)(2,1)S(1)} fusion(f32[2,1344,1280]{2,1,0:T(8,128)} %fusion.107, bf16[2,1344,896]{2,1,0:T(8,128)(2,1)} %get-tuple-element.124, bf16[2,1280,896]{2,1,0:T(8,128)(2,1)} %param.31), kind=kOutput, calls=%fused_computation.14 | convolution fusion | flops 6172508160 | bytes 30048256 | tf_op jit(solution)/shard_map/erf,edf->erd/dot_general | solution.py:221
  453.9 11.3 %copy.344 = f32[2048,1280]{0,1:T(8,128)} copy(f32[2048,1280]{1,0:T(8,128)} %bitcast.269) | data formatting | bytes 20971520 | tf_op jit(solution)/shard_map/reshape | solution.py:218
  481.6 8.5 fusion.10
  490.1 11.3 %copy.343 = f32[2048,1280]{0,1:T(8,128)} copy(f32[2048,1280]{1,0:T(8,128)} %bitcast.268) | data formatting | bytes 20971520 | tf_op jit(solution)/shard_map/reshape | solution.py:218
  511.9 32.8 %reduce-scatter.9.cloned.1.call-done = bf16[256,1408]{0,1:T(8,128)(2,1)} async-done(((bf16[2048,1408]{0,1:T(8,128)(2,1)}), bf16[256,1408]{0,1:T(8,128)(2,1)}) %reduce-scatter.9.cloned.1.call-update) | async-done | bytes 720912 | tf_op jit(solution)/shard_map/reduce_scatter | solution.py:275
  548.1 57.2 %reduce-scatter.7.cloned.1.call-done = bf16[256,1280]{0,1:T(8,128)(2,1)} async-done(((bf16[2048,1280]{0,1:T(8,128)(2,1)}), bf16[256,1280]{0,1:T(8,128)(2,1)}) %reduce-scatter.7.cloned.1.call-update) | async-done | bytes 655376 | tf_op jit(solution)/shard_map/reduce_scatter | solution.py:239
  718.4 20.9 %collective-permute-done.13 = bf16[112,640]{1,0:T(8,128)(2,1)S(1)} collective-permute-done((bf16[112,640]{1,0:T(8,128)(2,1)S(1)}, bf16[112,640]{1,0:T(8,128)(2,1)S(1)}, u32[]{:S(2)}, u32[]{:S(2)}) %collective-permute-start.13) | collective-permute-done | bytes 143392 | tf_op jit(solution)/shard_map/ppermute | solution.py:52
  739.7 13.7 %collective-permute-done.15 = bf16[112,640]{1,0:T(8,128)(2,1)S(1)} collective-permute-done((bf16[112,640]{1,0:T(8,128)(2,1)S(1)}, bf16[112,640]{1,0:T(8,128)(2,1)S(1)}, u32[]{:S(2)}, u32[]{:S(2)}) %collective-permute-start.15) | collective-permute-done | bytes 143392 | tf_op jit(solution)/shard_map/ppermute | solution.py:52
  767.8 14.1 %collective-permute-done.24 = bf16[2,224,1280]{2,1,0:T(8,128)(2,1)} collective-permute-done((bf16[2,224,1280]{2,1,0:T(8,128)(2,1)}, bf16[2,224,1280]{2,1,0:T(8,128)(2,1)}, u32[]{:S(2)}, u32[]{:S(2)}) %collective-permute-start.24) | collective-permute-done | bytes 1146912 | tf_op jit(solution)/shard_map/ppermute | solution.py:52
  792.9 23.9 %collective-permute-done.11 = bf16[160,896]{1,0:T(8,128)(2,1)S(1)} collective-permute-done((bf16[160,896]{1,0:T(8,128)(2,1)S(1)}, bf16[160,896]{1,0:T(8,128)(2,1)S(1)}, u32[]{:S(2)}, u32[]{:S(2)}) %collective-permute-start.11) | collective-permute-done | bytes 286752 | tf_op jit(solution)/shard_map/ppermute | solution.py:52
  823.0 9.7 %collective-permute-done.21 = bf16[320,896]{1,0:T(8,128)(2,1)S(1)} collective-permute-done((bf16[320,896]{1,0:T(8,128)(2,1)S(1)}, bf16[320,896]{1,0:T(8,128)(2,1)S(1)}, u32[]{:S(2)}, u32[]{:S(2)}) %collective-permute-start.21) | collective-permute-done | bytes 573472 | tf_op jit(solution)/shard_map/ppermute | solution.py:52
  889.6 10.6 %collective-permute-done.3 = bf16[160,1920]{1,0:T(8,128)(2,1)S(1)} collective-permute-done((bf16[160,1920]{1,0:T(8,128)(2,1)S(1)}, bf16[160,1920]{1,0:T(8,128)(2,1)S(1)}, u32[]{:S(2)}, u32[]{:S(2)}) %collective-permute-start.3) | collective-permute-done | bytes 614432 | tf_op jit(solution)/shard_map/ppermute | solution.py:52
  (437 shorter events, 332.9 us)
Async XLA Ops:
  7.2 59.6 %all-reduce.6.cloned.1.call-start = ((), (), s32[]{:S(2)}) async-start(), calls=%async_computation.13 | async-start | bytes 147456
  13.8 151.6 %all-gather.7.cloned.1.call-start = ((), (), s32[]{:S(2)}) async-start(), calls=%async_computation.6 | async-start | bytes 11059200 | tf_op jit(solution)/shard_map/all_gather | solution.py:128
  16.3 188.5 %all-gather.9.cloned.1.call-start = ((), (), s32[]{:S(2)}) async-start(), calls=%async_computation.7 | async-start | bytes 3686400 | tf_op jit(solution)/shard_map/all_gather | solution.py:129
  17.0 258.0 %all-gather.13.cloned.1.call-start = ((), (), s32[]{:S(2)}) async-start(), calls=%async_computation.12 | async-start | bytes 5898240 | tf_op jit(solution)/shard_map/all_gather | solution.py:182
  17.6 314.6 %all-gather.11.cloned.1.call-start = ((), (), s32[]{:S(2)}) async-start(), calls=%async_computation.8 | async-start | bytes 5898240 | tf_op jit(solution)/shard_map/all_gather | solution.py:181
  212.3 252.9 %all-to-all-start = ((bf16[8,160,224]{2,1,0:T(8,128)(2,1)}), bf16[8,160,224]{2,1,0:T(8,128)(2,1)S(1)}, u32[]{:S(2)}, u32[]{:S(2)}) async-start(bf16[8,160,224]{2,1,0:T(8,128)(2,1)} %pad_maximum_fusion.12), calls=%async_computation | async-start | bytes 1310720 | tf_op jit(solution)/shard_map/all_to_all | solution.py:149
  215.9 328.8 %reduce-scatter.9.cloned.1.call-start = ((), (), s32[]{:S(2)}) async-start(), calls=%async_computation.10 | async-start | bytes 6488064 | tf_op jit(solution)/shard_map/reduce_scatter | solution.py:275
  481.5 123.7 %reduce-scatter.7.cloned.1.call-start = ((), (), s32[]{:S(2)}) async-start(), calls=%async_computation.9 | async-start | bytes 5898240 | tf_op jit(solution)/shard_map/reduce_scatter | solution.py:239
  509.5 334.5 %reduce-scatter.13.cloned.1.call-start = ((), (), s32[]{:S(2)}) async-start(), calls=%async_computation.14 | async-start | bytes 4055040
  618.6 249.9 %reduce-scatter.11.cloned.1.call-start = ((), (), s32[]{:S(2)}) async-start(), calls=%async_computation.11 | async-start | bytes 11427840 | tf_op jit(solution)/shard_map/reduce_scatter | solution.py:342
  660.1 54.1 %collective-permute-start.12 = (bf16[112,640]{1,0:T(8,128)(2,1)}, bf16[112,640]{1,0:T(8,128)(2,1)S(1)}, u32[]{:S(2)}, u32[]{:S(2)}) collective-permute-start(bf16[112,640]{1,0:T(8,128)(2,1)} %get-tuple-element.157), channel_id=1, source_target_pairs={{0,8},{8,0},{16,24},{24,16},{1,9},{9,1},{17,25},{25,17},{2,10},{10... | collective-permute-start | bytes 430088 | tf_op jit(solution)/shard_map/ppermute | solution.py:52
  661.6 54.2 %collective-permute-start.14 = (bf16[112,640]{1,0:T(8,128)(2,1)S(1)}, bf16[112,640]{1,0:T(8,128)(2,1)}, u32[]{:S(2)}, u32[]{:S(2)}) collective-permute-start(bf16[112,640]{1,0:T(8,128)(2,1)S(1)} %get-tuple-element.158), channel_id=1, source_target_pairs={{0,16},{8,24},{16,0},{24,8},{1,17},{9,25},{17,1},{25,9},{2,18},{10... | collective-permute-start | bytes 430088 | tf_op jit(solution)/shard_map/ppermute | solution.py:52
  668.4 86.3 %all-to-all-start.1 = ((bf16[8,160,224]{2,1,0:T(8,128)(2,1)}), bf16[8,160,224]{2,1,0:T(8,128)(2,1)S(1)}, u32[]{:S(2)}, u32[]{:S(2)}) async-start(bf16[8,160,224]{2,1,0:T(8,128)(2,1)} %bitcast.289), calls=%async_computation.4 | async-start | bytes 1310720 | tf_op jit(solution)/shard_map/all_to_all | solution.py:291
  683.8 72.0 %collective-permute-start.18 = (bf16[2,320,896]{2,1,0:T(8,128)(2,1)}, bf16[2,320,896]{2,1,0:T(8,128)(2,1)}, u32[]{:S(2)}, u32[]{:S(2)}) collective-permute-start(bf16[2,320,896]{2,1,0:T(8,128)(2,1)} %dynamic-slice_bitcast_fusion.4), channel_id=1, source_target_pairs={{0,16},{8,24},{16,0},{24,8},{1,17},{9,25},{17,1},{25,9},{2,18},{10... | collective-permute-start | bytes 3440648 | tf_op jit(solution)/shard_map/ppermute | solution.py:52
  690.0 68.4 %collective-permute-start.22 = (bf16[2,320,896]{2,1,0:T(8,128)(2,1)}, bf16[2,320,896]{2,1,0:T(8,128)(2,1)}, u32[]{:S(2)}, u32[]{:S(2)}) collective-permute-start(bf16[2,320,896]{2,1,0:T(8,128)(2,1)} %dynamic-slice_bitcast_fusion.2), channel_id=1, source_target_pairs={{0,16},{8,24},{16,0},{24,8},{1,17},{9,25},{17,1},{25,9},{2,18},{10... | collective-permute-start | bytes 3440648 | tf_op jit(solution)/shard_map/ppermute | solution.py:52
  698.6 62.8 %collective-permute-start.16 = (bf16[2,320,896]{2,1,0:T(8,128)(2,1)}, bf16[2,320,896]{2,1,0:T(8,128)(2,1)}, u32[]{:S(2)}, u32[]{:S(2)}) collective-permute-start(bf16[2,320,896]{2,1,0:T(8,128)(2,1)} %dynamic-slice_bitcast_fusion.5), channel_id=1, source_target_pairs={{0,8},{8,0},{16,24},{24,16},{1,9},{9,1},{17,25},{25,17},{2,10},{10... | collective-permute-start | bytes 3440648 | tf_op jit(solution)/shard_map/ppermute | solution.py:52
  714.2 50.6 %collective-permute-start.20 = (bf16[2,320,896]{2,1,0:T(8,128)(2,1)}, bf16[2,320,896]{2,1,0:T(8,128)(2,1)}, u32[]{:S(2)}, u32[]{:S(2)}) collective-permute-start(bf16[2,320,896]{2,1,0:T(8,128)(2,1)} %dynamic-slice_bitcast_fusion.3), channel_id=1, source_target_pairs={{0,8},{8,0},{16,24},{24,16},{1,9},{9,1},{17,25},{25,17},{2,10},{10... | collective-permute-start | bytes 3440648 | tf_op jit(solution)/shard_map/ppermute | solution.py:52
  753.4 28.5 %collective-permute-start.24 = (bf16[2,224,1280]{2,1,0:T(8,128)(2,1)}, bf16[2,224,1280]{2,1,0:T(8,128)(2,1)}, u32[]{:S(2)}, u32[]{:S(2)}) collective-permute-start(bf16[2,224,1280]{2,1,0:T(8,128)(2,1)} %dynamic-slice_bitcast_fusion.1), channel_id=1, source_target_pairs={{0,8},{8,0},{16,24},{24,16},{1,9},{9,1},{17,25},{25,17},{2,10},{10... | collective-permute-start | bytes 3440648 | tf_op jit(solution)/shard_map/ppermute | solution.py:52
  755.8 28.4 %collective-permute-start.26 = (bf16[2,224,1280]{2,1,0:T(8,128)(2,1)}, bf16[2,224,1280]{2,1,0:T(8,128)(2,1)S(1)}, u32[]{:S(2)}, u32[]{:S(2)}) collective-permute-start(bf16[2,224,1280]{2,1,0:T(8,128)(2,1)} %dynamic-slice_bitcast_fusion), channel_id=1, source_target_pairs={{0,16},{8,24},{16,0},{24,8},{1,17},{9,25},{17,1},{25,9},{2,18},{10... | collective-permute-start | bytes 3440648 | tf_op jit(solution)/shard_map/ppermute | solution.py:52
  758.4 32.0 %collective-permute-start.10 = (bf16[160,896]{1,0:T(8,128)(2,1)S(1)}, bf16[160,896]{1,0:T(8,128)(2,1)S(1)}, u32[]{:S(2)}, u32[]{:S(2)}) collective-permute-start(bf16[160,896]{1,0:T(8,128)(2,1)S(1)} %reshape.373), channel_id=1, source_target_pairs={{0,16},{8,24},{16,0},{24,8},{1,17},{9,25},{17,1},{25,9},{2,18},{10... | collective-permute-start | bytes 860168 | tf_op jit(solution)/shard_map/ppermute | solution.py:52
  761.4 30.8 %collective-permute-start.8 = (bf16[160,896]{1,0:T(8,128)(2,1)S(1)}, bf16[160,896]{1,0:T(8,128)(2,1)S(1)}, u32[]{:S(2)}, u32[]{:S(2)}) collective-permute-start(bf16[160,896]{1,0:T(8,128)(2,1)S(1)} %reshape.372), channel_id=1, source_target_pairs={{0,8},{8,0},{16,24},{24,16},{1,9},{9,1},{17,25},{25,17},{2,10},{10... | collective-permute-start | bytes 860168 | tf_op jit(solution)/shard_map/ppermute | solution.py:52
  764.8 55.8 %collective-permute-start.19 = (bf16[320,896]{1,0:T(8,128)(2,1)S(1)}, bf16[320,896]{1,0:T(8,128)(2,1)S(1)}, u32[]{:S(2)}, u32[]{:S(2)}) collective-permute-start(bf16[320,896]{1,0:T(8,128)(2,1)S(1)} %dynamic-slice_bitcast_fusion.10), channel_id=1, source_target_pairs={{0,8},{8,0},{16,24},{24,16},{1,9},{9,1},{17,25},{25,17},{2,10},{10... | collective-permute-start | bytes 1720328 | tf_op jit(solution)/shard_map/ppermute | solution.py:52
  781.9 39.3 %collective-permute-start.23 = (bf16[320,896]{1,0:T(8,128)(2,1)S(1)}, bf16[320,896]{1,0:T(8,128)(2,1)S(1)}, u32[]{:S(2)}, u32[]{:S(2)}) collective-permute-start(bf16[320,896]{1,0:T(8,128)(2,1)S(1)} %dynamic-slice_bitcast_fusion.8), channel_id=1, source_target_pairs={{0,8},{8,0},{16,24},{24,16},{1,9},{9,1},{17,25},{25,17},{2,10},{10... | collective-permute-start | bytes 1720328 | tf_op jit(solution)/shard_map/ppermute | solution.py:52
  784.2 37.1 %collective-permute-start.17 = (bf16[320,896]{1,0:T(8,128)(2,1)S(1)}, bf16[320,896]{1,0:T(8,128)(2,1)S(1)}, u32[]{:S(2)}, u32[]{:S(2)}) collective-permute-start(bf16[320,896]{1,0:T(8,128)(2,1)S(1)} %dynamic-slice_bitcast_fusion.11), channel_id=1, source_target_pairs={{0,16},{8,24},{16,0},{24,8},{1,17},{9,25},{17,1},{25,9},{2,18},{10... | collective-permute-start | bytes 1720328 | tf_op jit(solution)/shard_map/ppermute | solution.py:52
  (98 other events, 2141.8 us)
Sparse Core Ops, SparseCore 0:
  13.9 52.8 all-reduce.5
  69.0 96.3 all-gather.6
  167.1 37.6 all-gather.8
  206.3 68.6 all-gather.12
  277.0 55.1 all-gather.10
  481.7 62.9 reduce-scatter.8
  547.0 58.2 reduce-scatter.6
  618.7 42.7 reduce-scatter.12
  663.9 115.2 reduce-scatter.10

commit v2 on v1

v2 whole, which is shorter than its diff:
```python
import functools
import math

import jax
import jax.numpy as jnp
from jax import lax
from jax.experimental import pallas as pl
from jax.experimental.pallas import tpu as pltpu
from jax.sharding import PartitionSpec as P


HEAD_DIM = 128
LANES = 128
EPS = 1e-06
LOW = jnp.bfloat16
WIDE = jnp.float32
INT = jnp.int32


def dot(a, b, dims=((1,), (0,))):
    return lax.dot_general(a, b, (dims, ((), ())), preferred_element_type=WIDE)


def dot_t(a, b):
    return dot(a, b, ((1,), (1,)))


def dot_rows(a, b):
    return dot(a, b, ((0,), (0,)))


def inverse_rms(v):
    return lax.rsqrt(jnp.mean(v * v, axis=-1, keepdims=True) + EPS)


def iota(shape, axis):
    return lax.broadcasted_iota(INT, shape, axis)


def lane_pick(x, lane):
    return jnp.sum(jnp.where(iota(x.shape, 1) == lane, x, jnp.zeros_like(x)), axis=1, keepdims=True)


def masked_softmax(logits, count):
    logits = jnp.where(iota(logits.shape, 1) < count, logits, -1e30)
    e = jnp.exp(logits - jnp.max(logits, axis=-1, keepdims=True))
    return e / jnp.sum(e, axis=-1, keepdims=True)


def whole(shape):
    n = len(shape)
    return pl.BlockSpec(shape, lambda *_: (0,) * n, pipeline_mode=pl.Buffered(1))


def cost(flops, size):
    return pl.CostEstimate(flops=int(flops), bytes_accessed=int(size), transcendentals=0)


def turn(v, cosine, sine):
    return v * cosine + pltpu.roll(v, HEAD_DIM // 2, 1) * sine


def head_probs(q, k, allowed):
    s = dot_t(q, k) * (1.0 / math.sqrt(HEAD_DIM))
    s = jnp.where(allowed, s, -1e30)
    e = jnp.exp(s - jnp.max(s, axis=-1, keepdims=True))
    return e * (1.0 / jnp.sum(e, axis=-1, keepdims=True))


def allowed_keys(seq, length):
    key = iota((seq, seq), 1)
    return (key <= iota((seq, seq), 0)) & (key < length)


def attend_kernel(
    pair, length_ref, x_ref, gain_ref, cos_ref, sin_ref, wq_ref, wk_ref, wv_ref, qkv_ref, out_ref, normed
):
    seq = x_ref.shape[0]
    part = pair * HEAD_DIM

    @pl.when(pl.program_id(0) == 0)
    def _():
        x = x_ref[...].astype(WIDE)
        normed[...] = (x * inverse_rms(x) * gain_ref[...]).astype(LOW)

    pre_q, pre_k, pre_v = (dot(normed[...], w[...]) for w in (wq_ref, wk_ref, wv_ref))
    allowed = allowed_keys(seq, length_ref[0])
    cosine, sine = cos_ref[...], sin_ref[...]
    for i in range(pair):
        at = i * HEAD_DIM
        q = turn(pre_q[:, at : at + HEAD_DIM], cosine, sine).astype(LOW)
        k = turn(pre_k[:, at : at + HEAD_DIM], cosine, sine).astype(LOW)
        v = pre_v[:, at : at + HEAD_DIM].astype(LOW)
        qkv_ref[:, at : at + HEAD_DIM] = q
        qkv_ref[:, part + at : part + at + HEAD_DIM] = k
        qkv_ref[:, 2 * part + at : 2 * part + at + HEAD_DIM] = v
        p = head_probs(q, k, allowed).astype(LOW)
        out_ref[:, at : at + HEAD_DIM] = dot(p, v).astype(LOW)


def assemble_kernel(rows_ref, columns_ref, *refs):
    *pieces, out_ref, sems = refs
    copies = []
    for n, piece in enumerate(pieces):
        r, c = piece.shape
        place = out_ref.at[
            pl.ds(pl.multiple_of(rows_ref[n] * r, r), r), pl.ds(pl.multiple_of(columns_ref[n] * c, c), c)
        ]
        copies.append(pltpu.make_async_copy(piece, place, sems.at[n]))
    for copy in copies:
        copy.start()
    for copy in copies:
        copy.wait()


def project_kernel(att_ref, w_ref, x_ref, gain_ref, middle_ref, second_ref):
    middle = x_ref[...].astype(WIDE) + dot(att_ref[...], w_ref[...])
    middle_ref[...] = middle
    second_ref[...] = (middle * inverse_rms(middle) * gain_ref[...]).astype(LOW)


def middle_kernel(
    routed, slots, back_ref, second_ref, router_ref, middle_ref, gain_ref, up_ref, att_ref,
    wide_ref, low_ref, grads_ref,
):
    width = middle_ref.shape[1]
    second, router = second_ref[...], router_ref[...]
    probs = masked_softmax(dot(second, router), routed)
    both = back_ref[:, width:]
    lane = iota(both.shape, 1)
    g_gates = jnp.where(lane < routed, both + pltpu.roll(both, LANES - slots, 1), 0.0)
    g_logits = probs * (g_gates - jnp.sum(g_gates * probs, axis=-1, keepdims=True))
    g_logits = g_logits.astype(LOW)
    g_second = back_ref[:, :width] + dot_t(g_logits, router)
    middle = middle_ref[...]
    r = inverse_rms(middle)
    scaled = g_second * gain_ref[...]
    g_norm = r * (scaled - middle * (r * r) * jnp.mean(scaled * middle, axis=-1, keepdims=True))
    g_middle = up_ref[...].astype(WIDE) + g_norm
    wide_ref[...] = g_middle
    low = g_middle.astype(LOW)
    low_ref[...] = low
    grads_ref[:, :width] = dot_rows(att_ref[...], low).astype(LOW)
    g_gain = jnp.sum(g_second * middle * r, axis=0, keepdims=True)
    first = jnp.where(iota((8, width), 0) == 0, jnp.broadcast_to(g_gain, (8, width)), 0.0)
    mark = ((iota((8, LANES), 0) == 0) & (iota((8, LANES), 1) == routed)).astype(LOW)
    grads_ref[:, width:] = (dot_rows(second, g_logits) + dot_rows(first.astype(LOW), mark)).astype(LOW)


def attend_back_kernel(
    pair, length_ref, low_ref, wide_ref, x_ref, gain_ref, cos_ref, sin_ref, qkv_ref, wq_ref, wk_ref, wv_ref,
    wo_ref, tokens_ref, grads_ref, normed, total, ready, gain_ready, sems,
):
    seq, width = x_ref.shape
    part = pair * HEAD_DIM
    step = pl.program_id(0)
    steps = pl.num_programs(0)
    slot = lax.rem(step, 2)

    def leave(n, at):
        copies = []
        for i in range(3):
            columns = pl.ds(pl.multiple_of(i * width + n * part, LANES), part)
            copies.append(
                pltpu.make_async_copy(ready.at[at, i], grads_ref.at[:, columns], sems.at[at, i])
            )
        return copies

    @pl.when(step == 0)
    def _():
        x = x_ref[...].astype(WIDE)
        normed[...] = (x * inverse_rms(x) * gain_ref[...]).astype(LOW)
        total[...] = jnp.zeros_like(total)

    allowed = allowed_keys(seq, length_ref[0])
    cosine, sine = cos_ref[...], sin_ref[...]
    g_att = dot_t(low_ref[...], wo_ref[...]).astype(LOW)
    root = 1.0 / math.sqrt(HEAD_DIM)
    gq, gk, gv = [], [], []
    for i in range(pair):
        at = i * HEAD_DIM
        q = qkv_ref[:, at : at + HEAD_DIM]
        k = qkv_ref[:, part + at : part + at + HEAD_DIM]
        v = qkv_ref[:, 2 * part + at : 2 * part + at + HEAD_DIM]
        ga = g_att[:, at : at + HEAD_DIM]
        p = head_probs(q, k, allowed)
        gp = dot_t(ga, v)
        gv.append(dot_rows(p.astype(LOW), ga))
        ds = (p * (gp - jnp.sum(gp * p, axis=-1, keepdims=True))).astype(LOW)
        gq.append(turn(dot(ds, k) * root, cosine, -sine))
        gk.append(turn(dot_rows(ds, q) * root, cosine, -sine))
    g = jnp.concatenate(gq + gk + gv, axis=1).astype(LOW)

    @pl.when(step >= 2)
    def _():
        for copy in leave(step - 2, slot):
            copy.wait()

    for i, w_ref in enumerate((wq_ref, wk_ref, wv_ref)):
        piece = g[:, i * part : (i + 1) * part]
        total[...] += dot_t(piece, w_ref[...])
        ready[slot, i] = dot_rows(normed[...], piece).astype(LOW)
    for copy in leave(step, slot):
        copy.start()

    @pl.when(step == steps - 1)
    def _():
        x = x_ref[...].astype(WIDE)
        r = inverse_rms(x)
        grad = total[...]
        scaled = grad * gain_ref[...]
        back = r * (scaled - x * (r * r) * jnp.mean(scaled * x, axis=-1, keepdims=True))
        tokens_ref[...] = wide_ref[...] + back
        g_gain = jnp.sum(grad * x * r, axis=0, keepdims=True)
        first = jnp.where(iota((8, width), 0) == 0, jnp.broadcast_to(g_gain, (8, width)), 0.0)
        mark = ((iota((8, LANES), 0) == 0) & (iota((8, LANES), 1) == 0)).astype(LOW)
        gain_ready[...] = dot_rows(first.astype(LOW), mark).astype(LOW)
        last = pltpu.make_async_copy(gain_ready, grads_ref.at[:, 3 * width :], sems.at[2, 0])
        last.start()
        for copy in leave(step - 1, 1 - slot) + leave(step, slot) + [last]:
            copy.wait()


def silu_parts(gate):
    sig = 1.0 / (1.0 + jnp.exp(-gate))
    return gate * sig, sig * (1.0 + gate * (1.0 - sig))


def slots_of(hits, blocks):
    return jnp.concatenate([dot(h, x) for h, x in zip(hits, blocks)], axis=0).astype(LOW)


def row_hits(prow_ref, cap):
    count, _, seq = prow_ref.shape[1:]
    return [
        (iota((cap, seq), 0) == prow_ref[0, i]).astype(WIDE).astype(LOW) for i in range(count)
    ]


def column_hit(pcol_ref, at, e, cap):
    place = lane_pick(pcol_ref[at, :], e)
    return (iota((at.stop - at.start, cap), 1) == place).astype(WIDE).astype(LOW)


def experts_kernel(
    routed, slots_ref, s0_ref, s1_ref, prow_ref, pcol_ref, router_ref, wgu_ref, wd_ref, sc_ref, sd_ref,
    *refs,
):
    (rows_ref, hid_ref, sh_ref, sec_ref, a_ref, b_ref, picked_ref, probs_ref, sa_ref, sb_ref,
     part0_ref, part1_ref, total) = refs[-13:]
    seq, _ = s0_ref.shape
    cap = rows_ref.shape[2] // 2
    ff = wd_ref.shape[1]
    fp = sd_ref.shape[0]
    e = pl.program_id(0)

    @pl.when(e == 0)
    def _():
        sec_ref[0, :seq] = s0_ref[...]
        sec_ref[0, seq:] = s1_ref[...]
        probs_ref[...] = masked_softmax(dot(sec_ref[0], router_ref[...]), routed)
        mid = dot(sec_ref[0], sc_ref[...])
        silu, slope = silu_parts(mid[:, :fp])
        up = mid[:, fp:]
        hidden = (silu * up).astype(LOW)
        sa_ref[...] = silu.astype(LOW)
        sb_ref[...] = (up * slope).astype(LOW)
        sh_ref[0] = hidden
        total[...] = dot(hidden, sd_ref[...])

    slot = slots_ref[e]
    x = slots_of(row_hits(prow_ref, cap), (s0_ref[...], s1_ref[...]))
    rows_ref[0, 0] = x
    mid = dot(x, wgu_ref[0])
    silu, slope = silu_parts(mid[:, :ff])
    up = mid[:, ff:]
    hidden = (silu * up).astype(LOW)
    a_ref[0] = silu.astype(LOW)
    b_ref[0] = (up * slope).astype(LOW)
    hid_ref[0, 0] = hidden
    out = dot(hidden, wd_ref[0])
    for i in range(2):
        at = slice(i * seq, (i + 1) * seq)
        picked = dot(column_hit(pcol_ref, at, e, cap), out[i * cap : (i + 1) * cap].astype(LOW))
        picked_ref[0, at] = picked.astype(LOW)
        total[at, :] += lane_pick(probs_ref[at, :], slot) * picked

    @pl.when(e == pl.num_programs(0) - 1)
    def _():
        part0_ref[...] = total[:seq].astype(LOW)
        part1_ref[...] = total[seq:].astype(LOW)


def experts_back_kernel(
    slot_count, slots_ref, g0_ref, g1_ref, prow_ref, pcol_ref, probs_ref, picked_ref, a_ref, b_ref,
    wgu_ref, wd_ref, sc_ref, sd_ref, sa_ref, sb_ref, *refs,
):
    grows_ref, ggu_ref, gs_ref, up_ref, back0_ref, back1_ref, total, extra = refs[-8:]
    seq, width = g0_ref.shape
    cap = grows_ref.shape[2] // 2
    e = pl.program_id(0)

    @pl.when(e == 0)
    def _():
        up_ref[0, :seq] = g0_ref[...]
        up_ref[0, seq:] = g1_ref[...]
        gh = dot_t(up_ref[0], sd_ref[...])
        gs = jnp.concatenate([gh * sb_ref[...].astype(WIDE), gh * sa_ref[...].astype(WIDE)], axis=1)
        gs = gs.astype(LOW)
        gs_ref[0] = gs
        total[...] = dot_t(gs, sc_ref[...])
        extra[...] = jnp.zeros_like(extra)

    slot = slots_ref[e]
    scaled = []
    for i, g_ref in enumerate((g0_ref, g1_ref)):
        at = slice(i * seq, (i + 1) * seq)
        up = g_ref[...].astype(WIDE)
        scaled.append((lane_pick(probs_ref[at, :], slot) * up).astype(LOW))
        choice = jnp.sum(up * picked_ref[0, at].astype(WIDE), axis=1, keepdims=True)
        high = choice.astype(LOW).astype(WIDE)
        lane = iota((seq, LANES), 1)
        extra[at, :] += jnp.where(
            lane == slot, high, jnp.where(lane == slot + slot_count, choice - high, 0.0)
        )
    x = slots_of(row_hits(prow_ref, cap), scaled)
    grows_ref[0, 0] = x
    gh = dot_t(x, wd_ref[0])
    g = jnp.concatenate([gh * b_ref[0].astype(WIDE), gh * a_ref[0].astype(WIDE)], axis=1)
    g = g.astype(LOW)
    ggu_ref[0, 0] = g
    out = dot_t(g, wgu_ref[0])
    for i in range(2):
        at = slice(i * seq, (i + 1) * seq)
        total[at, :] += dot(column_hit(pcol_ref, at, e, cap), out[i * cap : (i + 1) * cap].astype(LOW))

    @pl.when(e == pl.num_programs(0) - 1)
    def _():
        for i, ref in enumerate((back0_ref, back1_ref)):
            at = slice(i * seq, (i + 1) * seq)
            ref[:, :width] = total[at, :].astype(LOW)
            ref[:, width:] = extra[at, :].astype(LOW)


def around(x):
    count = lax.axis_size("expert")
    return lax.ppermute(x, "expert", [(i, (i + 2) % count) for i in range(count)])


def partner(x):
    count = lax.axis_size("expert")
    return lax.ppermute(x, "expert", [(i, i ^ 1) for i in range(count)])


def add(*xs):
    return sum(x.astype(WIDE) for x in xs)


def ring_gather(x, behind=None):
    blocks = []
    for k in range(lax.axis_size("expert") // 2):
        if k == 2 and behind:
            x, _ = after_that(x, behind[-1][0])
        if k:
            x = around(x)
        blocks.append((x, partner(x)))
    return blocks


def ring_sum(parts):
    chips = len(parts)
    total = None
    for k in [*range(1, chips), 0]:
        mine = (parts[k][0], partner(parts[k][1]))
        if total is None:
            total = add(*mine)
        else:
            total = around(total.astype(LOW))
            total = add(*mine, total)
    return total


def exchange(x, bit):
    count = lax.axis_size("dp")
    return lax.ppermute(x, "dp", [(i, i ^ bit) for i in range(count)])


def dp_bits():
    bits, b = [], 1
    while b < lax.axis_size("dp"):
        bits.append(b)
        b *= 2
    return bits


def dp_sum(x):
    bits = dp_bits()
    cut = x.shape[1] // 2 // LANES * LANES
    parts = []
    for piece, order in ((x[:, :cut], bits), (x[:, cut:], bits[::-1])):
        for bit in order:
            got = exchange(piece, bit)
            piece = (piece.astype(WIDE) + got.astype(WIDE)).astype(LOW)
        parts.append(piece)
    return jnp.concatenate(parts, axis=1)


def dp_scatter(x, order, axis=0):
    me = lax.axis_index("dp")
    left = list(reversed(dp_bits()))
    lead, tail = x.shape[:axis], x.shape[axis + 1 :]
    x = x.reshape(*lead, *(2 for _ in left), x.shape[axis] // lax.axis_size("dp"), *tail)
    for bit in order:
        at = axis + left.index(bit)
        mine = (me // bit) % 2
        kept = lax.dynamic_index_in_dim(x, mine, at, keepdims=False)
        sent = lax.dynamic_index_in_dim(x, 1 - mine, at, keepdims=False)
        got = exchange(sent, bit)
        left.remove(bit)
        total = kept.astype(WIDE) + got.astype(WIDE)
        x = total if not left else total.astype(LOW)
    return x


def after_that(x, needed):
    return lax.optimization_barrier((x, needed))


def per_device(
    tokens,
    lengths,
    routes,
    attn_gain,
    query_weight,
    key_weight,
    value_weight,
    out_weight,
    ffn_gain,
    shared_gate,
    shared_up,
    shared_down,
    router_weight,
    expert_gate,
    expert_up,
    expert_down,
    cotangent,
):
    group = lax.axis_size("expert")
    place_of_me = lax.axis_index("expert")
    local = expert_gate.shape[0]
    slot_count = local * group
    seq, width = tokens.shape[1:]
    top = routes.shape[2]
    heads = width // HEAD_DIM
    ff = expert_gate.shape[2]
    ff_part = ff // group
    fp = -(-ff_part // LANES) * LANES
    rows_w = width // group
    capacity = max(2, 3 * seq * top // (2 * slot_count))
    cap = -(-capacity // 8) * 8
    routed = router_weight.shape[1]
    pair = 2
    steps = heads // pair
    part = pair * HEAD_DIM
    shape = jax.ShapeDtypeStruct

    count = lax.axis_size("dp")
    dp = lax.axis_index("dp")
    vo_local = jnp.concatenate([value_weight, out_weight], axis=1)
    strip = 2 * width // count
    vo_part = lax.all_gather(
        lax.dynamic_slice_in_dim(vo_local, dp * strip, strip, 1), "expert", axis=0, tiled=True
    )
    qk = jnp.concatenate([query_weight, key_weight], axis=1)
    qk = lax.all_gather(qk, "expert", axis=0, tiled=True)
    half = width // 2
    core = place_of_me % 2
    pieces = [lax.dynamic_slice_in_dim(vo_part, core * half, half, 0)]
    for bit in dp_bits():
        pieces += [exchange(p, bit) for p in pieces]
    placed = [(p, core ^ other, dp ^ n) for n, piece in enumerate(pieces)
              for other, p in enumerate((piece, partner(piece)))]
    smem = pl.BlockSpec(memory_space=pltpu.SMEM)
    vo = pl.pallas_call(
        assemble_kernel,
        in_specs=[smem, smem] + [pl.BlockSpec(memory_space=pltpu.VMEM)] * len(placed),
        out_specs=pl.BlockSpec(memory_space=pl.ANY),
        out_shape=shape((width, 2 * width), LOW),
        scratch_shapes=[pltpu.SemaphoreType.DMA((len(placed),))],
        cost_estimate=cost(0, 8 * width * width),
        name="assemble",
    )(jnp.stack([p[1] for p in placed]), jnp.stack([p[2] for p in placed]), *(p[0] for p in placed))

    small = jnp.concatenate(
        [attn_gain, ffn_gain, router_weight.reshape(-1), routes[0].reshape(-1).astype(LOW)]
    )
    length_small = small.shape[0]
    small = jnp.pad(small, (0, -length_small % LANES)).reshape(-1, LANES)
    small_all = lax.all_gather(small, "expert", axis=0, tiled=True).reshape(group, -1)
    at = 0
    pieces = []
    for n in (rows_w, rows_w, rows_w * routed, seq * top):
        pieces.append(small_all[:, at : at + n])
        at += n
    gain_a = pieces[0].reshape(1, width).astype(WIDE)
    gain_f = pieces[1].reshape(1, width).astype(WIDE)
    router = jnp.pad(pieces[2].reshape(width, routed), ((0, 0), (0, LANES - routed)))
    routes_all = pieces[3].reshape(group, seq, top).astype(INT)
    chips = group // 2
    back = jnp.arange(chips, dtype=INT)[:, None]
    met = 2 * ((place_of_me // 2 - back) % chips) + (core ^ jnp.arange(2, dtype=INT)[None, :])
    routes_all = routes_all[met.reshape(-1)]

    def to_columns(w):
        w = w.reshape(w.shape[0], group, ff_part).transpose(1, 0, 2)
        return jnp.pad(w, ((0, 0), (0, 0), (0, fp - ff_part)))

    def trim(x):
        return x[..., :ff_part]

    cols_local = jnp.concatenate([to_columns(shared_gate), to_columns(shared_up)], axis=2)
    cols = lax.all_to_all(cols_local, "expert", split_axis=0, concat_axis=0, tiled=True)
    shared_cols = cols.reshape(width, 2 * fp)
    shared_rows = jnp.pad(shared_down, ((0, fp - ff_part), (0, 0)))
    w_gu = jnp.concatenate([expert_gate, expert_up], axis=2)

    my_slots = place_of_me * local + jnp.arange(local, dtype=INT)
    positions = jnp.arange(seq, dtype=INT)
    member = jnp.any(routes_all[None] == my_slots[:, None, None, None], axis=-1)
    earlier = (positions[:, None] < positions[None, :]).astype(LOW)
    place = jnp.einsum("egb,bt->egt", member.astype(LOW), earlier, preferred_element_type=WIDE)
    place = jnp.where(member, place.astype(INT), -1)
    place_row = place[:, :, None, :]
    place_col = jnp.pad(
        place.reshape(local, group * seq).T, ((0, 0), (0, LANES - local)), constant_values=-1
    )

    halfway = HEAD_DIM // 2
    inverse = 10000.0 ** (-2.0 * jnp.arange(halfway, dtype=WIDE) / HEAD_DIM)
    angles = jnp.arange(seq, dtype=WIDE)[:, None] * inverse[None, :]
    cosine = jnp.tile(jnp.cos(angles), (1, 2))
    sine = jnp.concatenate([-jnp.sin(angles), jnp.sin(angles)], axis=1)

    x_low = tokens[0]
    incoming = cotangent[0]
    early = (shared_cols, shared_rows, w_gu, place_row, place_col, router)
    qk, early = after_that(qk, early)
    incoming, qk = after_that(incoming, qk)
    shared_cols, shared_rows, w_gu, place_row, place_col, router = early

    def columns(n):
        return pl.BlockSpec((seq, n), lambda h: (0, h))

    qkv_specs = [pl.BlockSpec((width, part), lambda h: (0, h)),
                 pl.BlockSpec((width, part), lambda h: (0, steps + h)),
                 pl.BlockSpec((width, part), lambda h: (0, h))]

    saved, attended = pl.pallas_call(
        functools.partial(attend_kernel, pair),
        grid=(steps,),
        in_specs=[smem, whole((seq, width)), whole((1, width)), whole((seq, HEAD_DIM)),
                  whole((seq, HEAD_DIM)), *qkv_specs],
        out_specs=[columns(3 * part), columns(part)],
        out_shape=[shape((seq, 3 * width), LOW), shape((seq, width), LOW)],
        scratch_shapes=[pltpu.VMEM((seq, width), LOW)],
        cost_estimate=cost(2 * seq * width * 3 * width * 1.3, 6 * width * width),
        name="attend",
    )(lengths, x_low, gain_a, cosine, sine, qk, qk, vo)
    middle, second = pl.pallas_call(
        project_kernel,
        grid=(1,),
        in_specs=[whole((seq, width)), pl.BlockSpec((width, width), lambda _: (0, 1)),
                  whole((seq, width)), whole((1, width))],
        out_specs=[whole((seq, width)), whole((seq, width))],
        out_shape=[shape((seq, width), WIDE), shape((seq, width), LOW)],
        cost_estimate=cost(2 * seq * width * width, 4 * width * width),
        name="project",
    )(attended, vo, x_low, gain_f)

    anywhere = pl.BlockSpec(memory_space=pl.ANY)
    tok, row = 2 * seq, 2 * cap
    flops = 2 * local * row * 3 * width * ff
    weights = (w_gu, expert_down, shared_cols, shared_rows)
    weight_specs = [pl.BlockSpec((1, width, 2 * ff), lambda e: (e, 0, 0)),
                    pl.BlockSpec((1, ff, width), lambda e: (e, 0, 0)),
                    whole((width, 2 * fp)), whole((fp, width))]

    def low(*dims):
        return shape(dims, LOW)

    def per_slot(k, r, n):
        return pl.BlockSpec((1, 1, r, n), lambda e: (e, k, 0, 0))

    def per_chip(k, r, n):
        return pl.BlockSpec((1, r, n), lambda e: (k, 0, 0))

    def by_slot(r, n):
        return pl.BlockSpec((1, r, n), lambda e: (e, 0, 0))

    def place_specs(k):
        return [pl.BlockSpec((1, 2, 1, seq), lambda e: (e, k, 0, 0)),
                pl.BlockSpec((tok, LANES), lambda e: (k, 0))]

    kept, parts = [], []
    store = ()
    blocks = ring_gather(second)
    for k in range(chips):
        store_in = [anywhere] * len(store)
        fixed = (my_slots, *blocks[k], place_row, place_col, router, *weights)
        out = pl.pallas_call(
            functools.partial(experts_kernel, routed),
            grid=(local,),
            in_specs=[smem, whole((seq, width)), whole((seq, width)), *place_specs(k),
                      whole((width, LANES)), *weight_specs, *store_in],
            out_specs=[per_slot(k, row, width), per_slot(k, row, ff), per_chip(k, tok, fp),
                       per_chip(k, tok, width), by_slot(row, ff), by_slot(row, ff), by_slot(tok, width),
                       whole((tok, LANES)), whole((tok, fp)), whole((tok, fp)),
                       whole((seq, width)), whole((seq, width))],
            out_shape=[low(local, chips, row, width), low(local, chips, row, ff), low(chips, tok, fp),
                       low(chips, tok, width), low(local, row, ff), low(local, row, ff),
                       low(local, tok, width), shape((tok, LANES), WIDE), low(tok, fp), low(tok, fp),
                       low(seq, width), low(seq, width)],
            scratch_shapes=[pltpu.VMEM((tok, width), WIDE)],
            input_output_aliases={len(fixed) + i: i for i in range(len(store))},
            cost_estimate=cost(flops * 1.2, 6 * local * width * ff),
        )(*fixed, *store)
        store = tuple(out[:4])
        kept.append(out[4:10])
        parts.append(out[10:])
    rows, hidden, s_hidden, second_all = store

    blocks = ring_gather(incoming, blocks)
    back_parts = [None] * chips
    store = ()
    for k in [*range(1, chips), 0]:
        act_a, act_b, picked, probs, s_a, s_b = kept[k]
        store_in = [anywhere] * len(store)
        fixed = (my_slots, *blocks[k], place_row, place_col, probs, picked, act_a, act_b, *weights, s_a, s_b)
        out = pl.pallas_call(
            functools.partial(experts_back_kernel, slot_count),
            grid=(local,),
            in_specs=[smem, whole((seq, width)), whole((seq, width)), *place_specs(k),
                      whole((tok, LANES)), by_slot(tok, width), by_slot(row, ff), by_slot(row, ff),
                      *weight_specs, whole((tok, fp)), whole((tok, fp)), *store_in],
            out_specs=[per_slot(k, row, width), per_slot(k, row, 2 * ff), per_chip(k, tok, 2 * fp),
                       per_chip(k, tok, width), whole((seq, width + LANES)), whole((seq, width + LANES))],
            out_shape=[low(local, chips, row, width), low(local, chips, row, 2 * ff),
                       low(chips, tok, 2 * fp), low(chips, tok, width),
                       low(seq, width + LANES), low(seq, width + LANES)],
            scratch_shapes=[pltpu.VMEM((tok, width), WIDE), pltpu.VMEM((tok, LANES), WIDE)],
            input_output_aliases={len(fixed) + i: i for i in range(len(store))},
            cost_estimate=cost(flops * 1.2, 6 * local * width * ff),
        )(*fixed, *store)
        store = tuple(out[:4])
        back_parts[k] = out[4:]
    grows, g_gu, g_s, up_all = store
    back_sum = ring_sum(back_parts)

    rows, hidden, grows, g_gu = (
        x.reshape(local, chips * row, x.shape[-1]) for x in (rows, hidden, grows, g_gu)
    )
    s_hidden, second_all, g_s, up_all = (
        x.reshape(chips * tok, x.shape[-1]) for x in (s_hidden, second_all, g_s, up_all)
    )

    bits = dp_bits()
    orders = [bits if n % 2 == 0 else bits[::-1] for n in range(local)]
    wide_gu = [dot_rows(rows[n], g_gu[n]).astype(LOW) for n in range(local)]
    wide_gu = [dp_scatter(wide_gu[n], orders[n]) for n in range(local)]

    g_cols = dot_rows(second_all, g_s).astype(LOW)
    grad_sdown = dot_rows(s_hidden, up_all).astype(LOW)[:ff_part]
    g_cols = lax.all_to_all(g_cols.reshape(group, rows_w, 2 * fp), "expert", split_axis=0, concat_axis=0, tiled=True)
    g_cols = g_cols.transpose(1, 0, 2)
    grad_sgate = trim(g_cols[:, :, :fp]).reshape(rows_w, ff)
    grad_sup = trim(g_cols[:, :, fp:]).reshape(rows_w, ff)
    shared_sum = dp_sum(jnp.concatenate([grad_sgate, grad_sup], axis=1))
    sdown_sum = dp_sum(grad_sdown)

    g_middle, g_low, grads_out = pl.pallas_call(
        functools.partial(middle_kernel, routed, slot_count),
        out_shape=[shape((seq, width), WIDE), shape((seq, width), LOW),
                   shape((width, width + LANES), LOW)],
        cost_estimate=cost(2 * seq * width * width, 4 * width * width),
        name="middle_back",
    )(back_sum, second, router, middle, gain_f, incoming, attended)

    grad_tokens, grads_qkv = pl.pallas_call(
        functools.partial(attend_back_kernel, pair),
        grid=(steps,),
        in_specs=[smem, whole((seq, width)), whole((seq, width)), whole((seq, width)),
                  whole((1, width)), whole((seq, HEAD_DIM)), whole((seq, HEAD_DIM)),
                  columns(3 * part), *qkv_specs, pl.BlockSpec((part, width), lambda h: (h, 1))],
        out_specs=[whole((seq, width)), pl.BlockSpec(memory_space=pl.ANY)],
        out_shape=[shape((seq, width), WIDE), shape((width, 3 * width + LANES), LOW)],
        scratch_shapes=[pltpu.VMEM((seq, width), LOW), pltpu.VMEM((seq, width), WIDE),
                        pltpu.VMEM((2, 3, width, part), LOW), pltpu.VMEM((width, LANES), LOW),
                        pltpu.SemaphoreType.DMA((3, 3))],
        cost_estimate=cost(2 * seq * width * 3 * width * 3, 16 * width * width),
        name="attend_back",
    )(lengths, g_low, g_middle, x_low, gain_a, cosine, sine, saved, qk, qk, vo, vo)
    out_sum = lax.psum_scatter(grads_out, "expert", scatter_dimension=0, tiled=True)
    qkv_sum = lax.psum_scatter(grads_qkv, "expert", scatter_dimension=0, tiled=True)
    out_sum = dp_sum(out_sum)
    qkv_sum = dp_sum(qkv_sum)

    hidden, grows, _ = lax.optimization_barrier((hidden, grows, grad_tokens))
    wide_down = [dp_scatter(dot_rows(hidden[n], grows[n]).astype(LOW), orders[n]) for n in range(local)]
    wide_gu, wide_down = jnp.stack(wide_gu), jnp.stack(wide_down)

    parts, _ = after_that(parts, back_sum)
    output = (middle + ring_sum(parts)).astype(LOW)

    def wide(x):
        return x.astype(WIDE)

    return (
        output[None],
        grad_tokens[None],
        wide(qkv_sum[:, 3 * width]),
        wide(qkv_sum[:, :width]),
        wide(qkv_sum[:, width : 2 * width]),
        wide(qkv_sum[:, 2 * width : 3 * width]),
        wide(out_sum[:, :width]),
        wide(out_sum[:, width + routed]),
        wide(shared_sum[:, :ff]),
        wide(shared_sum[:, ff:]),
        wide(sdown_sum),
        wide(out_sum[:, width : width + routed]),
        wide_gu[:, :, :ff],
        wide_gu[:, :, ff:],
        wide_down,
    )


def solution(mesh):
    split = ("dp", "expert")
    e1, e2, e3 = P("expert"), P("expert", None), P("expert", None, None)
    s3 = P(split, None, None)
    scattered = P("expert", "dp", None)

    def step(*args):
        return per_device(*args)

    step = jax.shard_map(
        step,
        mesh=mesh,
        in_specs=(s3, P(split), s3, e1, e2, e2, e2, e2, e1, e2, e2, e2, e2, e3, e3, e3, s3),
        out_specs=(s3, s3, e1, e2, e2, e2, e2, e1, e2, e2, e2, e2) + (scattered,) * 3,
        check_vma=False,
    )
    return step
```

time: 922 us -> 657 us (0.71)
  waiting for transfers between devices: 453 us -> 239 us
  Pallas kernels: 0 us -> 185 us
  matrix products: 216 us -> 38.5 us
  local copies, waits for them, and re-layouts: 115 us -> 27.7 us
  blocking collectives: 0 us -> 36.4 us
  other arithmetic: 72.6 us -> 48.3 us
  starting transfers between devices: 35.4 us -> 57.6 us
    pallas_call x0 -> x13, Pallas kernels: none -> 185 us  [the longest x4 69.1 us: per_device(): pl.pallas_call(functools.partial(experts_back_kernel, slot_count), grid=(...]
    all_gather x4 -> x2, waiting for transfers between devices: 188 us -> 3.32 us  [the longest x1 3.31 us: per_device(): qk = lax.all_gather(qk, 'expert', axis=0, tiled=True)]
    dot_general x16 -> x0, matrix products: 123 us -> none  [the longest x6 84.7 us: per_slot(): return jnp.einsum(spec, a, b, preferred_element_type=WIDE)]
    reduce_scatter x3 -> x2, waiting for transfers between devices: 89.9 us -> 0.02 us  [the longest x1 0.02 us: per_device(): lax.psum_scatter(grads_out, 'expert', scatter_dimension=0, tiled=True)]
    ppermute x0 -> x32, waiting for transfers between devices: none -> 83.5 us  [the longest x12 83.5 us: around(): lax.ppermute(x, 'expert', [(i, (i + 2) % count) for i in range(count)])]
    dot_general x22 -> x6, matrix products: 88.2 us -> 38.3 us  [dot(): return lax.dot_general(a, b, (dims, ((), ())), preferred_element_type=WIDE)]
    unnamed x11 -> x4, waiting for transfers between devices: 47.5 us -> 0.07 us
    all_gather x0 -> x1, blocking collectives: none -> 36.4 us  [per_device(): lax.all_gather(small, 'expert', axis=0, tiled=True).reshape(group, -1)]
  transfers between devices with their start and end apart: 39 -> 65, of which waited for: 21 -> 26; matrix products, arithmetic and copies ran while one was open for 39% -> 16% of each run, Pallas kernels for 0% -> 25%
where the time goes in v2:
time: 657 us; the launch traced here: 649 us
  waiting for transfers between devices  239 us (36%)
  Pallas kernels  185 us (28%)
  starting transfers between devices  57.6 us (9%)
  other arithmetic  48.3 us (7%)
  matrix products  38.5 us (6%)
  blocking collectives  36.4 us (6%)
  local copies, waits for them, and re-layouts  27.7 us (4%)
  between operations  16 us (2%)
    ppermute x27, waiting for transfers between devices, exchange(): return lax.ppermute(x, 'dp', [(i, i ^ bit) for i in range(count)])  152 us
    ppermute x12, waiting for transfers between devices, around(): lax.ppermute(x, 'expert', [(i, (i + 2) % count) for i in range(count)])  83.5 us
    pallas_call x4, Pallas kernels, per_device(): pl.pallas_call(functools.partial(experts_back_kernel, slot_count), grid=(...  69.1 us
    pallas_call x4, Pallas kernels, per_device(): pl.pallas_call(functools.partial(experts_kernel, routed), grid=(local,),...  67.5 us
    dot_general x6, matrix products, dot(): return lax.dot_general(a, b, (dims, ((), ())), preferred_element_type=WIDE)  38.3 us
    all_gather x1, blocking collectives, per_device(): lax.all_gather(small, 'expert', axis=0, tiled=True).reshape(group, -1)  36.4 us
    ppermute x27, starting transfers between devices, exchange(): return lax.ppermute(x, 'dp', [(i, i ^ bit) for i in range(count)])  33.3 us
    pallas_call x1, Pallas kernels, per_device(): pl.pallas_call(functools.partial(attend_back_kernel, pair), grid=(steps,)...  20.7 us
  transfers between devices with their start and end apart: 65, of which 26 were waited for; matrix products, arithmetic and copies ran while one was open for 16% of the time, Pallas kernels for 25%

profile of v2, /device:TPU:0, one launch (start us, length us, event | category | flops | bytes accessed | tf_op | source)
XLA Modules:
  0.0 649.0 jit_solution(8156257384981864462)
XLA Ops:
  20.5 36.4 %all-gather = bf16[8,36,128]{2,1,0:T(8,128)(2,1)S(1)} all-gather(bf16[1,36,128]{2,1,0:T(8,128)(2,1)S(1)} %pad_bitcast_fusion), channel_id=1, replica_groups=mesh['dp'=4,'expert'=8] {'expert'}, dimensions={0}, use_global_device_ids=true | all-gather | bytes 82944 | tf_op jit(solution)/shard_map/all_gather | solution.py:499
  64.3 15.6 %collective-permute-done.1.refs_2_ = bf16[640,640]{1,0:T(8,128)(2,1)} collective-permute-done((bf16[640,640]{1,0:T(8,128)(2,1)}, bf16[640,640]{1,0:T(8,128)(2,1)}, u32[]{:S(2)}, u32[]{:S(2)}) %collective-permute-start.1) | collective-permute-done | bytes 819232 | tf_op jit(solution)/shard_map/ppermute | solution.py:385
  91.8 9.1 %collective-permute-done.5.refs_6_ = bf16[640,640]{1,0:T(8,128)(2,1)} collective-permute-done((bf16[640,640]{1,0:T(8,128)(2,1)}, bf16[640,640]{1,0:T(8,128)(2,1)}, u32[]{:S(2)}, u32[]{:S(2)}) %collective-permute-start.5) | collective-permute-done | bytes 819232 | tf_op jit(solution)/shard_map/ppermute | solution.py:385
  120.0 10.8 %attend.1 = (bf16[256,3840]{1,0:T(8,128)(2,1)}, bf16[256,1280]{1,0:T(8,128)(2,1)}) custom-call(s32[1]{0:T(128)S(6)} %copy.177.length_ref, bf16[256,1280]{1,0:T(8,128)(2,1)} %bitcast.152, f32[1,1280]{1,0:T(1,128)} %reshape.275.gain_ref, f32[256,128]{1,0:T(8,128)} %copy.135.cos_ref, f32[256,128]{1,0:T(8,128)} %pad_maximum_fusion.6.sin_ref, ...), custom_call_target="tpu_custom_call" | custom-call | flops 3271557120 | bytes 9830400 | tf_op jit(solution)/shard_map/attend/pallas_call | solution.py:558
  137.1 18.0 %collective-permute-done.8.s0_ref = bf16[256,1280]{1,0:T(8,128)(2,1)S(1)} collective-permute-done((bf16[256,1280]{1,0:T(8,128)(2,1)}, bf16[256,1280]{1,0:T(8,128)(2,1)S(1)}, u32[]{:S(2)}, u32[]{:S(2)}) %collective-permute-start.8) | collective-permute-done | bytes 655392 | tf_op jit(solution)/shard_map/ppermute | solution.py:347
  155.6 13.5 %collective-permute-done.15.g0_ref = bf16[256,1280]{1,0:T(8,128)(2,1)S(1)} collective-permute-done((bf16[256,1280]{1,0:T(8,128)(2,1)S(1)}, bf16[256,1280]{1,0:T(8,128)(2,1)S(1)}, u32[]{:S(2)}, u32[]{:S(2)}) %collective-permute-start.15) | collective-permute-done | bytes 655392 | tf_op jit(solution)/shard_map/ppermute | solution.py:347
  169.1 13.3 %collective-permute-done.10.s0_ref = bf16[256,1280]{1,0:T(8,128)(2,1)S(1)} collective-permute-done((bf16[256,1280]{1,0:T(8,128)(2,1)S(1)}, bf16[256,1280]{1,0:T(8,128)(2,1)S(1)}, u32[]{:S(2)}, u32[]{:S(2)}) %collective-permute-start.10) | collective-permute-done | bytes 655392 | tf_op jit(solution)/shard_map/ppermute | solution.py:347
  182.6 16.9 %shard_map.280 = (bf16[2,4,336,1280]{3,2,1,0:T(8,128)(2,1)}, bf16[2,4,336,896]{3,2,1,0:T(8,128)(2,1)}, bf16[4,512,128]{2,1,0:T(8,128)(2,1)}, bf16[4,512,1280]{2,...) custom-call(s32[2]{0:T(128)} %copy-done.28, ...), custom_call_target="tpu_custom_call" | custom-call | flops 5549064192 | bytes 13762560 | tf_op jit(solution)/shard_map/pallas_call | solution.py:610
  199.6 16.9 %shard_map.281 = (bf16[2,4,336,1280]{3,2,1,0:T(8,128)(2,1)}, bf16[2,4,336,896]{3,2,1,0:T(8,128)(2,1)}, bf16[4,512,128]{2,1,0:T(8,128)(2,1)}, bf16[4,512,1280]{2,...) custom-call(s32[2]{0:T(128)} %copy-done.28, ...), custom_call_target="tpu_custom_call", output_to_operand_aliasing={{0}: (10, {}), {1}: (11, {}), {2}: (12, {}), {3}: (13, {})} | custom-call | flops 5549064192 | bytes 13762560 | tf_op jit(solution)/shard_map/pallas_call | solution.py:610
  217.6 17.3 %shard_map.284 = (bf16[2,4,336,1280]{3,2,1,0:T(8,128)(2,1)}, bf16[2,4,336,1792]{3,2,1,0:T(8,128)(2,1)}, bf16[4,512,256]{2,1,0:T(8,128)(2,1)}, bf16[4,512,1280]{2...) custom-call(s32[2]{0:T(128)} %copy-done.28, bf16[256,1280]{1,0:T(8,128)(2,1)} %copy-done.16, ...), custom_call_target="tpu_custom_call" | custom-call | flops 5549064192 | bytes 13762560 | tf_op jit(solution)/shard_map/pallas_call | solution.py:639
  236.6 16.9 %shard_map.282 = (bf16[2,4,336,1280]{3,2,1,0:T(8,128)(2,1)}, bf16[2,4,336,896]{3,2,1,0:T(8,128)(2,1)}, bf16[4,512,128]{2,1,0:T(8,128)(2,1)}, bf16[4,512,1280]{2,...) custom-call(s32[2]{0:T(128)} %copy-done.28, ...), custom_call_target="tpu_custom_call", output_to_operand_aliasing={{0}: (10, {}), {1}: (11, {}), {2}: (12, {}), {3}: (13, {})} | custom-call | flops 5549064192 | bytes 13762560 | tf_op jit(solution)/shard_map/pallas_call | solution.py:610
  258.4 17.2 %shard_map.285 = (bf16[2,4,336,1280]{3,2,1,0:T(8,128)(2,1)}, bf16[2,4,336,1792]{3,2,1,0:T(8,128)(2,1)}, bf16[4,512,256]{2,1,0:T(8,128)(2,1)}, bf16[4,512,1280]{2...) custom-call(s32[2]{0:T(128)} %copy-done.28, ...), custom_call_target="tpu_custom_call", output_to_operand_aliasing={{0}: (15, {}), {1}: (16, {}), {2}: (17, {}), {3}: (18, {})} | custom-call | flops 5549064192 | bytes 13762560 | tf_op jit(solution)/shard_map/pallas_call | solution.py:639
  276.2 16.8 %shard_map.283 = (bf16[2,4,336,1280]{3,2,1,0:T(8,128)(2,1)}, bf16[2,4,336,896]{3,2,1,0:T(8,128)(2,1)}, bf16[4,512,128]{2,1,0:T(8,128)(2,1)}, bf16[4,512,1280]{2,...) custom-call(s32[2]{0:T(128)} %copy-done.28, ...), custom_call_target="tpu_custom_call", output_to_operand_aliasing={{0}: (10, {}), {1}: (11, {}), {2}: (12, {}), {3}: (13, {})} | custom-call | flops 5549064192 | bytes 13762560 | tf_op jit(solution)/shard_map/pallas_call | solution.py:610
  293.9 17.4 %shard_map.286 = (bf16[2,4,336,1280]{3,2,1,0:T(8,128)(2,1)}, bf16[2,4,336,1792]{3,2,1,0:T(8,128)(2,1)}, bf16[4,512,256]{2,1,0:T(8,128)(2,1)}, bf16[4,512,1280]{2...) custom-call(s32[2]{0:T(128)} %copy-done.28, ...), custom_call_target="tpu_custom_call", output_to_operand_aliasing={{0}: (15, {}), {1}: (16, {}), {2}: (17, {}), {3}: (18, {})} | custom-call | flops 5549064192 | bytes 13762560 | tf_op jit(solution)/shard_map/pallas_call | solution.py:639
  312.6 17.2 %shard_map.287 = (bf16[2,4,336,1280]{3,2,1,0:T(8,128)(2,1)}, bf16[2,4,336,1792]{3,2,1,0:T(8,128)(2,1)}, bf16[4,512,256]{2,1,0:T(8,128)(2,1)}, bf16[4,512,1280]{2...) custom-call(s32[2]{0:T(128)} %copy-done.28, ...), custom_call_target="tpu_custom_call", output_to_operand_aliasing={{0}: (15, {}), {1}: (16, {}), {2}: (17, {}), {3}: (18, {})} | custom-call | flops 5549064192 | bytes 13762560 | tf_op jit(solution)/shard_map/pallas_call | solution.py:639
  334.7 19.4 %collective-permute-done.27 = bf16[256,1408]{1,0:T(8,128)(2,1)S(1)} collective-permute-done((bf16[256,1408]{1,0:T(8,128)(2,1)S(1)}, bf16[256,1408]{1,0:T(8,128)(2,1)S(1)}, u32[]{:S(2)}, u32[]{:S(2)}) %collective-permute-start.27) | collective-permute-done | bytes 720928 | tf_op jit(solution)/shard_map/ppermute | solution.py:347
  362.4 20.7 %attend_back.1 = (f32[256,1280]{1,0:T(8,128)}, bf16[1280,3968]{1,0:T(8,128)(2,1)}) custom-call(s32[1]{0:T(128)S(6)} %copy.177.length_ref, bf16[256,1280]{1,0:T(8,128)(2,1)} %get-tuple-element.201.low_ref, f32[256,1280]{1,0:T(8,128)} %get-tuple-element.202.wide_ref, bf16[256,1280]{1,0:T(8,128)(2,1)} %bitcast.154, f32[1,1280]{1,0:T(1,128)} %reshape.275.gain_ref, ...), custom_call_target="tpu_custom_call" | custom-call | flops 7549747200 | bytes 26214400 | tf_op jit(solution)/shard_map/attend_back/pallas_call | solution.py:688
  397.0 11.1 %bitcast_convert_fusion = bf16[1280,1792]{1,0:T(8,128)(2,1)S(1)} fusion(bf16[2,4,336,1792]{3,2,1,0:T(8,128)(2,1)} %get-tuple-element.212, bf16[2,4,336,1280]{3,2,1,0:T(8,128)(2,1)} %get-tuple-element.211), kind=kOutput, calls=%fused_computation.2 | convolution fusion | flops 6167920640 | bytes 12845056 | tf_op jit(solution)/shard_map/dot_general | solution.py:21
  433.5 41.3 %collective-permute-done.50 = bf16[112,640]{1,0:T(8,128)(2,1)} collective-permute-done((bf16[112,640]{1,0:T(8,128)(2,1)S(1)}, bf16[112,640]{1,0:T(8,128)(2,1)}, u32[]{:S(2)}, u32[]{:S(2)}) %collective-permute-start.50) | collective-permute-done | bytes 143392 | tf_op jit(solution)/shard_map/ppermute | solution.py:385
  512.8 20.3 %collective-permute-done.55 = bf16[2,224,1280]{2,1,0:T(8,128)(2,1)S(1)} collective-permute-done((bf16[2,224,1280]{2,1,0:T(8,128)(2,1)S(1)}, bf16[2,224,1280]{2,1,0:T(8,128)(2,1)S(1)}, u32[]{:S(2)}, u32[]{:S(2)}) %collective-permute-start.55) | collective-permute-done | bytes 1146912 | tf_op jit(solution)/shard_map/ppermute | solution.py:385
  539.2 12.0 %collective-permute-done.32 = bf16[256,1280]{1,0:T(8,128)(2,1)S(1)} collective-permute-done((bf16[256,1280]{1,0:T(8,128)(2,1)S(1)}, bf16[256,1280]{1,0:T(8,128)(2,1)S(1)}, u32[]{:S(2)}, u32[]{:S(2)}) %collective-permute-start.32) | collective-permute-done | bytes 655392 | tf_op jit(solution)/shard_map/ppermute | solution.py:347
  553.7 13.3 %collective-permute-done.58 = bf16[224,1280]{1,0:T(8,128)(2,1)S(1)} collective-permute-done((bf16[224,1280]{1,0:T(8,128)(2,1)S(1)}, bf16[224,1280]{1,0:T(8,128)(2,1)S(1)}, u32[]{:S(2)}, u32[]{:S(2)}) %collective-permute-start.58) | collective-permute-done | bytes 573472 | tf_op jit(solution)/shard_map/ppermute | solution.py:385
  575.7 13.8 %collective-permute-done.54 = bf16[320,1792]{1,0:T(8,128)(2,1)S(1)} collective-permute-done((bf16[320,1792]{1,0:T(8,128)(2,1)S(1)}, bf16[320,1792]{1,0:T(8,128)(2,1)S(1)}, u32[]{:S(2)}, u32[]{:S(2)}) %collective-permute-start.54) | collective-permute-done | bytes 1146912 | tf_op jit(solution)/shard_map/ppermute | solution.py:385
  614.7 10.0 %collective-permute-done.37 = bf16[160,1920]{1,0:T(8,128)(2,1)S(1)} collective-permute-done((bf16[160,1920]{1,0:T(8,128)(2,1)S(1)}, bf16[160,1920]{1,0:T(8,128)(2,1)S(1)}, u32[]{:S(2)}, u32[]{:S(2)}) %collective-permute-start.37) | collective-permute-done | bytes 614432 | tf_op jit(solution)/shard_map/ppermute | solution.py:385
  (339 shorter events, 218.0 us)
Async XLA Ops:
  7.2 49.8 %all-gather.6.cloned.1.call-start = ((), (), s32[]{:S(2)}) async-start(), calls=%async_computation.5 | async-start | bytes 1843200 | tf_op jit(solution)/shard_map/all_gather | solution.py:471
  9.0 111.0 %all-gather.4.cloned.1.call-start = ((), (), s32[]{:S(2)}) async-start(), calls=%async_computation.4 | async-start | bytes 7372800 | tf_op jit(solution)/shard_map/all_gather | solution.py:475
  13.0 103.7 %all-to-all-start = ((bf16[8,160,256]{2,1,0:T(8,128)(2,1)}), bf16[8,160,256]{2,1,0:T(8,128)(2,1)S(1)}, u32[]{:S(2)}, u32[]{:S(2)}) async-start(bf16[8,160,256]{2,1,0:T(8,128)(2,1)} %fusion.30), calls=%async_computation | async-start | bytes 1310720 | tf_op jit(solution)/shard_map/all_to_all | solution.py:522
  19.4 572.2 %reduce-scatter.5.cloned.1.call-start = ((), (), s32[]{:S(2)}) async-start(), calls=%async_computation.7 | async-start | bytes 4055040 | tf_op jit(solution)/shard_map/reduce_scatter | solution.py:702
  135.5 33.7 %collective-permute-start.15 = (bf16[256,1280]{1,0:T(8,128)(2,1)S(1)}, bf16[256,1280]{1,0:T(8,128)(2,1)S(1)}, u32[]{:S(2)}, u32[]{:S(2)}) collective-permute-start(bf16[256,1280]{1,0:T(8,128)(2,1)S(1)} %bitcast.167), channel_id=1, source_target_pairs={{0,2},{1,3},{2,4},{3,5},{4,6},{5,7},{6,0},{7,1},{8,10},{9,11},{10,... | collective-permute-start | bytes 1966088 | tf_op jit(solution)/shard_map/ppermute | solution.py:347
  155.1 44.5 %collective-permute-start.9 = (bf16[256,1280]{1,0:T(8,128)(2,1)S(1)}, bf16[256,1280]{1,0:T(8,128)(2,1)}, u32[]{:S(2)}, u32[]{:S(2)}) collective-permute-start(bf16[256,1280]{1,0:T(8,128)(2,1)S(1)} %collective-permute-done.8.s0_ref), channel_id=1, source_target_pairs={{0,1},{1,0},{2,3},{3,2},{4,5},{5,4},{6,7},{7,6},{8,9},{9,8},{10,11... | collective-permute-start | bytes 1966088 | tf_op jit(solution)/shard_map/ppermute | solution.py:352
  169.1 47.6 %collective-permute-start.20 = (bf16[256,1280]{1,0:T(8,128)(2,1)S(1)}, bf16[256,1280]{1,0:T(8,128)(2,1)S(1)}, u32[]{:S(2)}, u32[]{:S(2)}) collective-permute-start(bf16[256,1280]{1,0:T(8,128)(2,1)S(1)} %collective-permute-done.15.g0_ref), channel_id=1, source_target_pairs={{0,1},{1,0},{2,3},{3,2},{4,5},{5,4},{6,7},{7,6},{8,9},{9,8},{10,11... | collective-permute-start | bytes 1966088 | tf_op jit(solution)/shard_map/ppermute | solution.py:352
  182.4 34.0 %collective-permute-start.12 = (bf16[256,1280]{1,0:T(8,128)(2,1)S(1)}, bf16[256,1280]{1,0:T(8,128)(2,1)}, u32[]{:S(2)}, u32[]{:S(2)}) collective-permute-start(bf16[256,1280]{1,0:T(8,128)(2,1)S(1)} %collective-permute-done.10.s0_ref), channel_id=1, source_target_pairs={{0,2},{1,3},{2,4},{3,5},{4,6},{5,7},{6,0},{7,1},{8,10},{9,11},{10,... | collective-permute-start | bytes 1966088 | tf_op jit(solution)/shard_map/ppermute | solution.py:347
  199.5 36.5 %collective-permute-start.11 = (bf16[256,1280]{1,0:T(8,128)(2,1)S(1)}, bf16[256,1280]{1,0:T(8,128)(2,1)}, u32[]{:S(2)}, u32[]{:S(2)}) collective-permute-start(bf16[256,1280]{1,0:T(8,128)(2,1)S(1)} %collective-permute-done.10.s0_ref), channel_id=1, source_target_pairs={{0,1},{1,0},{2,3},{3,2},{4,5},{5,4},{6,7},{7,6},{8,9},{9,8},{10,11... | collective-permute-start | bytes 1966088 | tf_op jit(solution)/shard_map/ppermute | solution.py:352
  235.4 77.2 %collective-permute-start.14 = (bf16[256,1280]{1,0:T(8,128)(2,1)S(1)}, bf16[256,1280]{1,0:T(8,128)(2,1)}, u32[]{:S(2)}, u32[]{:S(2)}) collective-permute-start(bf16[256,1280]{1,0:T(8,128)(2,1)S(1)} %bitcast.168), channel_id=1, source_target_pairs={{0,1},{1,0},{2,3},{3,2},{4,5},{5,4},{6,7},{7,6},{8,9},{9,8},{10,11... | collective-permute-start | bytes 1966088 | tf_op jit(solution)/shard_map/ppermute | solution.py:352
  235.5 40.7 %collective-permute-start.13 = (bf16[256,1280]{1,0:T(8,128)(2,1)}, bf16[256,1280]{1,0:T(8,128)(2,1)}, u32[]{:S(2)}, u32[]{:S(2)}) collective-permute-start(bf16[256,1280]{1,0:T(8,128)(2,1)} %collective-permute-done.12.s0_ref), channel_id=1, source_target_pairs={{0,1},{1,0},{2,3},{3,2},{4,5},{5,4},{6,7},{7,6},{8,9},{9,8},{10,11... | collective-permute-start | bytes 1966088 | tf_op jit(solution)/shard_map/ppermute | solution.py:352
  253.7 57.7 %collective-permute-start.25 = (bf16[256,1408]{1,0:T(8,128)(2,1)S(1)}, bf16[256,1408]{1,0:T(8,128)(2,1)S(1)}, u32[]{:S(2)}, u32[]{:S(2)}) collective-permute-start(bf16[256,1408]{1,0:T(8,128)(2,1)S(1)} %add_convert_fusion.2), channel_id=1, source_target_pairs={{0,2},{1,3},{2,4},{3,5},{4,6},{5,7},{6,0},{7,1},{8,10},{9,11},{10,... | collective-permute-start | bytes 2162696 | tf_op jit(solution)/shard_map/ppermute | solution.py:347
  258.4 34.6 %collective-permute-start.18 = (bf16[256,1280]{1,0:T(8,128)(2,1)}, bf16[256,1280]{1,0:T(8,128)(2,1)S(1)}, u32[]{:S(2)}, u32[]{:S(2)}) collective-permute-start(bf16[256,1280]{1,0:T(8,128)(2,1)} %collective-permute-done.17.g0_ref), channel_id=1, source_target_pairs={{0,1},{1,0},{2,3},{3,2},{4,5},{5,4},{6,7},{7,6},{8,9},{9,8},{10,11... | collective-permute-start | bytes 1966088 | tf_op jit(solution)/shard_map/ppermute | solution.py:352
  275.6 35.8 %collective-permute-start.23 = (bf16[256,1408]{1,0:T(8,128)(2,1)}, bf16[256,1408]{1,0:T(8,128)(2,1)S(1)}, u32[]{:S(2)}, u32[]{:S(2)}) collective-permute-start(bf16[256,1408]{1,0:T(8,128)(2,1)} %get-tuple-element.190), channel_id=1, source_target_pairs={{0,1},{1,0},{2,3},{3,2},{4,5},{5,4},{6,7},{7,6},{8,9},{9,8},{10,11... | collective-permute-start | bytes 2162696 | tf_op jit(solution)/shard_map/ppermute | solution.py:352
  362.4 248.1 %reduce-scatter.3.cloned.1.call-start = ((), (), s32[]{:S(2)}) async-start(), calls=%async_computation.6 | async-start | bytes 11427840 | tf_op jit(solution)/shard_map/reduce_scatter | solution.py:703
  389.4 40.5 %all-to-all-start.1 = ((bf16[8,160,256]{2,1,0:T(8,128)(2,1)}), bf16[8,160,256]{2,1,0:T(8,128)(2,1)S(1)}, u32[]{:S(2)}, u32[]{:S(2)}) async-start(bf16[8,160,256]{2,1,0:T(8,128)(2,1)} %bitcast.20), calls=%async_computation.3 | async-start | bytes 1310720 | tf_op jit(solution)/shard_map/all_to_all | solution.py:673
  419.5 85.6 %collective-permute-start.51 = (bf16[2,320,1792]{2,1,0:T(8,128)(2,1)S(1)}, bf16[2,320,1792]{2,1,0:T(8,128)(2,1)}, u32[]{:S(2)}, u32[]{:S(2)}) collective-permute-start(bf16[2,320,1792]{2,1,0:T(8,128)(2,1)S(1)} %dynamic-slice_bitcast_fusion.1), channel_id=1, source_target_pairs={{0,8},{8,0},{16,24},{24,16},{1,9},{9,1},{17,25},{25,17},{2,10},{10... | collective-permute-start | bytes 6881288 | tf_op jit(solution)/shard_map/ppermute | solution.py:385
  426.8 82.7 %collective-permute-start.53 = (bf16[2,320,1792]{2,1,0:T(8,128)(2,1)}, bf16[2,320,1792]{2,1,0:T(8,128)(2,1)}, u32[]{:S(2)}, u32[]{:S(2)}) collective-permute-start(bf16[2,320,1792]{2,1,0:T(8,128)(2,1)} %dynamic-slice_bitcast_fusion), channel_id=1, source_target_pairs={{0,16},{8,24},{16,0},{24,8},{1,17},{9,25},{17,1},{25,9},{2,18},{10... | collective-permute-start | bytes 6881288 | tf_op jit(solution)/shard_map/ppermute | solution.py:385
  427.4 47.4 %collective-permute-start.50 = (bf16[112,640]{1,0:T(8,128)(2,1)S(1)}, bf16[112,640]{1,0:T(8,128)(2,1)}, u32[]{:S(2)}, u32[]{:S(2)}) collective-permute-start(bf16[112,640]{1,0:T(8,128)(2,1)S(1)} %get-tuple-element.315), channel_id=1, source_target_pairs={{0,8},{8,0},{16,24},{24,16},{1,9},{9,1},{17,25},{25,17},{2,10},{10... | collective-permute-start | bytes 430088 | tf_op jit(solution)/shard_map/ppermute | solution.py:385
  431.1 53.2 %collective-permute-start.45 = (bf16[160,896]{1,0:T(8,128)(2,1)}, bf16[160,896]{1,0:T(8,128)(2,1)}, u32[]{:S(2)}, u32[]{:S(2)}) collective-permute-start(bf16[160,896]{1,0:T(8,128)(2,1)} %reshape.264), channel_id=1, source_target_pairs={{0,16},{8,24},{16,0},{24,8},{1,17},{9,25},{17,1},{25,9},{2,18},{10... | collective-permute-start | bytes 860168 | tf_op jit(solution)/shard_map/ppermute | solution.py:385
  502.2 101.4 %collective-permute-start.28 = (bf16[256,1280]{1,0:T(8,128)(2,1)}, bf16[256,1280]{1,0:T(8,128)(2,1)}, u32[]{:S(2)}, u32[]{:S(2)}) collective-permute-start(bf16[256,1280]{1,0:T(8,128)(2,1)} %get-tuple-element.194), channel_id=1, source_target_pairs={{0,1},{1,0},{2,3},{3,2},{4,5},{5,4},{6,7},{7,6},{8,9},{9,8},{10,11... | collective-permute-start | bytes 1966088 | tf_op jit(solution)/shard_map/ppermute | solution.py:352
  503.6 87.6 %collective-permute-start.29 = (bf16[256,1280]{1,0:T(8,128)(2,1)S(1)}, bf16[256,1280]{1,0:T(8,128)(2,1)S(1)}, u32[]{:S(2)}, u32[]{:S(2)}) collective-permute-start(bf16[256,1280]{1,0:T(8,128)(2,1)S(1)} %copy-done.35), channel_id=1, source_target_pairs={{0,1},{1,0},{2,3},{3,2},{4,5},{5,4},{6,7},{7,6},{8,9},{9,8},{10,11... | collective-permute-start | bytes 1966088 | tf_op jit(solution)/shard_map/ppermute | solution.py:352
  537.7 37.7 %collective-permute-start.52 = (bf16[320,1792]{1,0:T(8,128)(2,1)S(1)}, bf16[320,1792]{1,0:T(8,128)(2,1)S(1)}, u32[]{:S(2)}, u32[]{:S(2)}) collective-permute-start(bf16[320,1792]{1,0:T(8,128)(2,1)S(1)} %dynamic-slice_bitcast_fusion.5), channel_id=1, source_target_pairs={{0,16},{8,24},{16,0},{24,8},{1,17},{9,25},{17,1},{25,9},{2,18},{10... | collective-permute-start | bytes 3440648 | tf_op jit(solution)/shard_map/ppermute | solution.py:385
  552.9 36.6 %collective-permute-start.54 = (bf16[320,1792]{1,0:T(8,128)(2,1)S(1)}, bf16[320,1792]{1,0:T(8,128)(2,1)S(1)}, u32[]{:S(2)}, u32[]{:S(2)}) collective-permute-start(bf16[320,1792]{1,0:T(8,128)(2,1)S(1)} %dynamic-slice_bitcast_fusion.4), channel_id=1, source_target_pairs={{0,8},{8,0},{16,24},{24,16},{1,9},{9,1},{17,25},{25,17},{2,10},{10... | collective-permute-start | bytes 3440648 | tf_op jit(solution)/shard_map/ppermute | solution.py:385
  (90 other events, 1273.7 us)
Sparse Core Ops, SparseCore 0:
  10.2 42.0 all-gather.5
  54.6 65.4 all-gather.3
  362.5 47.8 reduce-scatter.4
  412.6 111.3 reduce-scatter.2

commit v3 on v2

--- a/solution.py
+++ b/solution.py
@@ -73,7 +73,8 @@
 
 
 def attend_kernel(
-    pair, length_ref, x_ref, gain_ref, cos_ref, sin_ref, wq_ref, wk_ref, wv_ref, qkv_ref, out_ref, normed
+    pair, turn_over, length_ref, x_ref, gain_ref, cos_ref, sin_ref, wq_ref, wk0_ref, wk1_ref, wv_ref,
+    qkv_ref, out_ref, normed,
 ):
     seq = x_ref.shape[0]
     part = pair * HEAD_DIM
@@ -83,7 +84,8 @@
         x = x_ref[...].astype(WIDE)
         normed[...] = (x * inverse_rms(x) * gain_ref[...]).astype(LOW)
 
-    pre_q, pre_k, pre_v = (dot(normed[...], w[...]) for w in (wq_ref, wk_ref, wv_ref))
+    wk = jnp.where(pl.program_id(0) < turn_over, wk0_ref[...], wk1_ref[...])
+    pre_q, pre_k, pre_v = (dot(normed[...], w) for w in (wq_ref[...], wk, wv_ref[...]))
     allowed = allowed_keys(seq, length_ref[0])
     cosine, sine = cos_ref[...], sin_ref[...]
     for i in range(pair):
@@ -148,8 +150,8 @@
 
 
 def attend_back_kernel(
-    pair, length_ref, low_ref, wide_ref, x_ref, gain_ref, cos_ref, sin_ref, qkv_ref, wq_ref, wk_ref, wv_ref,
-    wo_ref, tokens_ref, grads_ref, normed, total, ready, gain_ready, sems,
+    pair, turn_over, length_ref, low_ref, wide_ref, x_ref, gain_ref, cos_ref, sin_ref, qkv_ref, wq_ref, wk0_ref, wk1_ref,
+    wv_ref, wo_ref, tokens_ref, grads_ref, last_ref, normed, total, ready, gain_ready, sems,
 ):
     seq, width = x_ref.shape
     part = pair * HEAD_DIM
@@ -160,10 +162,9 @@
     def leave(n, at):
         copies = []
         for i in range(3):
-            columns = pl.ds(pl.multiple_of(i * width + n * part, LANES), part)
-            copies.append(
-                pltpu.make_async_copy(ready.at[at, i], grads_ref.at[:, columns], sems.at[at, i])
-            )
+            columns = pl.ds(pl.multiple_of(i % 2 * width + n * part, LANES), part)
+            place = (last_ref if i == 2 else grads_ref).at[:, columns]
+            copies.append(pltpu.make_async_copy(ready.at[at, i], place, sems.at[at, i]))
         return copies
 
     @pl.when(step == 0)
@@ -196,9 +197,10 @@
         for copy in leave(step - 2, slot):
             copy.wait()
 
-    for i, w_ref in enumerate((wq_ref, wk_ref, wv_ref)):
+    wk = jnp.where(step < turn_over, wk0_ref[...], wk1_ref[...])
+    for i, w in enumerate((wq_ref[...], wk, wv_ref[...])):
         piece = g[:, i * part : (i + 1) * part]
-        total[...] += dot_t(piece, w_ref[...])
+        total[...] += dot_t(piece, w)
         ready[slot, i] = dot_rows(normed[...], piece).astype(LOW)
     for copy in leave(step, slot):
         copy.start()
@@ -215,7 +217,7 @@
         first = jnp.where(iota((8, width), 0) == 0, jnp.broadcast_to(g_gain, (8, width)), 0.0)
         mark = ((iota((8, LANES), 0) == 0) & (iota((8, LANES), 1) == 0)).astype(LOW)
         gain_ready[...] = dot_rows(first.astype(LOW), mark).astype(LOW)
-        last = pltpu.make_async_copy(gain_ready, grads_ref.at[:, 3 * width :], sems.at[2, 0])
+        last = pltpu.make_async_copy(gain_ready, last_ref.at[:, width:], sems.at[2, 0])
         last.start()
         for copy in leave(step - 1, 1 - slot) + leave(step, slot) + [last]:
             copy.wait()
@@ -367,16 +369,19 @@
     return blocks
 
 
-def ring_sum(parts):
+def ring_sum(parts, needed=None):
     chips = len(parts)
     total = None
     for k in [*range(1, chips), 0]:
         mine = (parts[k][0], partner(parts[k][1]))
         if total is None:
-            total = add(*mine)
+            total = add(*mine).astype(LOW)
+            if needed is not None:
+                total, _ = after_that(total, needed)
         else:
-            total = around(total.astype(LOW))
+            total = around(total)
             total = add(*mine, total)
+            total = total.astype(LOW) if k else total
     return total
 
 
@@ -405,21 +410,21 @@
     return jnp.concatenate(parts, axis=1)
 
 
-def dp_scatter(x, order, axis=0):
+def scatter_leg(x, order, leg):
+    bit = order[leg]
+    left = sorted(order[leg:], reverse=True)
     me = lax.axis_index("dp")
-    left = list(reversed(dp_bits()))
-    lead, tail = x.shape[:axis], x.shape[axis + 1 :]
-    x = x.reshape(*lead, *(2 for _ in left), x.shape[axis] // lax.axis_size("dp"), *tail)
-    for bit in order:
-        at = axis + left.index(bit)
-        mine = (me // bit) % 2
-        kept = lax.dynamic_index_in_dim(x, mine, at, keepdims=False)
-        sent = lax.dynamic_index_in_dim(x, 1 - mine, at, keepdims=False)
-        got = exchange(sent, bit)
-        left.remove(bit)
-        total = kept.astype(WIDE) + got.astype(WIDE)
-        x = total if not left else total.astype(LOW)
-    return x
+    if x.ndim == 2:
+        x = x.reshape(*(2 for _ in left), x.shape[0] // lax.axis_size("dp"), x.shape[1])
+    at = left.index(bit)
+    mine = (me // bit) % 2
+    kept = lax.dynamic_index_in_dim(x, mine, at, keepdims=False)
+    sent = lax.dynamic_index_in_dim(x, 1 - mine, at, keepdims=False)
+    return kept, exchange(sent, bit)
+
+
+def chained(xs, needed):
+    return lax.optimization_barrier((xs, needed))[0]
 
 
 def after_that(x, needed):
@@ -466,46 +471,58 @@
 
     count = lax.axis_size("dp")
     dp = lax.axis_index("dp")
-    vo_local = jnp.concatenate([value_weight, out_weight], axis=1)
-    strip = 2 * width // count
-    vo_part = lax.all_gather(
-        lax.dynamic_slice_in_dim(vo_local, dp * strip, strip, 1), "expert", axis=0, tiled=True
+    near = part
+    far_local = jnp.concatenate([out_weight, value_weight, key_weight[:, near:]], axis=1)
+    strip = far_local.shape[1] // count
+    per_row = -(-seq * top // rows_w)
+    routes_low = jnp.pad(routes[0].reshape(-1).astype(LOW), (0, per_row * rows_w - seq * top))
+    small = jnp.concatenate(
+        [router_weight, attn_gain[:, None], ffn_gain[:, None], routes_low.reshape(rows_w, per_row)], axis=1
     )
-    qk = jnp.concatenate([query_weight, key_weight], axis=1)
+    small_lanes = -(-small.shape[1] // LANES) * LANES
+    small = jnp.pad(small, ((0, 0), (0, small_lanes - small.shape[1])))
+    far_part = jnp.concatenate([lax.dynamic_slice_in_dim(far_local, dp * strip, strip, 1), small], axis=1)
+    far_part = lax.all_gather(far_part, "expert", axis=0, tiled=True)
+    w_gu = jnp.concatenate([expert_gate, expert_up], axis=2)
+    far_part = chained(far_part, w_gu)
+    far_part, small = far_part[:, :strip], far_part[:, strip:]
+    router = jnp.where(jnp.arange(small_lanes, dtype=INT)[None, :] < routed, small, jnp.zeros_like(small))
+    router = router[:, :LANES]
+    gain_a = small[:, routed].reshape(1, width).astype(WIDE)
+    gain_f = small[:, routed + 1].reshape(1, width).astype(WIDE)
+    routes_all = small[:, routed + 2 : routed + 2 + per_row].reshape(group, rows_w * per_row)
+    routes_all = routes_all[:, : seq * top].reshape(group, seq, top).astype(INT)
+    qk = jnp.concatenate([query_weight, key_weight[:, :near]], axis=1)
     qk = lax.all_gather(qk, "expert", axis=0, tiled=True)
     half = width // 2
     core = place_of_me % 2
-    pieces = [lax.dynamic_slice_in_dim(vo_part, core * half, half, 0)]
-    for bit in dp_bits():
-        pieces += [exchange(p, bit) for p in pieces]
-    placed = [(p, core ^ other, dp ^ n) for n, piece in enumerate(pieces)
-              for other, p in enumerate((piece, partner(piece)))]
+    first = lax.dynamic_slice_in_dim(far_part, core * half, half, 0)
+    if count == 4:
+        one, two = exchange(first, 1), exchange(first, 2)
+        cut = half // 2
+        pieces = [(first, 0, 0), (one, 0, 1), (two, 0, 2),
+                  (exchange(one[:cut], 2), 0, 3), (exchange(two[cut:], 1), cut, 3)]
+    else:
+        pieces = [(first, 0, 0)]
+        for bit in dp_bits():
+            pieces += [(exchange(p, bit), r, n ^ bit) for p, r, n in pieces]
+    placed = []
+    for p, r, n in pieces:
+        for other, x in enumerate((p, partner(p))):
+            rows = x.shape[0]
+            placed.append((x, (core ^ other) * (half // rows) + r // rows, dp ^ n))
     smem = pl.BlockSpec(memory_space=pltpu.SMEM)
-    vo = pl.pallas_call(
+    far = pl.pallas_call(
         assemble_kernel,
         in_specs=[smem, smem] + [pl.BlockSpec(memory_space=pltpu.VMEM)] * len(placed),
         out_specs=pl.BlockSpec(memory_space=pl.ANY),
-        out_shape=shape((width, 2 * width), LOW),
+        out_shape=pltpu.HBM((width, strip * count), LOW),
         scratch_shapes=[pltpu.SemaphoreType.DMA((len(placed),))],
         cost_estimate=cost(0, 8 * width * width),
+        compiler_params=pltpu.CompilerParams(vmem_limit_bytes=24 << 20),
         name="assemble",
     )(jnp.stack([p[1] for p in placed]), jnp.stack([p[2] for p in placed]), *(p[0] for p in placed))
 
-    small = jnp.concatenate(
-        [attn_gain, ffn_gain, router_weight.reshape(-1), routes[0].reshape(-1).astype(LOW)]
-    )
-    length_small = small.shape[0]
-    small = jnp.pad(small, (0, -length_small % LANES)).reshape(-1, LANES)
-    small_all = lax.all_gather(small, "expert", axis=0, tiled=True).reshape(group, -1)
-    at = 0
-    pieces = []
-    for n in (rows_w, rows_w, rows_w * routed, seq * top):
-        pieces.append(small_all[:, at : at + n])
-        at += n
-    gain_a = pieces[0].reshape(1, width).astype(WIDE)
-    gain_f = pieces[1].reshape(1, width).astype(WIDE)
-    router = jnp.pad(pieces[2].reshape(width, routed), ((0, 0), (0, LANES - routed)))
-    routes_all = pieces[3].reshape(group, seq, top).astype(INT)
     chips = group // 2
     back = jnp.arange(chips, dtype=INT)[:, None]
     met = 2 * ((place_of_me // 2 - back) % chips) + (core ^ jnp.arange(2, dtype=INT)[None, :])
@@ -519,10 +536,10 @@
         return x[..., :ff_part]
 
     cols_local = jnp.concatenate([to_columns(shared_gate), to_columns(shared_up)], axis=2)
+    cols_local = chained(cols_local, far_part)
     cols = lax.all_to_all(cols_local, "expert", split_axis=0, concat_axis=0, tiled=True)
     shared_cols = cols.reshape(width, 2 * fp)
     shared_rows = jnp.pad(shared_down, ((0, fp - ff_part), (0, 0)))
-    w_gu = jnp.concatenate([expert_gate, expert_up], axis=2)
 
     my_slots = place_of_me * local + jnp.arange(local, dtype=INT)
     positions = jnp.arange(seq, dtype=INT)
@@ -543,20 +560,30 @@
 
     x_low = tokens[0]
     incoming = cotangent[0]
-    early = (shared_cols, shared_rows, w_gu, place_row, place_col, router)
+    early = (shared_rows, w_gu, place_row, place_col, router)
     qk, early = after_that(qk, early)
     incoming, qk = after_that(incoming, qk)
-    shared_cols, shared_rows, w_gu, place_row, place_col, router = early
+    shared_rows, w_gu, place_row, place_col, router = early
 
     def columns(n):
         return pl.BlockSpec((seq, n), lambda h: (0, h))
 
-    qkv_specs = [pl.BlockSpec((width, part), lambda h: (0, h)),
-                 pl.BlockSpec((width, part), lambda h: (0, steps + h)),
-                 pl.BlockSpec((width, part), lambda h: (0, h))]
+    def stored(*xs):
+        return [pltpu.with_memory_space_constraint(x, pltpu.HBM) for x in xs]
+
+    qk, far = stored(qk, far)
+
+    def weight_columns(place):
+        return pl.BlockSpec((width, part), lambda h: (0, place(h)))
+
+    turn_over = near // part
+    qkv_specs = [weight_columns(lambda h: h),
+                 weight_columns(lambda h: steps + jnp.minimum(h, turn_over - 1)),
+                 weight_columns(lambda h: 2 * steps + jnp.maximum(h - turn_over, 0)),
+                 weight_columns(lambda h: steps + h)]
 
     saved, attended = pl.pallas_call(
-        functools.partial(attend_kernel, pair),
+        functools.partial(attend_kernel, pair, turn_over),
         grid=(steps,),
         in_specs=[smem, whole((seq, width)), whole((1, width)), whole((seq, HEAD_DIM)),
                   whole((seq, HEAD_DIM)), *qkv_specs],
@@ -564,18 +591,20 @@
         out_shape=[shape((seq, 3 * width), LOW), shape((seq, width), LOW)],
         scratch_shapes=[pltpu.VMEM((seq, width), LOW)],
         cost_estimate=cost(2 * seq * width * 3 * width * 1.3, 6 * width * width),
+        compiler_params=pltpu.CompilerParams(vmem_limit_bytes=24 << 20),
         name="attend",
-    )(lengths, x_low, gain_a, cosine, sine, qk, qk, vo)
+    )(lengths, x_low, gain_a, cosine, sine, qk, qk, far, far)
     middle, second = pl.pallas_call(
         project_kernel,
         grid=(1,),
-        in_specs=[whole((seq, width)), pl.BlockSpec((width, width), lambda _: (0, 1)),
+        in_specs=[whole((seq, width)), pl.BlockSpec((width, width), lambda _: (0, 0)),
                   whole((seq, width)), whole((1, width))],
         out_specs=[whole((seq, width)), whole((seq, width))],
         out_shape=[shape((seq, width), WIDE), shape((seq, width), LOW)],
         cost_estimate=cost(2 * seq * width * width, 4 * width * width),
+        compiler_params=pltpu.CompilerParams(vmem_limit_bytes=24 << 20),
         name="project",
-    )(attended, vo, x_low, gain_f)
+    )(attended, far, x_low, gain_f)
 
     anywhere = pl.BlockSpec(memory_space=pl.ANY)
     tok, row = 2 * seq, 2 * cap
@@ -586,7 +615,7 @@
                     whole((width, 2 * fp)), whole((fp, width))]
 
     def low(*dims):
-        return shape(dims, LOW)
+        return pltpu.HBM(dims, LOW)
 
     def per_slot(k, r, n):
         return pl.BlockSpec((1, 1, r, n), lambda e: (e, k, 0, 0))
@@ -601,12 +630,16 @@
         return [pl.BlockSpec((1, 2, 1, seq), lambda e: (e, k, 0, 0)),
                 pl.BlockSpec((tok, LANES), lambda e: (k, 0))]
 
+    def held(x):
+        return pltpu.with_memory_space_constraint(x, pltpu.VMEM)
+
+    weights = (held(w_gu), held(expert_down), shared_cols, shared_rows)
     kept, parts = [], []
     store = ()
     blocks = ring_gather(second)
     for k in range(chips):
         store_in = [anywhere] * len(store)
-        fixed = (my_slots, *blocks[k], place_row, place_col, router, *weights)
+        fixed = (my_slots, *blocks[k], *stored(place_row, place_col), router, *weights)
         out = pl.pallas_call(
             functools.partial(experts_kernel, routed),
             grid=(local,),
@@ -618,12 +651,13 @@
                        whole((seq, width)), whole((seq, width))],
             out_shape=[low(local, chips, row, width), low(local, chips, row, ff), low(chips, tok, fp),
                        low(chips, tok, width), low(local, row, ff), low(local, row, ff),
-                       low(local, tok, width), shape((tok, LANES), WIDE), low(tok, fp), low(tok, fp),
+                       low(local, tok, width), pltpu.HBM((tok, LANES), WIDE), low(tok, fp), low(tok, fp),
                        low(seq, width), low(seq, width)],
             scratch_shapes=[pltpu.VMEM((tok, width), WIDE)],
             input_output_aliases={len(fixed) + i: i for i in range(len(store))},
             cost_estimate=cost(flops * 1.2, 6 * local * width * ff),
-        )(*fixed, *store)
+            compiler_params=pltpu.CompilerParams(vmem_limit_bytes=42 << 20),
+        )(*fixed, *stored(*store))
         store = tuple(out[:4])
         kept.append(out[4:10])
         parts.append(out[10:])
@@ -635,7 +669,8 @@
     for k in [*range(1, chips), 0]:
         act_a, act_b, picked, probs, s_a, s_b = kept[k]
         store_in = [anywhere] * len(store)
-        fixed = (my_slots, *blocks[k], place_row, place_col, probs, picked, act_a, act_b, *weights, s_a, s_b)
+        fixed = (my_slots, *blocks[k], *stored(place_row, place_col, probs, picked, act_a, act_b), *weights,
+                 *stored(s_a, s_b))
         out = pl.pallas_call(
             functools.partial(experts_back_kernel, slot_count),
             grid=(local,),
@@ -650,7 +685,8 @@
             scratch_shapes=[pltpu.VMEM((tok, width), WIDE), pltpu.VMEM((tok, LANES), WIDE)],
             input_output_aliases={len(fixed) + i: i for i in range(len(store))},
             cost_estimate=cost(flops * 1.2, 6 * local * width * ff),
-        )(*fixed, *store)
+            compiler_params=pltpu.CompilerParams(vmem_limit_bytes=42 << 20),
+        )(*fixed, *stored(*store))
         store = tuple(out[:4])
         back_parts[k] = out[4:]
     grows, g_gu, g_s, up_all = store
@@ -662,20 +698,6 @@
     s_hidden, second_all, g_s, up_all = (
         x.reshape(chips * tok, x.shape[-1]) for x in (s_hidden, second_all, g_s, up_all)
     )
-
-    bits = dp_bits()
-    orders = [bits if n % 2 == 0 else bits[::-1] for n in range(local)]
-    wide_gu = [dot_rows(rows[n], g_gu[n]).astype(LOW) for n in range(local)]
-    wide_gu = [dp_scatter(wide_gu[n], orders[n]) for n in range(local)]
-
-    g_cols = dot_rows(second_all, g_s).astype(LOW)
-    grad_sdown = dot_rows(s_hidden, up_all).astype(LOW)[:ff_part]
-    g_cols = lax.all_to_all(g_cols.reshape(group, rows_w, 2 * fp), "expert", split_axis=0, concat_axis=0, tiled=True)
-    g_cols = g_cols.transpose(1, 0, 2)
-    grad_sgate = trim(g_cols[:, :, :fp]).reshape(rows_w, ff)
-    grad_sup = trim(g_cols[:, :, fp:]).reshape(rows_w, ff)
-    shared_sum = dp_sum(jnp.concatenate([grad_sgate, grad_sup], axis=1))
-    sdown_sum = dp_sum(grad_sdown)
 
     g_middle, g_low, grads_out = pl.pallas_call(
         functools.partial(middle_kernel, routed, slot_count),
@@ -685,31 +707,59 @@
         name="middle_back",
     )(back_sum, second, router, middle, gain_f, incoming, attended)
 
-    grad_tokens, grads_qkv = pl.pallas_call(
-        functools.partial(attend_back_kernel, pair),
+    bits = dp_bits()
+    orders = [bits if n % 2 == 0 else bits[::-1] for n in range(local)]
+    rows, g_gu, _ = lax.optimization_barrier((rows, g_gu, g_low))
+    gu = [dot_rows(rows[n], g_gu[n]).astype(LOW) for n in range(local)]
+    g_low, gu = after_that(g_low, gu)
+    gu = [scatter_leg(gu[n], orders[n], 0) for n in range(local)]
+
+    grad_tokens, grads_qk, grads_v = pl.pallas_call(
+        functools.partial(attend_back_kernel, pair, turn_over),
         grid=(steps,),
         in_specs=[smem, whole((seq, width)), whole((seq, width)), whole((seq, width)),
                   whole((1, width)), whole((seq, HEAD_DIM)), whole((seq, HEAD_DIM)),
-                  columns(3 * part), *qkv_specs, pl.BlockSpec((part, width), lambda h: (h, 1))],
-        out_specs=[whole((seq, width)), pl.BlockSpec(memory_space=pl.ANY)],
-        out_shape=[shape((seq, width), WIDE), shape((width, 3 * width + LANES), LOW)],
+                  columns(3 * part), *qkv_specs, pl.BlockSpec((part, width), lambda h: (h, 0))],
+        out_specs=[whole((seq, width))] + [pl.BlockSpec(memory_space=pl.ANY)] * 2,
+        out_shape=[shape((seq, width), WIDE), shape((width, 2 * width), LOW),
+                   shape((width, width + LANES), LOW)],
         scratch_shapes=[pltpu.VMEM((seq, width), LOW), pltpu.VMEM((seq, width), WIDE),
                         pltpu.VMEM((2, 3, width, part), LOW), pltpu.VMEM((width, LANES), LOW),
                         pltpu.SemaphoreType.DMA((3, 3))],
         cost_estimate=cost(2 * seq * width * 3 * width * 3, 16 * width * width),
         name="attend_back",
-    )(lengths, g_low, g_middle, x_low, gain_a, cosine, sine, saved, qk, qk, vo, vo)
+    )(lengths, g_low, g_middle, x_low, gain_a, cosine, sine, saved, qk, qk, far, far, far)
     out_sum = lax.psum_scatter(grads_out, "expert", scatter_dimension=0, tiled=True)
-    qkv_sum = lax.psum_scatter(grads_qkv, "expert", scatter_dimension=0, tiled=True)
+    qk_sum = lax.psum_scatter(grads_qk, "expert", scatter_dimension=0, tiled=True)
+    v_sum = lax.psum_scatter(grads_v, "expert", scatter_dimension=0, tiled=True)
+
+    hidden, grows, g_s, s_hidden = chained((hidden, grows, g_s, s_hidden), grad_tokens)
+    down = [dot_rows(hidden[n], grows[n]).astype(LOW) for n in range(local)]
+    down = [scatter_leg(down[n], orders[n], 0) for n in range(local)]
+    g_cols = dot_rows(second_all, g_s).astype(LOW)
+    grad_sdown = dot_rows(s_hidden, up_all).astype(LOW)[:ff_part]
+    g_all = lax.all_to_all(
+        g_cols.reshape(group, rows_w, 2 * fp), "expert", split_axis=0, concat_axis=0, tiled=True
+    )
+
+    gu = chained(gu, ([x[0] for x in down], g_cols))
+    gu = [scatter_leg(add(*x).astype(LOW), orders[n], 1) for n, x in enumerate(gu)]
+    down = chained(down, [x[0] for x in gu])
+    down = [scatter_leg(add(*x).astype(LOW), orders[n], 1) for n, x in enumerate(down)]
+    g_cols = chained(g_all, [x[0] for x in down]).transpose(1, 0, 2)
+    grad_sgate = trim(g_cols[:, :, :fp]).reshape(rows_w, ff)
+    grad_sup = trim(g_cols[:, :, fp:]).reshape(rows_w, ff)
+    shared_cut = jnp.concatenate([grad_sgate, grad_sup], axis=1)
+    gu, down = chained((gu, down), ([x[0] for x in down], shared_cut))
+    shared_sum = dp_sum(shared_cut)
+    sdown_sum = dp_sum(grad_sdown)
+    wide_gu = jnp.stack([add(*x) for x in gu])
+    wide_down = jnp.stack([add(*x) for x in down])
     out_sum = dp_sum(out_sum)
-    qkv_sum = dp_sum(qkv_sum)
-
-    hidden, grows, _ = lax.optimization_barrier((hidden, grows, grad_tokens))
-    wide_down = [dp_scatter(dot_rows(hidden[n], grows[n]).astype(LOW), orders[n]) for n in range(local)]
-    wide_gu, wide_down = jnp.stack(wide_gu), jnp.stack(wide_down)
-
-    parts, _ = after_that(parts, back_sum)
-    output = (middle + ring_sum(parts)).astype(LOW)
+    qk_sum = dp_sum(qk_sum)
+    v_sum = dp_sum(v_sum)
+
+    output = (middle + ring_sum(parts, back_sum)).astype(LOW)
 
     def wide(x):
         return x.astype(WIDE)
@@ -717,10 +767,10 @@
     return (
         output[None],
         grad_tokens[None],
-        wide(qkv_sum[:, 3 * width]),
-        wide(qkv_sum[:, :width]),
-        wide(qkv_sum[:, width : 2 * width]),
-        wide(qkv_sum[:, 2 * width : 3 * width]),
+        wide(v_sum[:, width]),
+        wide(qk_sum[:, :width]),
+        wide(qk_sum[:, width:]),
+        wide(v_sum[:, :width]),
         wide(out_sum[:, :width]),
         wide(out_sum[:, width + routed]),
         wide(shared_sum[:, :ff]),

time: 657 us -> 670 us (1.020)
  local copies, waits for them, and re-layouts: 27.7 us -> 73.5 us
  blocking collectives: 36.4 us -> 0 us
  waiting for transfers between devices: 239 us -> 264 us
  Pallas kernels: 185 us -> 163 us
    all_gather x1 -> x0, blocking collectives: 36.4 us -> none  [per_device(): lax.all_gather(small, 'expert', axis=0, tiled=True).reshape(group, -1)]
    ppermute x27 -> x32, waiting for transfers between devices: 152 us -> 124 us  [exchange(): return lax.ppermute(x, 'dp', [(i, i ^ bit) for i in range(count)])]
    all_gather x1, waiting for transfers between devices: 0.01 us -> 26.7 us  [per_device(): far_part = lax.all_gather(far_part, 'expert', axis=0, tiled=True)]
    ppermute x12, waiting for transfers between devices: 83.5 us -> 110 us  [around(): lax.ppermute(x, 'expert', [(i, (i + 2) % count) for i in range(count)])]
    unnamed x102 -> x121, local copies, waits for them, and re-layouts: 5.01 us -> 25.1 us
    pallas_call x4, Pallas kernels: 67.5 us -> 54.3 us  [per_device(): pl.pallas_call(functools.partial(experts_kernel, routed), grid=(local,),...]
    squeeze x8, local copies, waits for them, and re-layouts: 2.11 us -> 14 us  [scatter_leg(): sent = lax.dynamic_index_in_dim(x, 1 - mine, at, keepdims=False)]
    concatenate x3 -> x4, other arithmetic: 12.7 us -> 2.83 us  [the longest x1 1.14 us: per_device(): jnp.concatenate([out_weight, value_weight, key_weight[:, near:]], axis=1)]
  transfers between devices with their start and end apart: 65 -> 72, of which waited for: 26 -> 32; matrix products, arithmetic and copies ran while one was open for 16% -> 16% of each run, Pallas kernels for 25% -> 17%
where the time goes in v3:
time: 670 us; the launch traced here: 657 us
  waiting for transfers between devices  264 us (39%)
  Pallas kernels  163 us (24%)
  local copies, waits for them, and re-layouts  73.5 us (11%)
  starting transfers between devices  54.4 us (8%)
  other arithmetic  44.5 us (7%)
  matrix products  42.2 us (6%)
  between operations  15.7 us (2%)
    ppermute x32, waiting for transfers between devices, exchange(): return lax.ppermute(x, 'dp', [(i, i ^ bit) for i in range(count)])  124 us
    ppermute x12, waiting for transfers between devices, around(): lax.ppermute(x, 'expert', [(i, (i + 2) % count) for i in range(count)])  110 us
    pallas_call x4, Pallas kernels, per_device(): pl.pallas_call(functools.partial(experts_back_kernel, slot_count), grid=(...  60.6 us
    pallas_call x4, Pallas kernels, per_device(): pl.pallas_call(functools.partial(experts_kernel, routed), grid=(local,),...  54.3 us
    dot_general x6, matrix products, dot(): return lax.dot_general(a, b, (dims, ((), ())), preferred_element_type=WIDE)  42 us
    ppermute x32, starting transfers between devices, exchange(): return lax.ppermute(x, 'dp', [(i, i ^ bit) for i in range(count)])  33.7 us
    all_gather x1, waiting for transfers between devices, per_device(): far_part = lax.all_gather(far_part, 'expert', axis=0, tiled=True)  26.7 us
    unnamed x121, local copies, waits for them, and re-layouts  25.1 us
  transfers between devices with their start and end apart: 72, of which 32 were waited for; matrix products, arithmetic and copies ran while one was open for 16% of the time, Pallas kernels for 17%

profile of v3, /device:TPU:0, one launch (start us, length us, event | category | flops | bytes accessed | tf_op | source)
XLA Modules:
  0.0 657.1 jit_solution(1598930138223801375)
XLA Ops:
  22.8 26.7 %all-gather.3.cloned.1.call-done = bf16[1280,1024]{1,0:T(8,128)(2,1)} async-done(((bf16[160,1024]{1,0:T(8,128)(2,1)}), bf16[1280,1024]{1,0:T(8,128)(2,1)}) %all-gather.3.cloned.1.call-update) | async-done | bytes 2621456 | tf_op jit(solution)/shard_map/all_gather | solution.py:485
  62.1 16.7 %collective-permute-done.1.refs_2_ = bf16[640,896]{1,0:T(8,128)(2,1)S(1)} collective-permute-done((bf16[640,896]{1,0:T(8,128)(2,1)S(1)}, bf16[640,896]{1,0:T(8,128)(2,1)S(1)}, u32[]{:S(2)}, u32[]{:S(2)}) %collective-permute-start.1) | collective-permute-done | bytes 1146912 | tf_op jit(solution)/shard_map/ppermute | solution.py:390
  108.8 10.1 %attend.1 = (bf16[256,3840]{1,0:T(8,128)(2,1)S(1)}, bf16[256,1280]{1,0:T(8,128)(2,1)S(1)}) custom-call(s32[1]{0:T(128)S(6)} %copy.144.length_ref, bf16[256,1280]{1,0:T(8,128)(2,1)S(1)} %bitcast.113, f32[1,1280]{1,0:T(1,128)S(1)} %reshape.248.gain_ref, f32[256,128]{1,0:T(8,128)S(1)} %copy.110.cos_ref, f32[256,128]{1,0:T(8,128)S(1)} %pad_maximum_fusion.6.sin_ref, ...), custom_call_target="tpu_custom_call" | custom-call | flops 3271557120 | bytes 9830400 | tf_op jit(solution)/shard_map/attend/pallas_call | solution.py:585
  132.9 11.4 %collective-permute-done.11.s0_ref = bf16[256,1280]{1,0:T(8,128)(2,1)} collective-permute-done((bf16[256,1280]{1,0:T(8,128)(2,1)S(1)}, bf16[256,1280]{1,0:T(8,128)(2,1)}, u32[]{:S(2)}, u32[]{:S(2)}) %collective-permute-start.11) | collective-permute-done | bytes 655392 | tf_op jit(solution)/shard_map/ppermute | solution.py:349
  144.8 24.0 %collective-permute-done.21.g0_ref = bf16[256,1280]{1,0:T(8,128)(2,1)S(1)} collective-permute-done((bf16[256,1280]{1,0:T(8,128)(2,1)S(1)}, bf16[256,1280]{1,0:T(8,128)(2,1)S(1)}, u32[]{:S(2)}, u32[]{:S(2)}) %collective-permute-start.21) | collective-permute-done | bytes 655392 | tf_op jit(solution)/shard_map/ppermute | solution.py:349
  168.9 13.6 %collective-permute-done.12.s0_ref = bf16[256,1280]{1,0:T(8,128)(2,1)} collective-permute-done((bf16[256,1280]{1,0:T(8,128)(2,1)}, bf16[256,1280]{1,0:T(8,128)(2,1)}, u32[]{:S(2)}, u32[]{:S(2)}) %collective-permute-start.12) | collective-permute-done | bytes 655392 | tf_op jit(solution)/shard_map/ppermute | solution.py:349
  192.5 13.5 %shard_map.280 = (bf16[2,4,336,1280]{3,2,1,0:T(8,128)(2,1)}, bf16[2,4,336,896]{3,2,1,0:T(8,128)(2,1)}, bf16[4,512,128]{2,1,0:T(8,128)(2,1)}, bf16[4,512,1280]{2,...) custom-call(s32[2]{0:T(128)} %copy-done.49, ...), custom_call_target="tpu_custom_call" | custom-call | flops 5549064192 | bytes 13762560 | tf_op jit(solution)/shard_map/pallas_call | solution.py:643
  206.1 13.6 %shard_map.281 = (bf16[2,4,336,1280]{3,2,1,0:T(8,128)(2,1)}, bf16[2,4,336,896]{3,2,1,0:T(8,128)(2,1)}, bf16[4,512,128]{2,1,0:T(8,128)(2,1)}, bf16[4,512,1280]{2,...) custom-call(s32[2]{0:T(128)} %copy-done.49, ...), custom_call_target="tpu_custom_call", output_to_operand_aliasing={{0}: (10, {}), {1}: (11, {}), {2}: (12, {}), {3}: (13, {})} | custom-call | flops 5549064192 | bytes 13762560 | tf_op jit(solution)/shard_map/pallas_call | solution.py:643
  221.4 15.1 %shard_map.284 = (bf16[2,4,336,1280]{3,2,1,0:T(8,128)(2,1)}, bf16[2,4,336,1792]{3,2,1,0:T(8,128)(2,1)}, bf16[4,512,256]{2,1,0:T(8,128)(2,1)}, bf16[4,512,1280]{2...) custom-call(s32[2]{0:T(128)} %copy-done.49, bf16[256,1280]{1,0:T(8,128)(2,1)} %copy-done.30, ...), custom_call_target="tpu_custom_call" | custom-call | flops 5549064192 | bytes 13762560 | tf_op jit(solution)/shard_map/pallas_call | solution.py:674
  239.8 13.6 %shard_map.282 = (bf16[2,4,336,1280]{3,2,1,0:T(8,128)(2,1)}, bf16[2,4,336,896]{3,2,1,0:T(8,128)(2,1)}, bf16[4,512,128]{2,1,0:T(8,128)(2,1)}, bf16[4,512,1280]{2,...) custom-call(s32[2]{0:T(128)} %copy-done.49, ...), custom_call_target="tpu_custom_call", output_to_operand_aliasing={{0}: (10, {}), {1}: (11, {}), {2}: (12, {}), {3}: (13, {})} | custom-call | flops 5549064192 | bytes 13762560 | tf_op jit(solution)/shard_map/pallas_call | solution.py:643
  258.7 15.1 %shard_map.285 = (bf16[2,4,336,1280]{3,2,1,0:T(8,128)(2,1)}, bf16[2,4,336,1792]{3,2,1,0:T(8,128)(2,1)}, bf16[4,512,256]{2,1,0:T(8,128)(2,1)}, bf16[4,512,1280]{2...) custom-call(s32[2]{0:T(128)} %copy-done.49, ...), custom_call_target="tpu_custom_call", output_to_operand_aliasing={{0}: (15, {}), {1}: (16, {}), {2}: (17, {}), {3}: (18, {})} | custom-call | flops 5549064192 | bytes 13762560 | tf_op jit(solution)/shard_map/pallas_call | solution.py:674
  275.2 13.6 %shard_map.283 = (bf16[2,4,336,1280]{3,2,1,0:T(8,128)(2,1)}, bf16[2,4,336,896]{3,2,1,0:T(8,128)(2,1)}, bf16[4,512,128]{2,1,0:T(8,128)(2,1)}, bf16[4,512,1280]{2,...) custom-call(s32[2]{0:T(128)} %copy-done.49, ...), custom_call_target="tpu_custom_call", output_to_operand_aliasing={{0}: (10, {}), {1}: (11, {}), {2}: (12, {}), {3}: (13, {})} | custom-call | flops 5549064192 | bytes 13762560 | tf_op jit(solution)/shard_map/pallas_call | solution.py:643
  289.6 15.3 %shard_map.286 = (bf16[2,4,336,1280]{3,2,1,0:T(8,128)(2,1)}, bf16[2,4,336,1792]{3,2,1,0:T(8,128)(2,1)}, bf16[4,512,256]{2,1,0:T(8,128)(2,1)}, bf16[4,512,1280]{2...) custom-call(s32[2]{0:T(128)} %copy-done.49, ...), custom_call_target="tpu_custom_call", output_to_operand_aliasing={{0}: (15, {}), {1}: (16, {}), {2}: (17, {}), {3}: (18, {})} | custom-call | flops 5549064192 | bytes 13762560 | tf_op jit(solution)/shard_map/pallas_call | solution.py:674
  306.2 15.1 %shard_map.287 = (bf16[2,4,336,1280]{3,2,1,0:T(8,128)(2,1)}, bf16[2,4,336,1792]{3,2,1,0:T(8,128)(2,1)}, bf16[4,512,256]{2,1,0:T(8,128)(2,1)}, bf16[4,512,1280]{2...) custom-call(s32[2]{0:T(128)} %copy-done.49, ...), custom_call_target="tpu_custom_call", output_to_operand_aliasing={{0}: (15, {}), {1}: (16, {}), {2}: (17, {}), {3}: (18, {})} | custom-call | flops 5549064192 | bytes 13762560 | tf_op jit(solution)/shard_map/pallas_call | solution.py:674
  326.0 19.4 %collective-permute-done.33 = bf16[256,1408]{1,0:T(8,128)(2,1)S(1)} collective-permute-done((bf16[256,1408]{1,0:T(8,128)(2,1)S(1)}, bf16[256,1408]{1,0:T(8,128)(2,1)S(1)}, u32[]{:S(2)}, u32[]{:S(2)}) %collective-permute-start.33) | collective-permute-done | bytes 720928 | tf_op jit(solution)/shard_map/ppermute | solution.py:349
  353.6 12.3 %convolution_convert_fusion.1 = bf16[1280,1792]{1,0:T(8,128)(2,1)} fusion(bf16[2,1344,1792]{2,1,0:T(8,128)(2,1)} %bitcast.115, bf16[2,1344,1280]{2,1,0:T(8,128)(2,1)} %bitcast.120), kind=kOutput, calls=%fused_computation.2 | convolution fusion | flops 6167920640 | bytes 12845056 | tf_op jit(solution)/shard_map/dot_general | solution.py:21
  365.9 10.5 %convolution_convert_fusion = bf16[1280,1792]{1,0:T(8,128)(2,1)} fusion(bf16[2,1344,1792]{2,1,0:T(8,128)(2,1)S(1)} %bitcast.118, bf16[2,1344,1280]{2,1,0:T(8,128)(2,1)} %bitcast.121), kind=kOutput, calls=%fused_computation.1 | convolution fusion | flops 6167920640 | bytes 12845056 | tf_op jit(solution)/shard_map/dot_general | solution.py:21
  376.4 20.9 %attend_back.1 = (f32[256,1280]{1,0:T(8,128)}, bf16[1280,2560]{1,0:T(8,128)(2,1)}, bf16[1280,1408]{1,0:T(8,128)(2,1)}) custom-call(s32[1]{0:T(128)S(6)} %copy.144.length_ref, bf16[256,1280]{1,0:T(8,128)(2,1)} %get-tuple-element.219.low_ref, f32[256,1280]{1,0:T(8,128)} %get-tuple-element.220.wide_ref, bf16[256,1280]{1,0:T(8,128)(2,1)} %bitcast.112, ...), custom_call_target="tpu_custom_call" | custom-call | flops 7549747200 | bytes 26214400 | tf_op jit(solution)/shard_map/attend_back/pallas_call | solution.py:717
  439.9 30.1 %collective-permute-done.57 = bf16[112,640]{1,0:T(8,128)(2,1)S(1)} collective-permute-done((bf16[112,640]{1,0:T(8,128)(2,1)S(1)}, bf16[112,640]{1,0:T(8,128)(2,1)S(1)}, u32[]{:S(2)}, u32[]{:S(2)}) %collective-permute-start.57) | collective-permute-done | bytes 143392 | tf_op jit(solution)/shard_map/ppermute | solution.py:390
  487.7 15.5 %collective-permute-done.34 = bf16[256,1280]{1,0:T(8,128)(2,1)S(1)} collective-permute-done((bf16[256,1280]{1,0:T(8,128)(2,1)S(1)}, bf16[256,1280]{1,0:T(8,128)(2,1)S(1)}, u32[]{:S(2)}, u32[]{:S(2)}) %collective-permute-start.34) | collective-permute-done | bytes 655392 | tf_op jit(solution)/shard_map/ppermute | solution.py:349
  515.7 13.7 %collective-permute-done.49 = bf16[2,224,1280]{2,1,0:T(8,128)(2,1)S(1)} collective-permute-done((bf16[2,224,1280]{2,1,0:T(8,128)(2,1)S(1)}, bf16[2,224,1280]{2,1,0:T(8,128)(2,1)S(1)}, u32[]{:S(2)}, u32[]{:S(2)}) %collective-permute-start.49) | collective-permute-done | bytes 1146912 | tf_op jit(solution)/shard_map/ppermute | solution.py:390
  556.6 16.6 %collective-permute-done.36 = bf16[256,1280]{1,0:T(8,128)(2,1)} collective-permute-done((bf16[256,1280]{1,0:T(8,128)(2,1)}, bf16[256,1280]{1,0:T(8,128)(2,1)}, u32[]{:S(2)}, u32[]{:S(2)}) %collective-permute-start.36) | collective-permute-done | bytes 655392 | tf_op jit(solution)/shard_map/ppermute | solution.py:349
  578.6 14.3 %collective-permute-done.56 = bf16[160,896]{1,0:T(8,128)(2,1)S(1)} collective-permute-done((bf16[160,896]{1,0:T(8,128)(2,1)S(1)}, bf16[160,896]{1,0:T(8,128)(2,1)S(1)}, u32[]{:S(2)}, u32[]{:S(2)}) %collective-permute-start.56) | collective-permute-done | bytes 286752 | tf_op jit(solution)/shard_map/ppermute | solution.py:390
  629.4 7.2 %collective-permute-done.41 = bf16[160,1280]{1,0:T(8,128)(2,1)S(1)} collective-permute-done((bf16[160,1280]{1,0:T(8,128)(2,1)S(1)}, bf16[160,1280]{1,0:T(8,128)(2,1)S(1)}, u32[]{:S(2)}, u32[]{:S(2)}) %collective-permute-start.41) | collective-permute-done | bytes 409632 | tf_op jit(solution)/shard_map/ppermute | solution.py:390
  (386 shorter events, 263.5 us)
Async XLA Ops:
  7.2 42.3 %all-gather.3.cloned.1.call-start = ((), (), s32[]{:S(2)}) async-start(), calls=%async_computation.5 | async-start | bytes 2949120 | tf_op jit(solution)/shard_map/all_gather | solution.py:485
  13.9 88.2 %all-gather.5.cloned.1.call-start = ((), (), s32[]{:S(2)}) async-start(), calls=%async_computation.6 | async-start | bytes 4423680 | tf_op jit(solution)/shard_map/all_gather | solution.py:496
  60.7 41.4 %collective-permute-start = (bf16[640,896]{1,0:T(8,128)(2,1)S(1)}, bf16[640,896]{1,0:T(8,128)(2,1)}, u32[]{:S(2)}, u32[]{:S(2)}) collective-permute-start(bf16[640,896]{1,0:T(8,128)(2,1)S(1)} %constant_dynamic-slice_fusion.refs_0_), channel_id=1, source_target_pairs={{0,1},{1,0},{2,3},{3,2},{4,5},{5,4},{6,7},{7,6},{8,9},{9,8},{10,11... | collective-permute-start | bytes 3440648 | tf_op jit(solution)/shard_map/ppermute | solution.py:354
  126.8 58.9 %all-to-all-start = ((bf16[8,160,256]{2,1,0:T(8,128)(2,1)}), bf16[8,160,256]{2,1,0:T(8,128)(2,1)S(1)}, u32[]{:S(2)}, u32[]{:S(2)}) async-start(bf16[8,160,256]{2,1,0:T(8,128)(2,1)} %fusion.20), calls=%async_computation | async-start | bytes 1310720 | tf_op jit(solution)/shard_map/all_to_all | solution.py:540
  130.8 466.8 %reduce-scatter.4.cloned.1.call-start = ((), (), s32[]{:S(2)}) async-start(), calls=%async_computation.7 | async-start | bytes 4055040 | tf_op jit(solution)/shard_map/reduce_scatter | solution.py:734
  130.9 38.0 %collective-permute-start.21 = (bf16[256,1280]{1,0:T(8,128)(2,1)S(1)}, bf16[256,1280]{1,0:T(8,128)(2,1)S(1)}, u32[]{:S(2)}, u32[]{:S(2)}) collective-permute-start(bf16[256,1280]{1,0:T(8,128)(2,1)S(1)} %bitcast.148), channel_id=1, source_target_pairs={{0,2},{1,3},{2,4},{3,5},{4,6},{5,7},{6,0},{7,1},{8,10},{9,11},{10,... | collective-permute-start | bytes 1966088 | tf_op jit(solution)/shard_map/ppermute | solution.py:349
  144.3 38.2 %collective-permute-start.12 = (bf16[256,1280]{1,0:T(8,128)(2,1)}, bf16[256,1280]{1,0:T(8,128)(2,1)}, u32[]{:S(2)}, u32[]{:S(2)}) collective-permute-start(bf16[256,1280]{1,0:T(8,128)(2,1)} %collective-permute-done.11.s0_ref), channel_id=1, source_target_pairs={{0,2},{1,3},{2,4},{3,5},{4,6},{5,7},{6,0},{7,1},{8,10},{9,11},{10,... | collective-permute-start | bytes 1966088 | tf_op jit(solution)/shard_map/ppermute | solution.py:349
  144.3 41.4 %collective-permute-start.9 = (bf16[256,1280]{1,0:T(8,128)(2,1)S(1)}, bf16[256,1280]{1,0:T(8,128)(2,1)}, u32[]{:S(2)}, u32[]{:S(2)}) collective-permute-start(bf16[256,1280]{1,0:T(8,128)(2,1)S(1)} %get-tuple-element.140.s0_ref.second_ref), channel_id=1, source_target_pairs={{0,1},{1,0},{2,3},{3,2},{4,5},{5,4},{6,7},{7,6},{8,9},{9,8},{10,11... | collective-permute-start | bytes 1966088 | tf_op jit(solution)/shard_map/ppermute | solution.py:354
  144.3 61.8 %collective-permute-start.16 = (bf16[256,1280]{1,0:T(8,128)(2,1)}, bf16[256,1280]{1,0:T(8,128)(2,1)}, u32[]{:S(2)}, u32[]{:S(2)}) collective-permute-start(bf16[256,1280]{1,0:T(8,128)(2,1)} %collective-permute-done.11.s0_ref), channel_id=1, source_target_pairs={{0,1},{1,0},{2,3},{3,2},{4,5},{5,4},{6,7},{7,6},{8,9},{9,8},{10,11... | collective-permute-start | bytes 1966088 | tf_op jit(solution)/shard_map/ppermute | solution.py:354
  168.9 51.7 %collective-permute-start.26 = (bf16[256,1280]{1,0:T(8,128)(2,1)S(1)}, bf16[256,1280]{1,0:T(8,128)(2,1)S(1)}, u32[]{:S(2)}, u32[]{:S(2)}) collective-permute-start(bf16[256,1280]{1,0:T(8,128)(2,1)S(1)} %collective-permute-done.21.g0_ref), channel_id=1, source_target_pairs={{0,1},{1,0},{2,3},{3,2},{4,5},{5,4},{6,7},{7,6},{8,9},{9,8},{10,11... | collective-permute-start | bytes 1966088 | tf_op jit(solution)/shard_map/ppermute | solution.py:354
  236.7 68.6 %collective-permute-start.20 = (bf16[256,1280]{1,0:T(8,128)(2,1)S(1)}, bf16[256,1280]{1,0:T(8,128)(2,1)S(1)}, u32[]{:S(2)}, u32[]{:S(2)}) collective-permute-start(bf16[256,1280]{1,0:T(8,128)(2,1)S(1)} %bitcast.149), channel_id=1, source_target_pairs={{0,1},{1,0},{2,3},{3,2},{4,5},{5,4},{6,7},{7,6},{8,9},{9,8},{10,11... | collective-permute-start | bytes 1966088 | tf_op jit(solution)/shard_map/ppermute | solution.py:354
  253.6 51.4 %collective-permute-start.31 = (bf16[256,1408]{1,0:T(8,128)(2,1)S(1)}, bf16[256,1408]{1,0:T(8,128)(2,1)S(1)}, u32[]{:S(2)}, u32[]{:S(2)}) collective-permute-start(bf16[256,1408]{1,0:T(8,128)(2,1)S(1)} %add_convert_fusion.6), channel_id=1, source_target_pairs={{0,2},{1,3},{2,4},{3,5},{4,6},{5,7},{6,0},{7,1},{8,10},{9,11},{10,... | collective-permute-start | bytes 2162696 | tf_op jit(solution)/shard_map/ppermute | solution.py:349
  397.3 207.7 %reduce-scatter.8.cloned.1.call-start = ((), (), s32[]{:S(2)}) async-start(), calls=%async_computation.9 | async-start | bytes 4055040 | tf_op jit(solution)/shard_map/reduce_scatter | solution.py:732
  398.0 89.2 %collective-permute-start.18 = (bf16[256,1280]{1,0:T(8,128)(2,1)}, bf16[256,1280]{1,0:T(8,128)(2,1)}, u32[]{:S(2)}, u32[]{:S(2)}) collective-permute-start(bf16[256,1280]{1,0:T(8,128)(2,1)} %get-tuple-element.164), channel_id=1, source_target_pairs={{0,1},{1,0},{2,3},{3,2},{4,5},{5,4},{6,7},{7,6},{8,9},{9,8},{10,11... | collective-permute-start | bytes 1966088 | tf_op jit(solution)/shard_map/ppermute | solution.py:354
  406.2 129.1 %all-to-all-start.1 = ((bf16[8,160,256]{2,1,0:T(8,128)(2,1)}), bf16[8,160,256]{2,1,0:T(8,128)(2,1)}, u32[]{:S(2)}, u32[]{:S(2)}) async-start(bf16[8,160,256]{2,1,0:T(8,128)(2,1)} %bitcast.33), calls=%async_computation.4 | async-start | bytes 1310720 | tf_op jit(solution)/shard_map/all_to_all | solution.py:741
  410.4 214.8 %reduce-scatter.6.cloned.1.call-start = ((), (), s32[]{:S(2)}) async-start(), calls=%async_computation.8 | async-start | bytes 7372800 | tf_op jit(solution)/shard_map/reduce_scatter | solution.py:733
  414.7 92.2 %collective-permute-start.51 = (bf16[2,320,1792]{2,1,0:T(8,128)(2,1)}, bf16[2,320,1792]{2,1,0:T(8,128)(2,1)}, u32[]{:S(2)}, u32[]{:S(2)}) collective-permute-start(bf16[2,320,1792]{2,1,0:T(8,128)(2,1)} %get-tuple-element.336), channel_id=1, source_target_pairs={{0,8},{8,0},{16,24},{24,16},{1,9},{9,1},{17,25},{25,17},{2,10},{10... | collective-permute-start | bytes 6881288 | tf_op jit(solution)/shard_map/ppermute | solution.py:390
  421.0 86.6 %collective-permute-start.52 = (bf16[2,320,1792]{2,1,0:T(8,128)(2,1)}, bf16[2,320,1792]{2,1,0:T(8,128)(2,1)}, u32[]{:S(2)}, u32[]{:S(2)}) collective-permute-start(bf16[2,320,1792]{2,1,0:T(8,128)(2,1)} %get-tuple-element.334), channel_id=1, source_target_pairs={{0,16},{8,24},{16,0},{24,8},{1,17},{9,25},{17,1},{25,9},{2,18},{10... | collective-permute-start | bytes 6881288 | tf_op jit(solution)/shard_map/ppermute | solution.py:390
  438.5 37.7 %collective-permute-start.59 = (bf16[112,640]{1,0:T(8,128)(2,1)S(1)}, bf16[112,640]{1,0:T(8,128)(2,1)S(1)}, u32[]{:S(2)}, u32[]{:S(2)}) collective-permute-start(bf16[112,640]{1,0:T(8,128)(2,1)S(1)} %get-tuple-element.359), channel_id=1, source_target_pairs={{0,16},{8,24},{16,0},{24,8},{1,17},{9,25},{17,1},{25,9},{2,18},{10... | collective-permute-start | bytes 430088 | tf_op jit(solution)/shard_map/ppermute | solution.py:390
  486.5 69.3 %collective-permute-start.10 = (bf16[256,1280]{1,0:T(8,128)(2,1)}, bf16[256,1280]{1,0:T(8,128)(2,1)}, u32[]{:S(2)}, u32[]{:S(2)}) collective-permute-start(bf16[256,1280]{1,0:T(8,128)(2,1)} %get-tuple-element.148), channel_id=1, source_target_pairs={{0,1},{1,0},{2,3},{3,2},{4,5},{5,4},{6,7},{7,6},{8,9},{9,8},{10,11... | collective-permute-start | bytes 1966088 | tf_op jit(solution)/shard_map/ppermute | solution.py:354
  487.2 50.8 %collective-permute-start.17 = (bf16[256,1280]{1,0:T(8,128)(2,1)}, bf16[256,1280]{1,0:T(8,128)(2,1)}, u32[]{:S(2)}, u32[]{:S(2)}) collective-permute-start(bf16[256,1280]{1,0:T(8,128)(2,1)} %get-tuple-element.162), channel_id=1, source_target_pairs={{0,1},{1,0},{2,3},{3,2},{4,5},{5,4},{6,7},{7,6},{8,9},{9,8},{10,11... | collective-permute-start | bytes 1966088 | tf_op jit(solution)/shard_map/ppermute | solution.py:354
  548.3 45.4 %collective-permute-start.61 = (bf16[320,1792]{1,0:T(8,128)(2,1)}, bf16[320,1792]{1,0:T(8,128)(2,1)S(1)}, u32[]{:S(2)}, u32[]{:S(2)}) collective-permute-start(bf16[320,1792]{1,0:T(8,128)(2,1)} %get-tuple-element.340), channel_id=1, source_target_pairs={{0,16},{8,24},{16,0},{24,8},{1,17},{9,25},{17,1},{25,9},{2,18},{10... | collective-permute-start | bytes 3440648 | tf_op jit(solution)/shard_map/ppermute | solution.py:390
  553.2 40.5 %collective-permute-start.62 = (bf16[320,1792]{1,0:T(8,128)(2,1)}, bf16[320,1792]{1,0:T(8,128)(2,1)S(1)}, u32[]{:S(2)}, u32[]{:S(2)}) collective-permute-start(bf16[320,1792]{1,0:T(8,128)(2,1)} %get-tuple-element.338), channel_id=1, source_target_pairs={{0,8},{8,0},{16,24},{24,16},{1,9},{9,1},{17,25},{25,17},{2,10},{10... | collective-permute-start | bytes 3440648 | tf_op jit(solution)/shard_map/ppermute | solution.py:390
  555.8 37.9 %collective-permute-start.63 = (bf16[224,1280]{1,0:T(8,128)(2,1)S(1)}, bf16[224,1280]{1,0:T(8,128)(2,1)S(1)}, u32[]{:S(2)}, u32[]{:S(2)}) collective-permute-start(bf16[224,1280]{1,0:T(8,128)(2,1)S(1)} %copy-done.44), channel_id=1, source_target_pairs={{0,16},{8,24},{16,0},{24,8},{1,17},{9,25},{17,1},{25,9},{2,18},{10... | collective-permute-start | bytes 1720328 | tf_op jit(solution)/shard_map/ppermute | solution.py:390
  (109 other events, 1669.0 us)
Sparse Core Ops, SparseCore 0:
  14.0 35.4 all-gather.2
  51.8 43.8 all-gather.4
  397.4 52.1 reduce-scatter.3
  451.8 61.1 reduce-scatter.7
  515.1 87.3 reduce-scatter.5

commit v4 on v3

--- a/solution.py
+++ b/solution.py
@@ -398,13 +398,15 @@
     return bits
 
 
-def dp_sum(x):
+def dp_sum(x, needed=None):
     bits = dp_bits()
     cut = x.shape[1] // 2 // LANES * LANES
     parts = []
     for piece, order in ((x[:, :cut], bits), (x[:, cut:], bits[::-1])):
         for bit in order:
             got = exchange(piece, bit)
+            if needed is not None:
+                got = chained(got, needed)
             piece = (piece.astype(WIDE) + got.astype(WIDE)).astype(LOW)
         parts.append(piece)
     return jnp.concatenate(parts, axis=1)
@@ -421,6 +423,34 @@
     kept = lax.dynamic_index_in_dim(x, mine, at, keepdims=False)
     sent = lax.dynamic_index_in_dim(x, 1 - mine, at, keepdims=False)
     return kept, exchange(sent, bit)
+
+
+def dp_scatter(x, axis, order):
+    me = lax.axis_index("dp")
+    left = list(reversed(dp_bits()))
+    x = x.reshape(*x.shape[:axis], *(2 for _ in left), x.shape[axis] // lax.axis_size("dp"), *x.shape[axis + 1 :])
+    for bit in order:
+        at = axis + left.index(bit)
+        mine = (me // bit) % 2
+        kept = lax.dynamic_index_in_dim(x, mine, at, keepdims=False)
+        sent = lax.dynamic_index_in_dim(x, 1 - mine, at, keepdims=False)
+        x = add(kept, exchange(sent, bit)).astype(LOW)
+        left.remove(bit)
+    return x
+
+
+def dp_gather(x):
+    dp, count = lax.axis_index("dp"), lax.axis_size("dp")
+    blocks = [x]
+    for bit in dp_bits():
+        blocks += [exchange(b, bit) for b in blocks]
+    ordered = []
+    for n in range(count):
+        block = blocks[0]
+        for m in range(1, count):
+            block = jnp.where((dp ^ n) == m, blocks[m], block)
+        ordered.append(block)
+    return jnp.concatenate(ordered, axis=0)
 
 
 def chained(xs, needed):
@@ -568,6 +598,9 @@
     def columns(n):
         return pl.BlockSpec((seq, n), lambda h: (0, h))
 
+    def held(x):
+        return pltpu.with_memory_space_constraint(x, pltpu.VMEM)
+
     def stored(*xs):
         return [pltpu.with_memory_space_constraint(x, pltpu.HBM) for x in xs]
 
@@ -630,16 +663,14 @@
         return [pl.BlockSpec((1, 2, 1, seq), lambda e: (e, k, 0, 0)),
                 pl.BlockSpec((tok, LANES), lambda e: (k, 0))]
 
-    def held(x):
-        return pltpu.with_memory_space_constraint(x, pltpu.VMEM)
-
     weights = (held(w_gu), held(expert_down), shared_cols, shared_rows)
     kept, parts = [], []
     store = ()
     blocks = ring_gather(second)
     for k in range(chips):
         store_in = [anywhere] * len(store)
-        fixed = (my_slots, *blocks[k], *stored(place_row, place_col), router, *weights)
+        own = weights if k else (*stored(w_gu, expert_down), *weights[2:])
+        fixed = (my_slots, *blocks[k], *stored(place_row, place_col), router, *own)
         out = pl.pallas_call(
             functools.partial(experts_kernel, routed),
             grid=(local,),
@@ -738,21 +769,23 @@
     down = [scatter_leg(down[n], orders[n], 0) for n in range(local)]
     g_cols = dot_rows(second_all, g_s).astype(LOW)
     grad_sdown = dot_rows(s_hidden, up_all).astype(LOW)[:ff_part]
-    g_all = lax.all_to_all(
-        g_cols.reshape(group, rows_w, 2 * fp), "expert", split_axis=0, concat_axis=0, tiled=True
-    )
+    parts_of_rows = [
+        dp_scatter(g_cols[:, at : at + fp].reshape(group, rows_w, fp), 1, order)
+        for at, order in ((0, bits), (fp, bits[::-1]))
+    ]
+    g_all = lax.all_to_all(jnp.concatenate(parts_of_rows, axis=2), "expert", split_axis=0, concat_axis=0, tiled=True)
 
     gu = chained(gu, ([x[0] for x in down], g_cols))
     gu = [scatter_leg(add(*x).astype(LOW), orders[n], 1) for n, x in enumerate(gu)]
     down = chained(down, [x[0] for x in gu])
     down = [scatter_leg(add(*x).astype(LOW), orders[n], 1) for n, x in enumerate(down)]
-    g_cols = chained(g_all, [x[0] for x in down]).transpose(1, 0, 2)
-    grad_sgate = trim(g_cols[:, :, :fp]).reshape(rows_w, ff)
-    grad_sup = trim(g_cols[:, :, fp:]).reshape(rows_w, ff)
-    shared_cut = jnp.concatenate([grad_sgate, grad_sup], axis=1)
-    gu, down = chained((gu, down), ([x[0] for x in down], shared_cut))
-    shared_sum = dp_sum(shared_cut)
-    sdown_sum = dp_sum(grad_sdown)
+    g_all = g_all.transpose(1, 0, 2)
+    shared_cut = jnp.concatenate(
+        [trim(g_all[:, :, at : at + fp]).reshape(rows_w // count, ff) for at in (0, fp)], axis=1
+    )
+    gu, down = chained((gu, down), ([x[0] for x in down], qk_sum))
+    shared_sum = dp_gather(shared_cut)
+    sdown_sum = dp_sum(grad_sdown, qk_sum)
     wide_gu = jnp.stack([add(*x) for x in gu])
     wide_down = jnp.stack([add(*x) for x in down])
     out_sum = dp_sum(out_sum)

time: 670 us -> 739 us (1.10)
  waiting for transfers between devices: 264 us -> 330 us
  Pallas kernels: 163 us -> 176 us
  local copies, waits for them, and re-layouts: 73.5 us -> 61.8 us
  starting transfers between devices: 54.4 us -> 63 us
    ppermute x32 -> x35, waiting for transfers between devices: 124 us -> 172 us  [exchange(): return lax.ppermute(x, 'dp', [(i, i ^ bit) for i in range(count)])]
    ppermute x12, waiting for transfers between devices: 110 us -> 124 us  [around(): lax.ppermute(x, 'expert', [(i, (i + 2) % count) for i in range(count)])]
    unnamed x121 -> x132, local copies, waits for them, and re-layouts: 25.1 us -> 14.7 us
    ppermute x32 -> x35, starting transfers between devices: 33.7 us -> 42 us  [exchange(): return lax.ppermute(x, 'dp', [(i, i ^ bit) for i in range(count)])]
  transfers between devices with their start and end apart: 72 -> 75, of which waited for: 32 -> 33; matrix products, arithmetic and copies ran while one was open for 16% -> 14% of each run, Pallas kernels for 17% -> 18%
where the time goes in v4:
time: 739 us; the launch traced here: 730 us
  waiting for transfers between devices  330 us (45%)
  Pallas kernels  176 us (24%)
  starting transfers between devices  63 us (9%)
  local copies, waits for them, and re-layouts  61.8 us (8%)
  other arithmetic  43.9 us (6%)
  matrix products  39 us (5%)
  between operations  16 us (2%)
    ppermute x35, waiting for transfers between devices, exchange(): return lax.ppermute(x, 'dp', [(i, i ^ bit) for i in range(count)])  172 us
    ppermute x12, waiting for transfers between devices, around(): lax.ppermute(x, 'expert', [(i, (i + 2) % count) for i in range(count)])  124 us
    pallas_call x4, Pallas kernels, per_device(): pl.pallas_call(functools.partial(experts_back_kernel, slot_count), grid=(...  66.8 us
    pallas_call x4, Pallas kernels, per_device(): pl.pallas_call(functools.partial(experts_kernel, routed), grid=(local,),...  61.3 us
    ppermute x35, starting transfers between devices, exchange(): return lax.ppermute(x, 'dp', [(i, i ^ bit) for i in range(count)])  42 us
    dot_general x6, matrix products, dot(): return lax.dot_general(a, b, (dims, ((), ())), preferred_element_type=WIDE)  38.8 us
    all_gather x1, waiting for transfers between devices, per_device(): far_part = lax.all_gather(far_part, 'expert', axis=0, tiled=True)  27.2 us
    pallas_call x1, Pallas kernels, per_device(): pl.pallas_call(functools.partial(attend_back_kernel, pair, turn_over), gr...  20.8 us
  transfers between devices with their start and end apart: 75, of which 33 were waited for; matrix products, arithmetic and copies ran while one was open for 14% of the time, Pallas kernels for 18%

profile of v4, /device:TPU:0, one launch (start us, length us, event | category | flops | bytes accessed | tf_op | source)
XLA Modules:
  0.0 729.9 jit_solution(1813992704325286278)
XLA Ops:
  22.4 27.2 %all-gather.3.cloned.1.call-done = bf16[1280,1024]{1,0:T(8,128)(2,1)} async-done(((bf16[160,1024]{1,0:T(8,128)(2,1)}), bf16[1280,1024]{1,0:T(8,128)(2,1)}) %all-gather.3.cloned.1.call-update) | async-done | bytes 2621456 | tf_op jit(solution)/shard_map/all_gather | solution.py:515
  58.8 20.1 %collective-permute-done.1.refs_2_ = bf16[640,896]{1,0:T(8,128)(2,1)} collective-permute-done((bf16[640,896]{1,0:T(8,128)(2,1)S(1)}, bf16[640,896]{1,0:T(8,128)(2,1)}, u32[]{:S(2)}, u32[]{:S(2)}) %collective-permute-start.1) | collective-permute-done | bytes 1146912 | tf_op jit(solution)/shard_map/ppermute | solution.py:390
  133.6 11.5 %collective-permute-done.11.s0_ref = bf16[256,1280]{1,0:T(8,128)(2,1)} collective-permute-done((bf16[256,1280]{1,0:T(8,128)(2,1)S(1)}, bf16[256,1280]{1,0:T(8,128)(2,1)}, u32[]{:S(2)}, u32[]{:S(2)}) %collective-permute-start.11) | collective-permute-done | bytes 655392 | tf_op jit(solution)/shard_map/ppermute | solution.py:349
  145.6 24.1 %collective-permute-done.21.g0_ref = bf16[256,1280]{1,0:T(8,128)(2,1)} collective-permute-done((bf16[256,1280]{1,0:T(8,128)(2,1)}, bf16[256,1280]{1,0:T(8,128)(2,1)}, u32[]{:S(2)}, u32[]{:S(2)}) %collective-permute-start.21) | collective-permute-done | bytes 655392 | tf_op jit(solution)/shard_map/ppermute | solution.py:349
  169.7 13.6 %collective-permute-done.12.s0_ref = bf16[256,1280]{1,0:T(8,128)(2,1)} collective-permute-done((bf16[256,1280]{1,0:T(8,128)(2,1)}, bf16[256,1280]{1,0:T(8,128)(2,1)}, u32[]{:S(2)}, u32[]{:S(2)}) %collective-permute-start.12) | collective-permute-done | bytes 655392 | tf_op jit(solution)/shard_map/ppermute | solution.py:349
  186.6 16.6 %shard_map.280 = (bf16[2,4,336,1280]{3,2,1,0:T(8,128)(2,1)}, bf16[2,4,336,896]{3,2,1,0:T(8,128)(2,1)}, bf16[4,512,128]{2,1,0:T(8,128)(2,1)}, bf16[4,512,1280]{2,...) custom-call(s32[2]{0:T(128)S(1)} %iota_add_fusion.slots_ref, ...), custom_call_target="tpu_custom_call" | custom-call | flops 5549064192 | bytes 13762560 | tf_op jit(solution)/shard_map/pallas_call | solution.py:674
  203.3 14.9 %shard_map.281 = (bf16[2,4,336,1280]{3,2,1,0:T(8,128)(2,1)}, bf16[2,4,336,896]{3,2,1,0:T(8,128)(2,1)}, bf16[4,512,128]{2,1,0:T(8,128)(2,1)}, bf16[4,512,1280]{2,...) custom-call(s32[2]{0:T(128)} %copy-done.13, ...), custom_call_target="tpu_custom_call", output_to_operand_aliasing={{0}: (10, {}), {1}: (11, {}), {2}: (12, {}), {3}: (13, {})} | custom-call | flops 5549064192 | bytes 13762560 | tf_op jit(solution)/shard_map/pallas_call | solution.py:674
  219.1 16.7 %shard_map.284 = (bf16[2,4,336,1280]{3,2,1,0:T(8,128)(2,1)}, bf16[2,4,336,1792]{3,2,1,0:T(8,128)(2,1)}, bf16[4,512,256]{2,1,0:T(8,128)(2,1)}, bf16[4,512,1280]{2...) custom-call(s32[2]{0:T(128)} %copy-done.13, bf16[256,1280]{1,0:T(8,128)(2,1)} %collective-permute-done.21.g0_ref, ...), custom_call_target="tpu_custom_call" | custom-call | flops 5549064192 | bytes 13762560 | tf_op jit(solution)/shard_map/pallas_call | solution.py:705
  238.6 15.0 %shard_map.282 = (bf16[2,4,336,1280]{3,2,1,0:T(8,128)(2,1)}, bf16[2,4,336,896]{3,2,1,0:T(8,128)(2,1)}, bf16[4,512,128]{2,1,0:T(8,128)(2,1)}, bf16[4,512,1280]{2,...) custom-call(s32[2]{0:T(128)} %copy-done.13, ...), custom_call_target="tpu_custom_call", output_to_operand_aliasing={{0}: (10, {}), {1}: (11, {}), {2}: (12, {}), {3}: (13, {})} | custom-call | flops 5549064192 | bytes 13762560 | tf_op jit(solution)/shard_map/pallas_call | solution.py:674
  257.5 16.7 %shard_map.285 = (bf16[2,4,336,1280]{3,2,1,0:T(8,128)(2,1)}, bf16[2,4,336,1792]{3,2,1,0:T(8,128)(2,1)}, bf16[4,512,256]{2,1,0:T(8,128)(2,1)}, bf16[4,512,1280]{2...) custom-call(s32[2]{0:T(128)} %copy-done.13, ...), custom_call_target="tpu_custom_call", output_to_operand_aliasing={{0}: (15, {}), {1}: (16, {}), {2}: (17, {}), {3}: (18, {})} | custom-call | flops 5549064192 | bytes 13762560 | tf_op jit(solution)/shard_map/pallas_call | solution.py:705
  275.6 14.9 %shard_map.283 = (bf16[2,4,336,1280]{3,2,1,0:T(8,128)(2,1)}, bf16[2,4,336,896]{3,2,1,0:T(8,128)(2,1)}, bf16[4,512,128]{2,1,0:T(8,128)(2,1)}, bf16[4,512,1280]{2,...) custom-call(s32[2]{0:T(128)} %copy-done.13, ...), custom_call_target="tpu_custom_call", output_to_operand_aliasing={{0}: (10, {}), {1}: (11, {}), {2}: (12, {}), {3}: (13, {})} | custom-call | flops 5549064192 | bytes 13762560 | tf_op jit(solution)/shard_map/pallas_call | solution.py:674
  291.4 16.8 %shard_map.286 = (bf16[2,4,336,1280]{3,2,1,0:T(8,128)(2,1)}, bf16[2,4,336,1792]{3,2,1,0:T(8,128)(2,1)}, bf16[4,512,256]{2,1,0:T(8,128)(2,1)}, bf16[4,512,1280]{2...) custom-call(s32[2]{0:T(128)} %copy-done.13, ...), custom_call_target="tpu_custom_call", output_to_operand_aliasing={{0}: (15, {}), {1}: (16, {}), {2}: (17, {}), {3}: (18, {})} | custom-call | flops 5549064192 | bytes 13762560 | tf_op jit(solution)/shard_map/pallas_call | solution.py:705
  309.9 16.6 %shard_map.287 = (bf16[2,4,336,1280]{3,2,1,0:T(8,128)(2,1)}, bf16[2,4,336,1792]{3,2,1,0:T(8,128)(2,1)}, bf16[4,512,256]{2,1,0:T(8,128)(2,1)}, bf16[4,512,1280]{2...) custom-call(s32[2]{0:T(128)} %copy-done.13, ...), custom_call_target="tpu_custom_call", output_to_operand_aliasing={{0}: (15, {}), {1}: (16, {}), {2}: (17, {}), {3}: (18, {})} | custom-call | flops 5549064192 | bytes 13762560 | tf_op jit(solution)/shard_map/pallas_call | solution.py:705
  329.3 19.4 %collective-permute-done.33 = bf16[256,1408]{1,0:T(8,128)(2,1)S(1)} collective-permute-done((bf16[256,1408]{1,0:T(8,128)(2,1)S(1)}, bf16[256,1408]{1,0:T(8,128)(2,1)S(1)}, u32[]{:S(2)}, u32[]{:S(2)}) %collective-permute-start.33) | collective-permute-done | bytes 720928 | tf_op jit(solution)/shard_map/ppermute | solution.py:349
  356.9 12.7 %convolution_convert_fusion.1 = bf16[1280,1792]{1,0:T(8,128)(2,1)} fusion(bf16[2,1344,1792]{2,1,0:T(8,128)(2,1)} %bitcast.149, bf16[2,1344,1280]{2,1,0:T(8,128)(2,1)} %bitcast.156), kind=kOutput, calls=%fused_computation.2 | convolution fusion | flops 6167920640 | bytes 12845056 | tf_op jit(solution)/shard_map/dot_general | solution.py:21
  369.6 10.5 %convolution_convert_fusion = bf16[1280,1792]{1,0:T(8,128)(2,1)} fusion(bf16[2,1344,1792]{2,1,0:T(8,128)(2,1)S(1)} %bitcast.152, bf16[2,1344,1280]{2,1,0:T(8,128)(2,1)} %bitcast.157), kind=kOutput, calls=%fused_computation.1 | convolution fusion | flops 6167920640 | bytes 12845056 | tf_op jit(solution)/shard_map/dot_general | solution.py:21
  380.1 20.8 %attend_back.1 = (f32[256,1280]{1,0:T(8,128)}, bf16[1280,2560]{1,0:T(8,128)(2,1)}, bf16[1280,1408]{1,0:T(8,128)(2,1)}) custom-call(s32[1]{0:T(128)S(6)} %copy.161.length_ref, bf16[256,1280]{1,0:T(8,128)(2,1)} %get-tuple-element.222.low_ref, f32[256,1280]{1,0:T(8,128)} %get-tuple-element.223.wide_ref, bf16[256,1280]{1,0:T(8,128)(2,1)} %bitcast.146, ...), custom_call_target="tpu_custom_call" | custom-call | flops 7549747200 | bytes 26214400 | tf_op jit(solution)/shard_map/attend_back/pallas_call | solution.py:748
  440.0 49.5 %collective-permute-done.52 = bf16[8,40,128]{2,1,0:T(8,128)(2,1)S(1)} collective-permute-done((bf16[8,40,128]{2,1,0:T(8,128)(2,1)S(1)}, bf16[8,40,128]{2,1,0:T(8,128)(2,1)S(1)}, u32[]{:S(2)}, u32[]{:S(2)}) %collective-permute-start.52) | collective-permute-done | bytes 81952 | tf_op jit(solution)/shard_map/ppermute | solution.py:390
  514.3 19.7 %collective-permute-done.35 = bf16[256,1280]{1,0:T(8,128)(2,1)} collective-permute-done((bf16[256,1280]{1,0:T(8,128)(2,1)}, bf16[256,1280]{1,0:T(8,128)(2,1)}, u32[]{:S(2)}, u32[]{:S(2)}) %collective-permute-start.35) | collective-permute-done | bytes 655392 | tf_op jit(solution)/shard_map/ppermute | solution.py:349
  535.8 12.9 %collective-permute-done.55 = bf16[40,1792]{1,0:T(8,128)(2,1)S(1)} collective-permute-done((bf16[40,1792]{1,0:T(8,128)(2,1)S(1)}, bf16[40,1792]{1,0:T(8,128)(2,1)S(1)}, u32[]{:S(2)}, u32[]{:S(2)}) %collective-permute-start.55) | collective-permute-done | bytes 143392 | tf_op jit(solution)/shard_map/ppermute | solution.py:390
  552.9 29.7 %collective-permute-done.36 = bf16[256,1280]{1,0:T(8,128)(2,1)S(1)} collective-permute-done((bf16[256,1280]{1,0:T(8,128)(2,1)S(1)}, bf16[256,1280]{1,0:T(8,128)(2,1)S(1)}, u32[]{:S(2)}, u32[]{:S(2)}) %collective-permute-start.36) | collective-permute-done | bytes 655392 | tf_op jit(solution)/shard_map/ppermute | solution.py:349
  593.6 13.2 %collective-permute-done.64 = bf16[2,224,1280]{2,1,0:T(8,128)(2,1)S(1)} collective-permute-done((bf16[2,224,1280]{2,1,0:T(8,128)(2,1)S(1)}, bf16[2,224,1280]{2,1,0:T(8,128)(2,1)S(1)}, u32[]{:S(2)}, u32[]{:S(2)}) %collective-permute-start.64) | collective-permute-done | bytes 1146912 | tf_op jit(solution)/shard_map/ppermute | solution.py:390
  630.4 11.9 %collective-permute-done.37 = bf16[160,768]{1,0:T(8,128)(2,1)S(1)} collective-permute-done((bf16[160,768]{1,0:T(8,128)(2,1)S(1)}, bf16[160,768]{1,0:T(8,128)(2,1)S(1)}, u32[]{:S(2)}, u32[]{:S(2)}) %collective-permute-start.37) | collective-permute-done | bytes 245792 | tf_op jit(solution)/shard_map/ppermute | solution.py:390
  675.4 25.4 %collective-permute-done.67 = bf16[224,1280]{1,0:T(8,128)(2,1)} collective-permute-done((bf16[224,1280]{1,0:T(8,128)(2,1)}, bf16[224,1280]{1,0:T(8,128)(2,1)}, u32[]{:S(2)}, u32[]{:S(2)}) %collective-permute-start.67) | collective-permute-done | bytes 573472 | tf_op jit(solution)/shard_map/ppermute | solution.py:390
  (417 shorter events, 263.4 us)
Async XLA Ops:
  7.2 42.3 %all-gather.3.cloned.1.call-start = ((), (), s32[]{:S(2)}) async-start(), calls=%async_computation.5 | async-start | bytes 2949120 | tf_op jit(solution)/shard_map/all_gather | solution.py:515
  13.9 88.7 %all-gather.5.cloned.1.call-start = ((), (), s32[]{:S(2)}) async-start(), calls=%async_computation.6 | async-start | bytes 4423680 | tf_op jit(solution)/shard_map/all_gather | solution.py:526
  58.2 44.3 %collective-permute-start = (bf16[640,896]{1,0:T(8,128)(2,1)S(1)}, bf16[640,896]{1,0:T(8,128)(2,1)}, u32[]{:S(2)}, u32[]{:S(2)}) collective-permute-start(bf16[640,896]{1,0:T(8,128)(2,1)S(1)} %constant_dynamic-slice_fusion.2.refs_0_), channel_id=1, source_target_pairs={{0,1},{1,0},{2,3},{3,2},{4,5},{5,4},{6,7},{7,6},{8,9},{9,8},{10,11... | collective-permute-start | bytes 3440648 | tf_op jit(solution)/shard_map/ppermute | solution.py:354
  127.5 59.1 %all-to-all-start = ((bf16[8,160,256]{2,1,0:T(8,128)(2,1)}), bf16[8,160,256]{2,1,0:T(8,128)(2,1)S(1)}, u32[]{:S(2)}, u32[]{:S(2)}) async-start(bf16[8,160,256]{2,1,0:T(8,128)(2,1)} %fusion.20), calls=%async_computation | async-start | bytes 1310720 | tf_op jit(solution)/shard_map/all_to_all | solution.py:570
  131.6 482.6 %reduce-scatter.4.cloned.1.call-start = ((), (), s32[]{:S(2)}) async-start(), calls=%async_computation.7 | async-start | bytes 4055040 | tf_op jit(solution)/shard_map/reduce_scatter | solution.py:765
  145.1 41.5 %collective-permute-start.9 = (bf16[256,1280]{1,0:T(8,128)(2,1)S(1)}, bf16[256,1280]{1,0:T(8,128)(2,1)S(1)}, u32[]{:S(2)}, u32[]{:S(2)}) collective-permute-start(bf16[256,1280]{1,0:T(8,128)(2,1)S(1)} %get-tuple-element.143.s0_ref.second_ref), channel_id=1, source_target_pairs={{0,1},{1,0},{2,3},{3,2},{4,5},{5,4},{6,7},{7,6},{8,9},{9,8},{10,11... | collective-permute-start | bytes 1966088 | tf_op jit(solution)/shard_map/ppermute | solution.py:354
  145.1 58.3 %collective-permute-start.16 = (bf16[256,1280]{1,0:T(8,128)(2,1)}, bf16[256,1280]{1,0:T(8,128)(2,1)}, u32[]{:S(2)}, u32[]{:S(2)}) collective-permute-start(bf16[256,1280]{1,0:T(8,128)(2,1)} %collective-permute-done.11.s0_ref), channel_id=1, source_target_pairs={{0,1},{1,0},{2,3},{3,2},{4,5},{5,4},{6,7},{7,6},{8,9},{9,8},{10,11... | collective-permute-start | bytes 1966088 | tf_op jit(solution)/shard_map/ppermute | solution.py:354
  169.7 49.4 %collective-permute-start.26 = (bf16[256,1280]{1,0:T(8,128)(2,1)}, bf16[256,1280]{1,0:T(8,128)(2,1)}, u32[]{:S(2)}, u32[]{:S(2)}) collective-permute-start(bf16[256,1280]{1,0:T(8,128)(2,1)} %collective-permute-done.21.g0_ref), channel_id=1, source_target_pairs={{0,1},{1,0},{2,3},{3,2},{4,5},{5,4},{6,7},{7,6},{8,9},{9,8},{10,11... | collective-permute-start | bytes 1966088 | tf_op jit(solution)/shard_map/ppermute | solution.py:354
  236.1 72.9 %collective-permute-start.20 = (bf16[256,1280]{1,0:T(8,128)(2,1)}, bf16[256,1280]{1,0:T(8,128)(2,1)S(1)}, u32[]{:S(2)}, u32[]{:S(2)}) collective-permute-start(bf16[256,1280]{1,0:T(8,128)(2,1)} %bitcast.2.g0_ref.up_ref), channel_id=1, source_target_pairs={{0,1},{1,0},{2,3},{3,2},{4,5},{5,4},{6,7},{7,6},{8,9},{9,8},{10,11... | collective-permute-start | bytes 1966088 | tf_op jit(solution)/shard_map/ppermute | solution.py:354
  253.7 54.6 %collective-permute-start.31 = (bf16[256,1408]{1,0:T(8,128)(2,1)S(1)}, bf16[256,1408]{1,0:T(8,128)(2,1)S(1)}, u32[]{:S(2)}, u32[]{:S(2)}) collective-permute-start(bf16[256,1408]{1,0:T(8,128)(2,1)S(1)} %add_convert_fusion.6), channel_id=1, source_target_pairs={{0,2},{1,3},{2,4},{3,5},{4,6},{5,7},{6,0},{7,1},{8,10},{9,11},{10,... | collective-permute-start | bytes 2162696 | tf_op jit(solution)/shard_map/ppermute | solution.py:349
  401.0 219.0 %reduce-scatter.8.cloned.1.call-start = ((), (), s32[]{:S(2)}) async-start(), calls=%async_computation.9 | async-start | bytes 4055040 | tf_op jit(solution)/shard_map/reduce_scatter | solution.py:763
  401.6 269.3 %reduce-scatter.6.cloned.1.call-start = ((), (), s32[]{:S(2)}) async-start(), calls=%async_computation.8 | async-start | bytes 7372800 | tf_op jit(solution)/shard_map/reduce_scatter | solution.py:764
  402.1 99.0 %collective-permute-start.18 = (bf16[256,1280]{1,0:T(8,128)(2,1)}, bf16[256,1280]{1,0:T(8,128)(2,1)}, u32[]{:S(2)}, u32[]{:S(2)}) collective-permute-start(bf16[256,1280]{1,0:T(8,128)(2,1)} %get-tuple-element.167), channel_id=1, source_target_pairs={{0,1},{1,0},{2,3},{3,2},{4,5},{5,4},{6,7},{7,6},{8,9},{9,8},{10,11... | collective-permute-start | bytes 1966088 | tf_op jit(solution)/shard_map/ppermute | solution.py:354
  405.1 105.0 %collective-permute-start.17 = (bf16[256,1280]{1,0:T(8,128)(2,1)}, bf16[256,1280]{1,0:T(8,128)(2,1)}, u32[]{:S(2)}, u32[]{:S(2)}) collective-permute-start(bf16[256,1280]{1,0:T(8,128)(2,1)} %get-tuple-element.165), channel_id=1, source_target_pairs={{0,1},{1,0},{2,3},{3,2},{4,5},{5,4},{6,7},{7,6},{8,9},{9,8},{10,11... | collective-permute-start | bytes 1966088 | tf_op jit(solution)/shard_map/ppermute | solution.py:354
  405.3 95.8 %collective-permute-start.34 = (bf16[256,1280]{1,0:T(8,128)(2,1)}, bf16[256,1280]{1,0:T(8,128)(2,1)}, u32[]{:S(2)}, u32[]{:S(2)}) collective-permute-start(bf16[256,1280]{1,0:T(8,128)(2,1)} %add_convert_fusion.10), channel_id=1, source_target_pairs={{0,2},{1,3},{2,4},{3,5},{4,6},{5,7},{6,0},{7,1},{8,10},{9,11},{10,... | collective-permute-start | bytes 1966088 | tf_op jit(solution)/shard_map/ppermute | solution.py:349
  435.9 148.4 %collective-permute-start.60 = (bf16[2,320,1792]{2,1,0:T(8,128)(2,1)}, bf16[2,320,1792]{2,1,0:T(8,128)(2,1)}, u32[]{:S(2)}, u32[]{:S(2)}) collective-permute-start(bf16[2,320,1792]{2,1,0:T(8,128)(2,1)} %get-tuple-element.342), channel_id=1, source_target_pairs={{0,8},{8,0},{16,24},{24,16},{1,9},{9,1},{17,25},{25,17},{2,10},{10... | collective-permute-start | bytes 6881288 | tf_op jit(solution)/shard_map/ppermute | solution.py:390
  437.6 51.8 %collective-permute-start.52 = (bf16[8,40,128]{2,1,0:T(8,128)(2,1)S(1)}, bf16[8,40,128]{2,1,0:T(8,128)(2,1)S(1)}, u32[]{:S(2)}, u32[]{:S(2)}) collective-permute-start(bf16[8,40,128]{2,1,0:T(8,128)(2,1)S(1)} %dynamic-slice_bitcast_fusion.17), channel_id=1, source_target_pairs={{0,8},{8,0},{16,24},{24,16},{1,9},{9,1},{17,25},{25,17},{2,10},{10... | collective-permute-start | bytes 245768 | tf_op jit(solution)/shard_map/ppermute | solution.py:390
  493.9 92.1 %collective-permute-start.61 = (bf16[2,320,1792]{2,1,0:T(8,128)(2,1)}, bf16[2,320,1792]{2,1,0:T(8,128)(2,1)}, u32[]{:S(2)}, u32[]{:S(2)}) collective-permute-start(bf16[2,320,1792]{2,1,0:T(8,128)(2,1)} %get-tuple-element.340), channel_id=1, source_target_pairs={{0,16},{8,24},{16,0},{24,8},{1,17},{9,25},{17,1},{25,9},{2,18},{10... | collective-permute-start | bytes 6881288 | tf_op jit(solution)/shard_map/ppermute | solution.py:390
  510.2 41.4 %collective-permute-start.10 = (bf16[256,1280]{1,0:T(8,128)(2,1)}, bf16[256,1280]{1,0:T(8,128)(2,1)S(1)}, u32[]{:S(2)}, u32[]{:S(2)}) collective-permute-start(bf16[256,1280]{1,0:T(8,128)(2,1)} %get-tuple-element.151), channel_id=1, source_target_pairs={{0,1},{1,0},{2,3},{3,2},{4,5},{5,4},{6,7},{7,6},{8,9},{9,8},{10,11... | collective-permute-start | bytes 1966088 | tf_op jit(solution)/shard_map/ppermute | solution.py:354
  548.8 120.9 %collective-permute-start.56 = (bf16[112,640]{1,0:T(8,128)(2,1)}, bf16[112,640]{1,0:T(8,128)(2,1)}, u32[]{:S(2)}, u32[]{:S(2)}) collective-permute-start(bf16[112,640]{1,0:T(8,128)(2,1)} %get-tuple-element.370), channel_id=1, source_target_pairs={{0,8},{8,0},{16,24},{24,16},{1,9},{9,1},{17,25},{25,17},{2,10},{10... | collective-permute-start | bytes 430088 | tf_op jit(solution)/shard_map/ppermute | solution.py:390
  551.5 120.5 %collective-permute-start.58 = (bf16[112,640]{1,0:T(8,128)(2,1)}, bf16[112,640]{1,0:T(8,128)(2,1)}, u32[]{:S(2)}, u32[]{:S(2)}) collective-permute-start(bf16[112,640]{1,0:T(8,128)(2,1)} %get-tuple-element.371), channel_id=1, source_target_pairs={{0,16},{8,24},{16,0},{24,8},{1,17},{9,25},{17,1},{25,9},{2,18},{10... | collective-permute-start | bytes 430088 | tf_op jit(solution)/shard_map/ppermute | solution.py:390
  589.4 113.1 %collective-permute-start.62 = (bf16[320,1792]{1,0:T(8,128)(2,1)}, bf16[320,1792]{1,0:T(8,128)(2,1)}, u32[]{:S(2)}, u32[]{:S(2)}) collective-permute-start(bf16[320,1792]{1,0:T(8,128)(2,1)} %get-tuple-element.350), channel_id=1, source_target_pairs={{0,16},{8,24},{16,0},{24,8},{1,17},{9,25},{17,1},{25,9},{2,18},{10... | collective-permute-start | bytes 3440648 | tf_op jit(solution)/shard_map/ppermute | solution.py:390
  658.6 45.2 %collective-permute-start.63 = (bf16[320,1792]{1,0:T(8,128)(2,1)}, bf16[320,1792]{1,0:T(8,128)(2,1)}, u32[]{:S(2)}, u32[]{:S(2)}) collective-permute-start(bf16[320,1792]{1,0:T(8,128)(2,1)} %get-tuple-element.348), channel_id=1, source_target_pairs={{0,8},{8,0},{16,24},{24,16},{1,9},{9,1},{17,25},{25,17},{2,10},{10... | collective-permute-start | bytes 3440648 | tf_op jit(solution)/shard_map/ppermute | solution.py:390
  672.1 40.2 %collective-permute-start.41 = (bf16[160,1280]{1,0:T(8,128)(2,1)S(1)}, bf16[160,1280]{1,0:T(8,128)(2,1)S(1)}, u32[]{:S(2)}, u32[]{:S(2)}) collective-permute-start(bf16[160,1280]{1,0:T(8,128)(2,1)S(1)} %get-tuple-element.358), channel_id=1, source_target_pairs={{0,16},{8,24},{16,0},{24,8},{1,17},{9,25},{17,1},{25,9},{2,18},{10... | collective-permute-start | bytes 1228808 | tf_op jit(solution)/shard_map/ppermute | solution.py:390
  (117 other events, 2227.1 us)
Sparse Core Ops, SparseCore 0:
  14.0 35.4 all-gather.2
  51.8 43.8 all-gather.4
  401.1 55.5 reduce-scatter.3
  458.9 42.7 reduce-scatter.7
  503.8 95.6 reduce-scatter.5
